TPU v7x, 128 devices: a whole 4x4x4 slice. The times are simulated.
128 devices in a mesh: net: 32 (over y, z, core), hour: 4 (over x).
Axes of the slice: x: 4, y: 4, z: 4, core: 2. Of those that a mesh axis runs over, the one named last changes fastest.
Arguments:
- measured: float32 [4096, 2048], P('net', 'hour')
- prior_flow: float32 [4096, 2048], P('net', 'hour'), may hold values from -6 to 6
- demand: float32 [3072, 2048], P('net', 'hour'), may hold values from -6 to 6
- pipe_sigma: float32 [4096], P('net'), may hold values from 0.5 to 2
- whiten_coef: float32 [512], replicated
- pipe_tail: int32 [4096], P('net'), may hold values from 0 to 95
- pipe_head: int32 [4096], P('net'), may hold values from 0 to 95
- boundary_pipe: int32 [32, 2, 8], P('net'), may hold values from 0 to 127, as said below
- boundary_count: int32 [32, 2], P('net'), may hold values from 0 to 8, as said below
- arrival_junction: int32 [32, 2, 8], P('net'), may hold values from 0 to 95
Outputs:
- flows: float32 [4096, 2048], P('net', 'hour')
- residual: float32 [4096, 2048], P('net', 'hour')
Inputs may be any that keep to these rules, and one draw needn't show every extreme that they name: `boundary_pipe`: the 16 entries of one partition's two lists are distinct local pipe numbers. `boundary_count`: partition 0 has no live slot toward side 0 and partition 32 - 1 none toward side 1.
All inputs are finite; a program needn't handle non-finite values.
Results may differ from a plain program's by a relative error of at most 0.00026.
Values sent between devices are 32-bit elements; how exact they have to be, the bound alone decides.
No kernel may reach another device: no remote copies, remote signals or barrier semaphores. Data moves between devices by JAX's collectives and lax.ppermute only.
A program may use at most 64 MiB of HBM per device.

v0:
```python
import jax
import jax.numpy as jnp
from jax import lax
from jax.sharding import PartitionSpec as P

ITERS = 3


huber_edge = 1.5
penalty = 4.0
highest = lax.Precision.HIGHEST


def with_halo(cells, sides, width):
    for axis, dim in sides:
        count = lax.axis_size(axis)
        ends = count - 1
        head = lax.slice_in_dim(cells, 0, width, axis=dim)
        tail = lax.slice_in_dim(cells, cells.shape[dim] - width, cells.shape[dim], axis=dim)
        cells = jnp.concatenate(
            [
                lax.ppermute(tail, axis, [(i, (i + 1) % count) for i in range(ends)]),
                cells,
                lax.ppermute(head, axis, [((i + 1) % count, i) for i in range(ends)]),
            ],
            axis=dim,
        )
    return cells


def whiten_transposed(whiten_coef):
    length = whiten_coef.shape[0]
    padded = jnp.concatenate([whiten_coef, jnp.zeros((length,), jnp.float32)])
    tiled = jnp.tile(padded, length)[: length * (2 * length - 1)]
    return tiled.reshape(length, 2 * length - 1)[:, :length]


def send_forward(slot_rows, capacity):
    extended = with_halo(slot_rows, (("net", 0),), capacity)
    return jnp.concatenate([extended[:capacity], extended[3 * capacity :]], axis=0)


def send_back(slot_rows, capacity):
    extended = with_halo(slot_rows, (("net", 0),), capacity)
    return jnp.concatenate([extended[:capacity], extended[3 * capacity :]], axis=0)


def squares(residual):
    return lax.psum(jnp.sum(residual * residual), ("net", "hour"))


def shards(
    measured,
    prior_flow,
    demand,
    pipe_sigma,
    whiten_coef,
    pipe_tail,
    pipe_head,
    boundary_pipe,
    boundary_count,
    arrival_junction,
):
    junctions = demand.shape[0]
    pipe_count = measured.shape[0]
    capacity = boundary_pipe.shape[2]
    whiten_tr = whiten_transposed(whiten_coef)
    whitener = whiten_tr.T
    variance = (pipe_sigma * pipe_sigma)[:, None]
    scaled = (measured - prior_flow) / pipe_sigma[:, None]
    whitened = jnp.dot(scaled, whiten_tr, precision=highest)
    huber_weight = huber_edge / jnp.maximum(jnp.abs(whitened), huber_edge)
    slot_ids = jnp.arange(capacity, dtype=jnp.int32)
    live_flat = (slot_ids[None, :] < boundary_count[0][:, None]).astype(jnp.float32).reshape(-1)
    source_pipes = boundary_pipe[0].reshape(-1)
    targets = arrival_junction[0].reshape(-1)
    pipe_ids = jnp.arange(pipe_count, dtype=jnp.int32)
    junction_ids = jnp.arange(junctions, dtype=jnp.int32)
    selector = (source_pipes[:, None] == pipe_ids[None, :]).astype(jnp.float32) * live_flat[:, None]
    interior = 1.0 - jnp.sum(selector, axis=0)
    head_onehot = (junction_ids[:, None] == pipe_head[None, :]).astype(jnp.float32) * interior[
        None, :
    ]
    tail_onehot = (junction_ids[:, None] == pipe_tail[None, :]).astype(jnp.float32)
    incidence = head_onehot - tail_onehot
    landing = (junction_ids[:, None] == targets[None, :]).astype(jnp.float32)

    def quadratic(field):
        filtered = jnp.dot(field, whiten_tr, precision=highest)
        return jnp.dot(huber_weight * filtered, whitener, precision=highest) / variance

    def adjoint_of(balance):
        returned = send_back(jnp.dot(landing.T, balance, precision=highest), capacity)
        local_part = jnp.dot(incidence.T, balance, precision=highest)
        return local_part + jnp.dot(selector.T, returned, precision=highest)

    def operator(field):
        arrivals = send_forward(jnp.dot(selector, field, precision=highest), capacity)
        near_part = quadratic(field)
        local_part = jnp.dot(incidence, field, precision=highest)
        balance = local_part + jnp.dot(landing, arrivals, precision=highest)
        return near_part + penalty * adjoint_of(balance)

    rhs = quadratic(measured) + penalty * adjoint_of(demand)
    flows = prior_flow
    residual = rhs - operator(flows)
    direction = residual
    norm_now = squares(residual)
    for iteration in range(ITERS):
        image = operator(direction)
        step_size = norm_now / lax.psum(jnp.sum(direction * image), ("net", "hour"))
        flows = flows + step_size * direction
        residual = residual - step_size * image
        norm_next = squares(residual)
        direction = residual + norm_next / norm_now * direction
        norm_now = norm_next
    return (flows, residual)


def solution(mesh):
    placed = (
        P("net", "hour"),
        P("net", "hour"),
        P("net", "hour"),
        P("net"),
        P(),
        P("net"),
        P("net"),
        P("net", None, None),
        P("net", None),
        P("net", None, None),
    )
    return jax.shard_map(
        shards,
        mesh=mesh,
        in_specs=placed,
        out_specs=(P("net", "hour"), P("net", "hour")),
        check_vma=False,
    )
```

profile of v0, /device:TPU:1, one launch (start us, length us, event | category | flops | bytes accessed | tf_op | source)
XLA Modules:
  0.0 442.6 jit_solution(16197144370421191570)
XLA Ops:
  0.6 0.8 eq.67
  1.8 4.9 %collective-permute-start = (f32[8,512]{1,0:T(8,128)S(1)}, f32[8,512]{1,0:T(8,128)S(1)}, u32[]{:S(2)}, u32[]{:S(2)}) collective-permute-start(f32[8,512]{1,0:T(8,128)S(1)} %get-tuple-element.24), channel_id=1, source_target_pairs={{0,4},{4,8},{8,12},{12,16},{16,20},{20,24},{24,28},{28,32},{32,36}... | collective-permute-start | bytes 49160 | tf_op jit(solution)/shard_map/ppermute | solution.py:22
  6.7 1.9 collective-permute-start.1
  8.7 0.7 compare_convert_fusion
  9.5 0.8 eq.59
  10.2 1.2 fusion.80
  11.5 3.6 collective-permute-start.2
  15.1 1.9 collective-permute-start.3
  17.1 0.7 concatenate.30
  18.1 1.8 copy.12
  19.9 3.0 reshape.35
  22.9 0.8 fusion.12
  23.7 0.7 fusion.13
  24.4 0.7 fusion.14
  25.2 1.2 convolution_divide_fusion.4
  26.4 1.2 convolution_divide_fusion.3
  27.6 0.4 fusion.42
  28.0 0.3 fusion.41
  28.8 3.6 collective-permute-start.4
  32.4 1.9 collective-permute-start.5
  34.4 0.5 fusion.10
  34.9 0.4 fusion.40
  35.4 2.2 collective-permute-done.5
  37.5 0.5 fusion.8
  38.3 0.7 convolution_multiply_fusion.2
  39.0 1.9 collective-permute-start.6
  41.0 2.4 collective-permute-start.7
  43.4 1.2 convolution_divide_fusion.2
  44.6 0.3 fusion.39
  44.9 1.4 collective-permute-done.7
  46.8 2.0 collective-permute-start.8
  48.8 2.3 collective-permute-start.9
  51.1 0.4 fusion.38
  51.5 2.3 collective-permute-done.9
  53.9 1.2 multiply_reduce_fusion.4
  55.0 75.2 %all-reduce.1 = (f32[]{:T(128)}, f32[]{:T(128)}) all-reduce(f32[]{:T(128)} %get-tuple-element.3, f32[]{:T(128)} %get-tuple-element.2), channel_id=1, replica_groups=mesh['net'=32,'hour'=4] {'net','hour'}, use_global_device_ids=true, to_apply=%region_2.0 | all-reduce | flops 2 | bytes 16 | tf_op jit(solution)/shard_map/psum | solution.py:49
  131.6 0.7 multiply_reduce_fusion.3
  132.3 63.5 %psum.44 = f32[]{:T(128)} all-reduce(f32[]{:T(128)} %multiply_reduce_fusion.3), channel_id=1, replica_groups=mesh['net'=32,'hour'=4] {'net','hour'}, use_global_device_ids=true, to_apply=%region_6.0 | all-reduce | flops 1 | bytes 8 | tf_op jit(solution)/shard_map/psum | solution.py:49
  197.4 0.7 convolution_multiply_fusion.1
  198.1 2.4 collective-permute-start.10
  200.5 2.0 collective-permute-start.11
  202.5 1.2 convolution_divide_fusion.1
  204.0 1.6 collective-permute-done.11
  206.0 2.0 collective-permute-start.12
  208.1 2.3 collective-permute-start.13
  210.3 0.4 fusion.36
  210.8 2.3 collective-permute-done.13
  213.1 1.8 multiply_reduce_fusion.2
  214.9 69.4 %psum.45 = f32[]{:T(128)} all-reduce(f32[]{:T(128)} %get-tuple-element.27), channel_id=1, replica_groups=mesh['net'=32,'hour'=4] {'net','hour'}, use_global_device_ids=true, to_apply=%region_8.0 | all-reduce | flops 1 | bytes 8 | tf_op jit(solution)/shard_map/psum | solution.py:111
  285.6 2.3 multiply_reduce_fusion.1
  287.9 62.8 %psum.46 = f32[]{:T(128)} all-reduce(f32[]{:T(128)} %get-tuple-element.6), channel_id=1, replica_groups=mesh['net'=32,'hour'=4] {'net','hour'}, use_global_device_ids=true, to_apply=%region_10.0 | all-reduce | flops 1 | bytes 8 | tf_op jit(solution)/shard_map/psum | solution.py:49
  352.1 1.0 multiply_add_fusion.1
  353.3 0.7 convolution_multiply_fusion
  354.1 3.3 collective-permute-start.14
  357.4 2.1 collective-permute-start.15
  359.4 1.2 convolution_divide_fusion
  360.9 1.6 collective-permute-done.15
  363.0 2.0 collective-permute-start.16
  365.0 2.3 collective-permute-start.17
  367.3 0.4 fusion.34
  367.8 2.3 collective-permute-done.17
  370.1 1.2 multiply_reduce_fusion
  371.3 68.2 %psum.47 = f32[]{:T(128)} all-reduce(f32[]{:T(128)} %get-tuple-element.29), channel_id=1, replica_groups=mesh['net'=32,'hour'=4] {'net','hour'}, use_global_device_ids=true, to_apply=%region_12.0 | all-reduce | flops 1 | bytes 8 | tf_op jit(solution)/shard_map/psum | solution.py:111
  440.7 1.9 multiply_subtract_fusion
  (54 shorter events, 4.1 us)
Async XLA Ops:
  0.6 0.9 copy-start
  1.8 32.6 %collective-permute-start = (f32[8,512]{1,0:T(8,128)S(1)}, f32[8,512]{1,0:T(8,128)S(1)}, u32[]{:S(2)}, u32[]{:S(2)}) collective-permute-start(f32[8,512]{1,0:T(8,128)S(1)} %get-tuple-element.24), channel_id=1, source_target_pairs={{0,4},{4,8},{8,12},{12,16},{16,20},{20,24},{24,28},{28,32},{32,36}... | collective-permute-start | bytes 49160 | tf_op jit(solution)/shard_map/ppermute | solution.py:22
  6.7 27.7 %collective-permute-start.1 = (f32[8,512]{1,0:T(8,128)S(1)}, f32[8,512]{1,0:T(8,128)S(1)}, u32[]{:S(2)}, u32[]{:S(2)}) collective-permute-start(f32[8,512]{1,0:T(8,128)S(1)} %get-tuple-element.25), channel_id=1, source_target_pairs={{4,0},{8,4},{12,8},{16,12},{20,16},{24,20},{28,24},{32,28},{36,32}... | collective-permute-start | bytes 49160 | tf_op jit(solution)/shard_map/ppermute | solution.py:24
  11.5 16.9 %collective-permute-start.2 = (f32[8,512]{1,0:T(8,128)S(1)}, f32[8,512]{1,0:T(8,128)S(1)}, u32[]{:S(2)}, u32[]{:S(2)}) collective-permute-start(f32[8,512]{1,0:T(8,128)S(1)} %get-tuple-element.22), channel_id=1, source_target_pairs={{0,4},{4,8},{8,12},{12,16},{16,20},{20,24},{24,28},{28,32},{32,36}... | collective-permute-start | bytes 49160 | tf_op jit(solution)/shard_map/ppermute | solution.py:22
  15.1 13.2 %collective-permute-start.3 = (f32[8,512]{1,0:T(8,128)S(1)}, f32[8,512]{1,0:T(8,128)S(1)}, u32[]{:S(2)}, u32[]{:S(2)}) collective-permute-start(f32[8,512]{1,0:T(8,128)S(1)} %get-tuple-element.23), channel_id=1, source_target_pairs={{4,0},{8,4},{12,8},{16,12},{20,16},{24,20},{28,24},{32,28},{36,32}... | collective-permute-start | bytes 49160 | tf_op jit(solution)/shard_map/ppermute | solution.py:24
  19.9 3.0 copy-start.6
  19.9 3.1 copy-start.1
  19.9 3.1 copy-start.3
  24.4 3.1 copy-start.4
  24.4 3.1 copy-start.5
  28.8 6.5 %collective-permute-start.4 = (f32[8,512]{1,0:T(8,128)S(1)}, f32[8,512]{1,0:T(8,128)S(1)}, u32[]{:S(2)}, u32[]{:S(2)}) collective-permute-start(f32[8,512]{1,0:T(8,128)S(1)} %get-tuple-element.20), channel_id=1, source_target_pairs={{0,4},{4,8},{8,12},{12,16},{16,20},{20,24},{24,28},{28,32},{32,36}... | collective-permute-start | bytes 49160 | tf_op jit(solution)/shard_map/ppermute | solution.py:22
  32.4 5.1 %collective-permute-start.5 = (f32[8,512]{1,0:T(8,128)S(1)}, f32[8,512]{1,0:T(8,128)S(1)}, u32[]{:S(2)}, u32[]{:S(2)}) collective-permute-start(f32[8,512]{1,0:T(8,128)S(1)} %get-tuple-element.21), channel_id=1, source_target_pairs={{4,0},{8,4},{12,8},{16,12},{20,16},{24,20},{28,24},{32,28},{36,32}... | collective-permute-start | bytes 49160 | tf_op jit(solution)/shard_map/ppermute | solution.py:24
  39.0 5.9 %collective-permute-start.6 = (f32[8,512]{1,0:T(8,128)S(1)}, f32[8,512]{1,0:T(8,128)S(1)}, u32[]{:S(2)}, u32[]{:S(2)}) collective-permute-start(f32[8,512]{1,0:T(8,128)S(1)} %get-tuple-element.18), channel_id=1, source_target_pairs={{0,4},{4,8},{8,12},{12,16},{16,20},{20,24},{24,28},{28,32},{32,36}... | collective-permute-start | bytes 49160 | tf_op jit(solution)/shard_map/ppermute | solution.py:22
  41.0 5.3 %collective-permute-start.7 = (f32[8,512]{1,0:T(8,128)S(1)}, f32[8,512]{1,0:T(8,128)S(1)}, u32[]{:S(2)}, u32[]{:S(2)}) collective-permute-start(f32[8,512]{1,0:T(8,128)S(1)} %get-tuple-element.19), channel_id=1, source_target_pairs={{4,0},{8,4},{12,8},{16,12},{20,16},{24,20},{28,24},{32,28},{36,32}... | collective-permute-start | bytes 49160 | tf_op jit(solution)/shard_map/ppermute | solution.py:24
  46.8 4.8 %collective-permute-start.8 = (f32[8,512]{1,0:T(8,128)S(1)}, f32[8,512]{1,0:T(8,128)S(1)}, u32[]{:S(2)}, u32[]{:S(2)}) collective-permute-start(f32[8,512]{1,0:T(8,128)S(1)} %get-tuple-element.16), channel_id=1, source_target_pairs={{0,4},{4,8},{8,12},{12,16},{16,20},{20,24},{24,28},{28,32},{32,36}... | collective-permute-start | bytes 49160 | tf_op jit(solution)/shard_map/ppermute | solution.py:22
  48.8 5.1 %collective-permute-start.9 = (f32[8,512]{1,0:T(8,128)S(1)}, f32[8,512]{1,0:T(8,128)S(1)}, u32[]{:S(2)}, u32[]{:S(2)}) collective-permute-start(f32[8,512]{1,0:T(8,128)S(1)} %get-tuple-element.17), channel_id=1, source_target_pairs={{4,0},{8,4},{12,8},{16,12},{20,16},{24,20},{28,24},{32,28},{36,32}... | collective-permute-start | bytes 49160 | tf_op jit(solution)/shard_map/ppermute | solution.py:24
  198.1 5.9 %collective-permute-start.10 = (f32[8,512]{1,0:T(8,128)S(1)}, f32[8,512]{1,0:T(8,128)S(1)}, u32[]{:S(2)}, u32[]{:S(2)}) collective-permute-start(f32[8,512]{1,0:T(8,128)S(1)} %get-tuple-element.14), channel_id=1, source_target_pairs={{0,4},{4,8},{8,12},{12,16},{16,20},{20,24},{24,28},{28,32},{32,36}... | collective-permute-start | bytes 49160 | tf_op jit(solution)/shard_map/ppermute | solution.py:22
  200.5 5.1 %collective-permute-start.11 = (f32[8,512]{1,0:T(8,128)S(1)}, f32[8,512]{1,0:T(8,128)S(1)}, u32[]{:S(2)}, u32[]{:S(2)}) collective-permute-start(f32[8,512]{1,0:T(8,128)S(1)} %get-tuple-element.15), channel_id=1, source_target_pairs={{4,0},{8,4},{12,8},{16,12},{20,16},{24,20},{28,24},{32,28},{36,32}... | collective-permute-start | bytes 49160 | tf_op jit(solution)/shard_map/ppermute | solution.py:24
  206.0 4.8 %collective-permute-start.12 = (f32[8,512]{1,0:T(8,128)S(1)}, f32[8,512]{1,0:T(8,128)S(1)}, u32[]{:S(2)}, u32[]{:S(2)}) collective-permute-start(f32[8,512]{1,0:T(8,128)S(1)} %get-tuple-element.12), channel_id=1, source_target_pairs={{0,4},{4,8},{8,12},{12,16},{16,20},{20,24},{24,28},{28,32},{32,36}... | collective-permute-start | bytes 49160 | tf_op jit(solution)/shard_map/ppermute | solution.py:22
  208.1 5.1 %collective-permute-start.13 = (f32[8,512]{1,0:T(8,128)S(1)}, f32[8,512]{1,0:T(8,128)S(1)}, u32[]{:S(2)}, u32[]{:S(2)}) collective-permute-start(f32[8,512]{1,0:T(8,128)S(1)} %get-tuple-element.13), channel_id=1, source_target_pairs={{4,0},{8,4},{12,8},{16,12},{20,16},{24,20},{28,24},{32,28},{36,32}... | collective-permute-start | bytes 49160 | tf_op jit(solution)/shard_map/ppermute | solution.py:24
  354.1 6.9 %collective-permute-start.14 = (f32[8,512]{1,0:T(8,128)S(1)}, f32[8,512]{1,0:T(8,128)S(1)}, u32[]{:S(2)}, u32[]{:S(2)}) collective-permute-start(f32[8,512]{1,0:T(8,128)S(1)} %get-tuple-element.10), channel_id=1, source_target_pairs={{0,4},{4,8},{8,12},{12,16},{16,20},{20,24},{24,28},{28,32},{32,36}... | collective-permute-start | bytes 49160 | tf_op jit(solution)/shard_map/ppermute | solution.py:22
  357.3 83.4 %copy-start.2 = (f32[128,512]{1,0:T(8,128)S(1)}, f32[128,512]{1,0:T(8,128)}, u32[]{:S(2)}) copy-start(f32[128,512]{1,0:T(8,128)} %param.11) | copy-start | bytes 786436
  357.4 5.2 %collective-permute-start.15 = (f32[8,512]{1,0:T(8,128)S(1)}, f32[8,512]{1,0:T(8,128)S(1)}, u32[]{:S(2)}, u32[]{:S(2)}) collective-permute-start(f32[8,512]{1,0:T(8,128)S(1)} %get-tuple-element.11), channel_id=1, source_target_pairs={{4,0},{8,4},{12,8},{16,12},{20,16},{24,20},{28,24},{32,28},{36,32}... | collective-permute-start | bytes 49160 | tf_op jit(solution)/shard_map/ppermute | solution.py:24
  363.0 4.8 %collective-permute-start.16 = (f32[8,512]{1,0:T(8,128)S(1)}, f32[8,512]{1,0:T(8,128)S(1)}, u32[]{:S(2)}, u32[]{:S(2)}) collective-permute-start(f32[8,512]{1,0:T(8,128)S(1)} %get-tuple-element.8), channel_id=1, source_target_pairs={{0,4},{4,8},{8,12},{12,16},{16,20},{20,24},{24,28},{28,32},{32,36}... | collective-permute-start | bytes 49160 | tf_op jit(solution)/shard_map/ppermute | solution.py:22
  365.0 5.1 %collective-permute-start.17 = (f32[8,512]{1,0:T(8,128)S(1)}, f32[8,512]{1,0:T(8,128)S(1)}, u32[]{:S(2)}, u32[]{:S(2)}) collective-permute-start(f32[8,512]{1,0:T(8,128)S(1)} %get-tuple-element.9), channel_id=1, source_target_pairs={{4,0},{8,4},{12,8},{16,12},{20,16},{24,20},{28,24},{32,28},{36,32}... | collective-permute-start | bytes 49160 | tf_op jit(solution)/shard_map/ppermute | solution.py:24
where the time goes:
time: 444 us; the launch traced here: 443 us
  blocking collectives  339 us (76%)
  starting transfers between devices  44.9 us (10%)
  matrix products  22.8 us (5%)
  waiting for transfers between devices  13.8 us (3%)
  between operations  7.75 us (2%)
  local copies, waits for them, and re-layouts  7.62 us (2%)
  other arithmetic  6.74 us (2%)
    psum x3, blocking collectives, squares(): return lax.psum(jnp.sum(residual * residual), ('net', 'hour'))  202 us
    psum x2, blocking collectives, shards(): step_size = norm_now / lax.psum(jnp.sum(direction * image), ('net', 'hour'))  138 us
    ppermute x9, starting transfers between devices, with_halo(): lax.ppermute(tail, axis, [(i, (i + 1) % count) for i in range(ends)])  25.9 us
    ppermute x9, starting transfers between devices, with_halo(): lax.ppermute(head, axis, [((i + 1) % count, i) for i in range(ends)])  19 us
    ppermute x9, waiting for transfers between devices, with_halo(): lax.ppermute(head, axis, [((i + 1) % count, i) for i in range(ends)])  13.7 us
  transfers between devices with their start and end apart: 18, of which 7 were waited for; matrix products, arithmetic and copies ran while one was open for 5% of the time, Pallas kernels for 0%

commit v1 on v0

v1 whole, which is shorter than its diff:
```python
import jax
import jax.numpy as jnp
from jax import lax
from jax.experimental import pallas as pl
from jax.experimental.pallas import tpu as pltpu
from jax.sharding import PartitionSpec as P

EDGE = 1.5
PENALTY = 4.0
F32 = jnp.float32
BF16 = jnp.bfloat16


def iota(shape, dim):
    return lax.broadcasted_iota(jnp.int32, shape, dim)


def thirds(v):
    a = v.astype(BF16)
    rest = v - a.astype(F32)
    b = rest.astype(BF16)
    c = (rest - b.astype(F32)).astype(BF16)
    return a, b, c


def halves(v):
    a = v.astype(BF16)
    return a, (v - a.astype(F32)).astype(BF16)


def mm(a, b):
    return jnp.dot(a, b, preferred_element_type=F32)


def pick(exact, v):
    a, b, c = thirds(v)
    return (mm(exact, c) + mm(exact, b)) + mm(exact, a)


def product(x, t_hi, t_lo):
    hi, lo = halves(x)
    return (mm(lo, t_hi) + mm(hi, t_lo)) + mm(hi, t_hi)


def forward(v, taps):
    t0h, t0l, t1h, t1l = taps
    rows = v.shape[0]
    half = v.shape[1] // 2
    both = jnp.concatenate([v[:, :half], v[:, half:]], axis=0)
    near = product(both, t0h[...], t0l[...])
    far = product(v[:, :half], t1h[...], t1l[...])
    return jnp.concatenate([near[:rows], near[rows:] + far], axis=1)


def backward(v, taps):
    t0h, t0l, t1h, t1l = taps
    rows = v.shape[0]
    half = v.shape[1] // 2
    both = jnp.concatenate([v[:, :half], v[:, half:]], axis=0)
    near = product(both, t0h[...], t0l[...])
    far = product(v[:, half:], t1h[...], t1l[...])
    return jnp.concatenate([near[:rows] + far, near[rows:]], axis=1)


def lanes_sum(v):
    rows, cols = v.shape
    total = None
    for i in range(0, rows, 8):
        for j in range(0, cols, 128):
            part = v[i : i + 8, j : j + 128]
            total = part if total is None else total + part
    return total


def column(row, n):
    return jnp.sum(jnp.where(iota((n, n), 0) == iota((n, n), 1), row, 0.0), axis=1, keepdims=True)


def lists_kernel(par, prior, bp, bc, aj, head, tail, msg, s_a, s_b, inc, l_a, l_b, match):
    cap = bp.shape[2]
    pipes = prior.shape[0]
    juncs = inc.shape[0]
    odd = par[0, 0] == 1

    def side(ref, flip):
        lower, upper = ref[0, 0:1, :].astype(F32), ref[0, 1:2, :].astype(F32)
        return jnp.where(odd != flip, lower, upper)

    counts = bc[0:1, :].astype(F32)
    count_a = jnp.where(odd, counts[:, 0:1], counts[:, 1:2])
    count_b = jnp.where(odd, counts[:, 1:2], counts[:, 0:1])
    slot = iota((cap, 1), 0).astype(F32)
    live_a = jnp.where(slot < count_a, 1.0, 0.0)
    live_b = jnp.where(slot < count_b, 1.0, 0.0)
    pipe = iota((cap, pipes), 1).astype(F32)
    sel_a = jnp.where(column(side(bp, False), cap) == pipe, live_a, 0.0)
    sel_b = jnp.where(column(side(bp, True), cap) == pipe, live_b, 0.0)
    inner = 1.0 - jnp.sum(sel_a + sel_b, axis=0, keepdims=True)
    junction = iota((juncs, pipes), 0)
    heads = jnp.where(junction == head[...], inner, 0.0)
    tails = jnp.where(junction == tail[...], 1.0, 0.0)
    s_a[...] = sel_a.astype(BF16)
    s_b[...] = sel_b.astype(BF16)
    inc[...] = (heads - tails).astype(BF16)
    land = iota((juncs, cap), 0).astype(F32)
    to_a, to_b = side(aj, False), side(aj, True)
    l_a[...] = jnp.where(land == to_a, 1.0, 0.0).astype(BF16)
    l_b[...] = jnp.where(land == to_b, 1.0, 0.0).astype(BF16)
    same = jnp.where(column(to_b, cap) == to_b, 1.0, 0.0)
    match[...] = jnp.concatenate([same, jnp.zeros((cap, 128 - cap), F32)], axis=1)
    msg[0:cap, :] = -pick(sel_a.astype(BF16), prior[...])
    msg[cap:, :] = jnp.broadcast_to(live_a, (cap, prior.shape[1]))


def whiten_kernel(coef, sigma, measured, prior, t0h, t0l, t1h, t1l, u0h, u0l, u1h, u1l, weight, base, rvar, tau):
    length = coef.shape[1]
    half = length // 2
    c = coef[...]
    shifted = pltpu.roll(jnp.broadcast_to(c, (half, length)), 0, 1, stride=1, stride_axis=0)
    upper = iota((half, half), 1) >= iota((half, half), 0)
    t0 = jnp.where(upper, shifted[:, :half], 0.0)
    t1 = shifted[:, half:]
    for hi, lo, x in ((t0h, t0l, t0), (t1h, t1l, t1), (u0h, u0l, t0.T), (u1h, u1l, t1.T)):
        a, b = halves(x)
        hi[...] = a
        lo[...] = b
    size = jnp.sum(jnp.abs(c), axis=1, keepdims=True)
    scale = 1.0 / (4.0 * size * size + 64.0)
    tau[...] = jnp.broadcast_to(scale, tau.shape)
    sig = jnp.transpose(jnp.broadcast_to(sigma[...], (128, 128)))[:, 0:1]
    rsig = 1.0 / sig
    whitened = forward((measured[...] - prior[...]) * rsig, (t0h, t0l, t1h, t1l))
    h = EDGE / jnp.maximum(jnp.abs(whitened), EDGE)
    weight[...] = h
    base[...] = backward(h * whitened, (u0h, u0l, u1h, u1l)) * rsig
    rvar[...] = jnp.broadcast_to(rsig * rsig * scale, rvar.shape)


def first_kernel(demand, prior, got, s_b, inc, l_a, l_b, match, part, msg, l_am):
    cap = s_b.shape[0]
    live = jnp.sum(jnp.where(iota((cap, cap), 0) == iota((cap, cap), 1), got[cap:, 0:cap], 0.0), axis=0, keepdims=True)
    masked = (l_a[...].astype(F32) * live).astype(BF16)
    l_am[...] = masked
    part[...] = demand[...] - pick(inc[...], prior[...]) + pick(masked, got[0:cap, :])
    msg[0:cap, :] = -pick(s_b[...], prior[...])
    msg[cap : 2 * cap, :] = pick(l_b[...].T, part[...])
    msg[2 * cap :, :] = jnp.broadcast_to(match[:, 0:1], (cap, prior.shape[1]))
    msg[2 * cap :, 0:128] = match[...]


def meet(near, gain, part, sent, got, s_a, s_b, inc, l_am, l_b, match, y_out, w_out, msg):
    cap = s_a.shape[0]
    y = part[...] + pick(l_b[...], got[0:cap, :])
    y_far = got[cap : 2 * cap, :] + pick(match, sent[0:cap, :])
    w = near + gain * (pick(inc[...].T, y) + pick(s_b[...].T, y_far))
    y_out[...] = y
    w_out[...] = w
    msg[0:cap, :] = pick(l_am[...].T, y)
    msg[cap:, :] = pick(s_a[...], w)


def meet_first(base, part, sent, got, s_a, s_b, inc, l_am, l_b, y_out, w_out, msg, match):
    cap = s_a.shape[0]
    match[...] = got[2 * cap :, 0:128]
    meet(base[...], PENALTY, part, sent, got, s_a, s_b, inc, l_am, l_b, match[:, 0:cap].astype(BF16), y_out, w_out, msg)


def meet_next(q, rvar, tau, part, sent, got, s_a, s_b, inc, l_am, l_b, match, y_out, w_out, msg):
    cap = s_a.shape[0]
    near = q[...] * rvar[:, 0:1]
    meet(near, PENALTY * tau[0:1, 0:1], part, sent, got, s_a, s_b, inc, l_am, l_b, match[:, 0:cap].astype(BF16), y_out, w_out, msg)


def meet_last(r0m, r1m, r2m, r, q, rvar, tau, part, sent, got, s_a, s_b, inc, l_am, l_b, match, w_out, msg, row, y_s):
    cap = s_a.shape[0]
    near = q[...] * rvar[:, 0:1]
    gain = PENALTY * tau[0:1, 0:1]
    meet(near, gain, part, sent, got, s_a, s_b, inc, l_am, l_b, match[:, 0:cap].astype(BF16), y_s, w_out, msg)
    y = y_s[...]
    m5 = lanes_sum(r[...] * near) + gain * lanes_sum(y * y)
    lane = iota((1, 128), 1) // 16
    out = jnp.zeros((1, 128), F32)
    for g, tile in enumerate((r0m[0:8, :], r1m[0:8, :], r1m[8:16, :], r2m[0:8, :], r2m[8:16, :], m5)):
        x = jnp.sum(tile, axis=0, keepdims=True)
        for s in (64, 32, 16):
            x = x + pltpu.roll(x, s, 1)
        out = jnp.where(lane == g, x, out)
    row[...] = out


def open_kernel(gain, w, sent, got, s_a, s_b, inc, l_am, l_b, r_out, part, msg):
    cap = s_a.shape[0]
    r = w[...] + gain * pick(s_a[...].T, got[0:cap, :])
    arrived = got[cap:, :] + gain * sent[0:cap, :]
    r_out[...] = r
    part[...] = pick(inc[...], r) + pick(l_am[...], arrived)
    msg[0:cap, :] = pick(s_b[...], r)
    msg[cap:, :] = pick(l_b[...].T, part[...])


def open_first(*refs):
    open_kernel(PENALTY, *refs)


def open_next(tau, *refs):
    open_kernel(PENALTY * tau[0:1, 0:1], *refs)


def filter_first(r, weight, t0h, t0l, t1h, t1l, u0h, u0l, u1h, u1l, q, sums):
    x = r[...]
    q[...] = backward(weight[...] * forward(x, (t0h, t0l, t1h, t1l)), (u0h, u0l, u1h, u1l))
    sums[...] = lanes_sum(x * x)


def filter_next(r, before, weight, t0h, t0l, t1h, t1l, u0h, u0l, u1h, u1l, q, sums):
    x = r[...]
    q[...] = backward(weight[...] * forward(x, (t0h, t0l, t1h, t1l)), (u0h, u0l, u1h, u1l))
    sums[0:8, :] = lanes_sum(before[...] * x)
    sums[8:16, :] = lanes_sum(x * x)


def two_sum(a, b):
    s = a + b
    t = s - a
    return s, (a - (s - t)) + (b - t)


def split(a):
    t = 4097.0 * a
    hi = t - (t - a)
    return hi, a - hi


def two_prod(a, b):
    p = a * b
    ah, al = split(a)
    bh, bl = split(b)
    return p, ((ah * bh - p) + ah * bl + al * bh) + al * bl


def pair_add(x, y):
    s, e = two_sum(x[0], y[0])
    return two_sum(s, e + (x[1] + y[1]))


def finish_kernel(rows, tau, prior, r0, r1, r2, w, got, s_a, flows, residual):
    n = rows.shape[0]
    tot = (rows[0:8, :], jnp.zeros((8, 128), F32))
    for i in range(8, n, 8):
        s, e = two_sum(tot[0], rows[i : i + 8, :])
        tot = (s, tot[1] + e)
    for sh in (4, 2, 1):
        tot = pair_add(tot, tuple(pltpu.roll(t, sh, 0) for t in tot))
    for sh in (8, 4, 2, 1):
        tot = pair_add(tot, tuple(pltpu.roll(t, 128 - sh, 1) for t in tot))
    hi, lo = tot
    s0 = pltpu.roll(hi, 112, 1) / hi
    s = jnp.broadcast_to(s0[:, 0:1], (8, 128))
    mu = [hi]
    for _ in range(5):
        ph, pe = two_prod(hi, s)
        pe = pe + lo * s
        nh, nl = pltpu.roll(hi, 112, 1), pltpu.roll(lo, 112, 1)
        a, e = two_sum(nh, -ph)
        hi, lo = two_sum(a, e + (nl - pe))
        mu.append(hi)
    nu = [mu[k + 1] + s * mu[k] for k in range(5)]

    def form(u, v, m):
        total = None
        for i, a in enumerate(u):
            for j, b in enumerate(v):
                term = a * b * m[i + j]
                total = term if total is None else total + term
        return total

    def image(d):
        out = [s * x for x in d] + [jnp.zeros_like(s)]
        return [out[k] + (d[k - 1] if k else 0.0) for k in range(len(out))]

    a0 = mu[0] / nu[0]
    res1 = [mu[1] / nu[0], -a0]
    rr1 = form(res1, res1, mu)
    b0 = rr1 / mu[0]
    d1 = [res1[0] + b0, res1[1]]
    a1 = rr1 / form(d1, d1, nu)
    im1 = image(d1)
    res2 = [res1[0] - a1 * im1[0], res1[1] - a1 * im1[1], -a1 * im1[2]]
    rr2 = form(res2, res2, mu)
    b1 = rr2 / rr1
    d2 = [res2[0] + b1 * d1[0], res2[1] + b1 * d1[1], res2[2]]
    a2 = rr2 / form(d2, d2, nu)
    im2 = image(d2)
    f = [a0 + a1 * d1[0] + a2 * d2[0], a1 * d1[1] + a2 * d2[1], a2 * d2[2]]
    e = [res2[0] - a2 * im2[0], res2[1] - a2 * im2[1], res2[2] - a2 * im2[2], -a2 * im2[3]]
    ss = s * s
    f = [f[0] - s * f[1] + ss * f[2], f[1] - 2.0 * s * f[2], f[2]]
    e = [
        ((e[0] - s * e[1]) + ss * e[2]) - ss * s * e[3],
        (e[1] - 2.0 * s * e[2]) + 3.0 * ss * e[3],
        e[2] - 3.0 * s * e[3],
        e[3],
    ]
    f = [x[0:1, 0:1] * tau[0:1, 0:1] for x in f]
    e = [x[0:1, 0:1] for x in e]
    cap = s_a.shape[0]
    x0, x1, x2 = r0[...], r1[...], r2[...]
    x3 = w[...] + PENALTY * tau[0:1, 0:1] * pick(s_a[...].T, got[0:cap, :])
    flows[...] = prior[...] + ((f[0] * x0 + f[1] * x1) + f[2] * x2)
    residual[...] = ((e[0] * x0 + e[1] * x1) + e[2] * x2) + e[3] * x3


def call(kernel, outs, *args, smem=0, scratch=()):
    specs = [pl.BlockSpec(memory_space=pltpu.SMEM)] * smem
    specs += [pl.BlockSpec(memory_space=pltpu.VMEM)] * (len(args) - smem)
    return pl.pallas_call(
        kernel,
        out_shape=tuple(jax.ShapeDtypeStruct(s, d) for s, d in outs),
        in_specs=specs,
        out_specs=tuple(pl.BlockSpec(memory_space=pltpu.VMEM) for _ in outs),
        scratch_shapes=list(scratch),
    )(*args)


def shards(
    measured,
    prior_flow,
    demand,
    pipe_sigma,
    whiten_coef,
    pipe_tail,
    pipe_head,
    boundary_pipe,
    boundary_count,
    arrival_junction,
):
    pipes, hours = prior_flow.shape
    juncs = demand.shape[0]
    cap = boundary_pipe.shape[2]
    nets = lax.axis_size("net")
    devices = nets * lax.axis_size("hour")
    field = ((pipes, hours), F32)
    heads = ((juncs, hours), F32)
    msg2 = ((2 * cap, hours), F32)
    half = ((hours // 2, hours // 2), BF16)
    on_chip = [(i, i ^ 1) for i in range(nets)]
    across = [(i, i + 1) for i in range(1, nets - 1, 2)] + [(i + 1, i) for i in range(1, nets - 1, 2)]

    def swap(x):
        return lax.ppermute(x, "net", on_chip)

    def cross(x):
        return lax.ppermute(x, "net", across)

    odd = (lax.axis_index("net") % 2).astype(jnp.int32).reshape(1, 1)
    msg, s_a, s_b, inc, l_a, l_b, own_match = call(
        lists_kernel,
        [msg2, ((cap, pipes), BF16), ((cap, pipes), BF16), ((juncs, pipes), BF16), ((juncs, cap), BF16), ((juncs, cap), BF16), ((cap, 128), F32)],
        odd,
        prior_flow,
        boundary_pipe,
        boundary_count,
        arrival_junction,
        pipe_head.reshape(1, pipes),
        pipe_tail.reshape(1, pipes),
        smem=1,
    )
    got = swap(msg)
    part, msg, l_am = call(
        first_kernel,
        [heads, ((3 * cap, hours), F32), ((juncs, cap), BF16)],
        demand, prior_flow, got, s_b, inc, l_a, l_b, own_match,
    )
    got = cross(msg)
    out = call(
        whiten_kernel,
        [half] * 8 + [field, field, ((pipes, 128), F32), ((8, 128), F32)],
        whiten_coef.reshape(1, hours), pipe_sigma.reshape(1, pipes), measured, prior_flow,
    )
    taps, (weight, base, rvar, tau) = out[:8], out[8:]
    lists = (s_a, s_b, inc, l_am, l_b)
    y, w, msg, match = call(
        meet_first, [heads, field, msg2, ((cap, 128), F32)], base, part, msg, got, *lists
    )
    fields, sums = [], []
    for step in range(3):
        got = swap(msg)
        if step == 0:
            r, part, msg = call(open_first, [field, heads, msg2], w, msg, got, *lists)
        else:
            r, part, msg = call(open_next, [field, heads, msg2], tau, w, msg, got, *lists)
        got = cross(msg)
        if step == 0:
            q, acc = call(filter_first, [field, ((8, 128), F32)], r, weight, *taps)
        else:
            q, acc = call(filter_next, [field, ((16, 128), F32)], r, fields[-1], weight, *taps)
        fields.append(r)
        sums.append(acc)
        if step < 2:
            y, w, msg = call(meet_next, [heads, field, msg2], q, rvar, tau, part, msg, got, *lists, match)
    w, msg, row = call(
        meet_last, [field, msg2, ((1, 128), F32)],
        *sums, r, q, rvar, tau, part, msg, got, *lists, match,
        scratch=[pltpu.VMEM((juncs, hours), F32)],
    )
    got = swap(msg)
    rows = lax.all_to_all(
        jnp.broadcast_to(row[None], (devices, 1, 128)), ("net", "hour"), 0, 0, tiled=True
    ).reshape(devices, 128)
    return call(finish_kernel, [field, field], rows, tau, prior_flow, *fields, w, got, s_a)


def solution(mesh):
    placed = (
        P("net", "hour"),
        P("net", "hour"),
        P("net", "hour"),
        P("net"),
        P(),
        P("net"),
        P("net"),
        P("net", None, None),
        P("net", None),
        P("net", None, None),
    )
    return jax.shard_map(
        shards,
        mesh=mesh,
        in_specs=placed,
        out_specs=(P("net", "hour"), P("net", "hour")),
        check_vma=False,
    )
```

time: 444 us -> 89.2 us (0.20)
  blocking collectives: 339 us -> 0 us
  Pallas kernels: 0 us -> 35.7 us
  matrix products: 22.8 us -> 0 us
  starting transfers between devices: 44.9 us -> 31.3 us
  between operations: 7.75 us -> 0.74 us
  other arithmetic: 6.74 us -> 0 us
    psum x5 -> x0, blocking collectives: 339 us -> none  [the longest x3 202 us: squares(): return lax.psum(jnp.sum(residual * residual), ('net', 'hour'))]
    pallas_call x0 -> x14, Pallas kernels: none -> 35.7 us  [call(): pl.pallas_call(kernel, out_shape=tuple((jax.ShapeDtypeStruct(s, d) for s,...]
    ppermute x18 -> x9, starting transfers between devices: 44.9 us -> 18 us  [the longest x4 15.4 us: cross(): return lax.ppermute(x, 'net', across)]
    dot_general x38 -> x0, matrix products: 22.8 us -> none  [the longest x5 5.91 us: quadratic(): jnp.dot(huber_weight * filtered, whitener, precision=highest) / variance]
    all_to_all x0 -> x1, starting transfers between devices: none -> 13.4 us  [shards(): lax.all_to_all(jnp.broadcast_to(row[None], (devices, 1, 128)), ('net', 'h...]
    all_to_all x0 -> x1, waiting for transfers between devices: none -> 7.82 us  [shards(): lax.all_to_all(jnp.broadcast_to(row[None], (devices, 1, 128)), ('net', 'h...]
    ppermute x18 -> x9, waiting for transfers between devices: 13.8 us -> 6.19 us  [the longest x5 6.18 us: swap(): return lax.ppermute(x, 'net', on_chip)]
  transfers between devices with their start and end apart: 18 -> 10, of which waited for: 7 -> 6; matrix products, arithmetic and copies ran while one was open for 5% -> 0% of each run, Pallas kernels for 0% -> 13%
where the time goes in v1:
time: 89.2 us; the launch traced here: 88.6 us
  Pallas kernels  35.7 us (40%)
  starting transfers between devices  31.3 us (35%)
  waiting for transfers between devices  14 us (16%)
  local copies, waits for them, and re-layouts  6.75 us (8%)
    pallas_call x14, Pallas kernels, call(): pl.pallas_call(kernel, out_shape=tuple((jax.ShapeDtypeStruct(s, d) for s,...  35.7 us
    ppermute x4, starting transfers between devices, cross(): return lax.ppermute(x, 'net', across)  15.4 us
    all_to_all x1, starting transfers between devices, shards(): lax.all_to_all(jnp.broadcast_to(row[None], (devices, 1, 128)), ('net', 'h...  13.4 us
    all_to_all x1, waiting for transfers between devices, shards(): lax.all_to_all(jnp.broadcast_to(row[None], (devices, 1, 128)), ('net', 'h...  7.82 us
    ppermute x5, waiting for transfers between devices, swap(): return lax.ppermute(x, 'net', on_chip)  6.18 us
    unnamed x24, local copies, waits for them, and re-layouts  6.09 us
    ppermute x5, starting transfers between devices, swap(): return lax.ppermute(x, 'net', on_chip)  2.54 us
  transfers between devices with their start and end apart: 10, of which 6 were waited for; matrix products, arithmetic and copies ran while one was open for 0% of the time, Pallas kernels for 13%

profile of v1, /device:TPU:1, one launch (start us, length us, event | category | flops | bytes accessed | tf_op | source)
XLA Modules:
  0.0 88.6 jit_solution(6894614736722016338)
XLA Ops:
  0.6 1.9 %shard_map.114 = (f32[16,512]{1,0:T(8,128)}, bf16[8,128]{1,0:T(8,128)(2,1)}, bf16[8,128]{1,0:T(8,128)(2,1)}, bf16[96,128]{1,0:T(8,128)(2,1)}, bf16[96,8]{1,0:T(8...) custom-call(s32[1,1]{1,0:T(1,128)} %bitcast.2.par, f32[128,512]{1,0:T(8,128)} %prior.7, s32[1,2,8]{2,1,0:T(2,128)} %bp.1, ...), custom_call_target="tpu_custom_call" | custom-call | tf_op jit(solution)/shard_map/pallas_call | solution.py:316
  2.5 1.4 %collective-permute-start = (f32[16,512]{1,0:T(8,128)}, f32[16,512]{1,0:T(8,128)S(1)}, u32[]{:S(2)}, u32[]{:S(2)}) collective-permute-start(f32[16,512]{1,0:T(8,128)} %get-tuple-element.50), channel_id=1, source_target_pairs={{0,4},{4,0},{8,12},{12,8},{16,20},{20,16},{24,28},{28,24},{32,36},... | collective-permute-start | bytes 98312 | tf_op jit(solution)/shard_map/ppermute | solution.py:350
  3.9 1.1 %collective-permute-done.got = f32[16,512]{1,0:T(8,128)S(1)} collective-permute-done((f32[16,512]{1,0:T(8,128)}, f32[16,512]{1,0:T(8,128)S(1)}, u32[]{:S(2)}, u32[]{:S(2)}) %collective-permute-start) | collective-permute-done | bytes 32800 | tf_op jit(solution)/shard_map/ppermute | solution.py:350
  5.0 0.0 copy-start.3
  5.0 0.6 copy-done.3
  5.6 2.1 %shard_map.115 = (f32[96,512]{1,0:T(8,128)}, f32[24,512]{1,0:T(8,128)}, bf16[96,8]{1,0:T(8,128)(2,1)}) custom-call(f32[96,512]{1,0:T(8,128)} %demand.1, f32[128,512]{1,0:T(8,128)} %prior.7, f32[16,512]{1,0:T(8,128)} %copy-done.3, bf16[8,128]{1,0:T(8,128)(2,1)} %get-tuple-element.51.s_b.refs_4_, bf16[96,128]{1,0:T(8,128)(2,1)} %get-tuple-element.52.inc.refs_5_, ...), custom_call_target="tpu_custom_call" | custom-call | tf_op jit(solution)/shard_map/pallas_call | solution.py:316
  7.8 3.9 %collective-permute-start.1 = (f32[24,512]{1,0:T(8,128)}, f32[24,512]{1,0:T(8,128)S(1)}, u32[]{:S(2)}, u32[]{:S(2)}) collective-permute-start(f32[24,512]{1,0:T(8,128)} %get-tuple-element.57.sent), channel_id=1, source_target_pairs={{4,8},{12,16},{20,24},{28,32},{36,40},{44,48},{52,56},{60,64},{68,... | collective-permute-start | bytes 147464 | tf_op jit(solution)/shard_map/ppermute | solution.py:353
  11.6 2.8 %shard_map.113 = (bf16[256,256]{1,0:T(8,128)(2,1)}, bf16[256,256]{1,0:T(8,128)(2,1)}, bf16[256,256]{1,0:T(8,128)(2,1)}, bf16[256,256]{1,0:T(8,128)(2,1)}, bf16[2...) custom-call(f32[1,512]{1,0:T(1,128)} %bitcast.8, ...), custom_call_target="tpu_custom_call" | custom-call | tf_op jit(solution)/shard_map/pallas_call | solution.py:316
  14.5 0.0 collective-permute-done.1.got
  14.5 0.0 copy-start.1
  14.5 0.6 copy-done.1
  15.1 2.4 %shard_map.116 = (f32[96,512]{1,0:T(8,128)}, f32[128,512]{1,0:T(8,128)}, f32[16,512]{1,0:T(8,128)}, f32[8,128]{1,0:T(8,128)}) custom-call(f32[128,512]{1,0:T(8,128)} %get-tuple-element.49.base, f32[96,512]{1,0:T(8,128)} %get-tuple-element.56.part, f32[24,512]{1,0:T(8,128)} %get-tuple-element.57.sent, f32[24,512]{1,0:T(8,128)} %copy-done.1, ...), custom_call_target="tpu_custom_call" | custom-call | tf_op jit(solution)/shard_map/pallas_call | solution.py:316
  17.5 0.0 collective-permute-start.2
  17.5 1.4 %collective-permute-done.2.refs_2_ = f32[16,512]{1,0:T(8,128)S(1)} collective-permute-done((f32[16,512]{1,0:T(8,128)}, f32[16,512]{1,0:T(8,128)S(1)}, u32[]{:S(2)}, u32[]{:S(2)}) %collective-permute-start.2) | collective-permute-done | bytes 32800 | tf_op jit(solution)/shard_map/ppermute | solution.py:350
  18.9 0.0 copy-start.6
  18.9 0.6 copy-done.6
  19.6 2.3 %shard_map.117 = (f32[128,512]{1,0:T(8,128)}, f32[96,512]{1,0:T(8,128)}, f32[16,512]{1,0:T(8,128)}) custom-call(f32[128,512]{1,0:T(8,128)} %get-tuple-element.60.refs_0_, f32[16,512]{1,0:T(8,128)} %get-tuple-element.61.refs_1_, f32[16,512]{1,0:T(8,128)} %copy-done.6, bf16[8,128]{1,0:T(8,128)(2,1)} %get-tuple-element.58.s_a.refs_3_, ...), custom_call_target="tpu_custom_call" | custom-call | tf_op jit(solution)/shard_map/pallas_call | solution.py:316
  21.9 3.6 %collective-permute-start.3 = (f32[16,512]{1,0:T(8,128)}, f32[16,512]{1,0:T(8,128)S(1)}, u32[]{:S(2)}, u32[]{:S(2)}) collective-permute-start(f32[16,512]{1,0:T(8,128)} %get-tuple-element.77.sent), channel_id=1, source_target_pairs={{4,8},{12,16},{20,24},{28,32},{36,40},{44,48},{52,56},{60,64},{68,... | collective-permute-start | bytes 98312 | tf_op jit(solution)/shard_map/ppermute | solution.py:353
  25.5 2.9 %shard_map.118 = (f32[128,512]{1,0:T(8,128)}, f32[8,128]{1,0:T(8,128)}) custom-call(f32[128,512]{1,0:T(8,128)} %get-tuple-element.62.r.before.r0, f32[128,512]{1,0:T(8,128)} %get-tuple-element.63.weight, bf16[256,256]{1,0:T(8,128)(2,1)} %get-tuple-element.64.t0h, bf16[256,256]{1,0:T(8,128)(2,1)} %get-tuple-element.65.t0l, ...), custom_call_target="tpu_custom_call" | custom-call | tf_op jit(solution)/shard_map/pallas_call | solution.py:316
  28.4 0.0 collective-permute-done.3.got
  28.4 0.0 copy-start.7
  28.4 0.6 copy-done.7
  29.0 2.5 %shard_map.119 = (f32[96,512]{1,0:T(8,128)}, f32[128,512]{1,0:T(8,128)}, f32[16,512]{1,0:T(8,128)}) custom-call(f32[128,512]{1,0:T(8,128)} %get-tuple-element.74.q, f32[128,128]{1,0:T(8,128)} %get-tuple-element.75.rvar, f32[8,128]{1,0:T(8,128)} %get-tuple-element.73.tau, f32[96,512]{1,0:T(8,128)} %get-tuple-element.76.part, ...), custom_call_target="tpu_custom_call" | custom-call | tf_op jit(solution)/shard_map/pallas_call | solution.py:316
  31.5 0.0 collective-permute-start.4
  31.5 1.4 %collective-permute-done.4.refs_2_ = f32[16,512]{1,0:T(8,128)S(1)} collective-permute-done((f32[16,512]{1,0:T(8,128)}, f32[16,512]{1,0:T(8,128)S(1)}, u32[]{:S(2)}, u32[]{:S(2)}) %collective-permute-start.4) | collective-permute-done | bytes 32800 | tf_op jit(solution)/shard_map/ppermute | solution.py:350
  32.9 0.0 copy-start.4
  32.9 0.6 copy-done.4
  33.5 2.3 %shard_map.120 = (f32[128,512]{1,0:T(8,128)}, f32[96,512]{1,0:T(8,128)}, f32[16,512]{1,0:T(8,128)}) custom-call(f32[8,128]{1,0:T(8,128)} %get-tuple-element.73.tau, f32[128,512]{1,0:T(8,128)} %get-tuple-element.79.refs_0_, f32[16,512]{1,0:T(8,128)} %get-tuple-element.80.refs_1_, f32[16,512]{1,0:T(8,128)} %copy-done.4, ...), custom_call_target="tpu_custom_call" | custom-call | tf_op jit(solution)/shard_map/pallas_call | solution.py:316
  35.8 3.3 %collective-permute-start.5 = (f32[16,512]{1,0:T(8,128)}, f32[16,512]{1,0:T(8,128)S(1)}, u32[]{:S(2)}, u32[]{:S(2)}) collective-permute-start(f32[16,512]{1,0:T(8,128)} %get-tuple-element.85.sent), channel_id=1, source_target_pairs={{4,8},{12,16},{20,24},{28,32},{36,40},{44,48},{52,56},{60,64},{68,... | collective-permute-start | bytes 98312 | tf_op jit(solution)/shard_map/ppermute | solution.py:353
  39.1 3.0 %shard_map.121 = (f32[128,512]{1,0:T(8,128)}, f32[16,128]{1,0:T(8,128)}) custom-call(f32[128,512]{1,0:T(8,128)} %get-tuple-element.81.r.before.r1, f32[128,512]{1,0:T(8,128)} %get-tuple-element.62.r.before.r0, f32[128,512]{1,0:T(8,128)} %get-tuple-element.63.weight, bf16[256,256]{1,0:T(8,128)(2,1)} %get-tuple-element.64.t0h, ...), custom_call_target="tpu_custom_call" | custom-call | tf_op jit(solution)/shard_map/pallas_call | solution.py:316
  42.1 0.0 collective-permute-done.5.got
  42.1 0.0 copy-start.8
  42.1 0.6 copy-done.8
  42.7 2.5 %shard_map.122 = (f32[96,512]{1,0:T(8,128)}, f32[128,512]{1,0:T(8,128)}, f32[16,512]{1,0:T(8,128)}) custom-call(f32[128,512]{1,0:T(8,128)} %get-tuple-element.83.q, f32[128,128]{1,0:T(8,128)} %get-tuple-element.75.rvar, f32[8,128]{1,0:T(8,128)} %get-tuple-element.73.tau, f32[96,512]{1,0:T(8,128)} %get-tuple-element.84.part, ...), custom_call_target="tpu_custom_call" | custom-call | tf_op jit(solution)/shard_map/pallas_call | solution.py:316
  45.2 0.0 collective-permute-start.6
  45.2 1.4 %collective-permute-done.6.refs_2_ = f32[16,512]{1,0:T(8,128)S(1)} collective-permute-done((f32[16,512]{1,0:T(8,128)}, f32[16,512]{1,0:T(8,128)S(1)}, u32[]{:S(2)}, u32[]{:S(2)}) %collective-permute-start.6) | collective-permute-done | bytes 32800 | tf_op jit(solution)/shard_map/ppermute | solution.py:350
  46.6 0.0 copy-start.5
  46.6 0.6 copy-done.5
  47.2 2.3 %shard_map.123 = (f32[128,512]{1,0:T(8,128)}, f32[96,512]{1,0:T(8,128)}, f32[16,512]{1,0:T(8,128)}) custom-call(f32[8,128]{1,0:T(8,128)} %get-tuple-element.73.tau, f32[128,512]{1,0:T(8,128)} %get-tuple-element.86.refs_0_, f32[16,512]{1,0:T(8,128)} %get-tuple-element.87.refs_1_, f32[16,512]{1,0:T(8,128)} %copy-done.5, ...), custom_call_target="tpu_custom_call" | custom-call | tf_op jit(solution)/shard_map/pallas_call | solution.py:316
  49.5 4.7 %collective-permute-start.7 = (f32[16,512]{1,0:T(8,128)}, f32[16,512]{1,0:T(8,128)S(1)}, u32[]{:S(2)}, u32[]{:S(2)}) collective-permute-start(f32[16,512]{1,0:T(8,128)} %get-tuple-element.92.sent), channel_id=1, source_target_pairs={{4,8},{12,16},{20,24},{28,32},{36,40},{44,48},{52,56},{60,64},{68,... | collective-permute-start | bytes 98312 | tf_op jit(solution)/shard_map/ppermute | solution.py:353
  54.2 3.0 %shard_map.124 = (f32[128,512]{1,0:T(8,128)}, f32[16,128]{1,0:T(8,128)}) custom-call(f32[128,512]{1,0:T(8,128)} %get-tuple-element.88.r.r2, f32[128,512]{1,0:T(8,128)} %get-tuple-element.81.r.before.r1, f32[128,512]{1,0:T(8,128)} %get-tuple-element.63.weight, bf16[256,256]{1,0:T(8,128)(2,1)} %get-tuple-element.64.t0h, ...), custom_call_target="tpu_custom_call" | custom-call | tf_op jit(solution)/shard_map/pallas_call | solution.py:316
  57.2 0.0 collective-permute-done.7.got
  57.2 0.0 copy-start.9
  57.2 0.6 copy-done.9
  57.8 2.6 %shard_map.125 = (f32[128,512]{1,0:T(8,128)}, f32[16,512]{1,0:T(8,128)}, f32[1,128]{1,0:T(1,128)}) custom-call(f32[8,128]{1,0:T(8,128)} %get-tuple-element.72.r0m, f32[16,128]{1,0:T(8,128)} %get-tuple-element.82.r1m, f32[16,128]{1,0:T(8,128)} %get-tuple-element.89.r2m, f32[128,512]{1,0:T(8,128)} %get-tuple-element.88.r.r2, f32[128,512]{1,0:T(8,128)} %get-tuple-element.90.q, ...), custom_call_target="tpu_custom_call" | custom-call | tf_op jit(solution)/shard_map/pallas_call | solution.py:316
  60.4 0.0 copy-start.10
  60.4 0.6 copy-done.10
  61.0 0.7 broadcast_in_dim.9
  61.6 0.0 copy-start.11
  61.6 13.4 %all-to-all-start = ((f32[128,1,128]{2,1,0:T(1,128)}), f32[128,1,128]{2,1,0:T(1,128)S(1)}, u32[]{:S(2)}, u32[]{:S(2)}) async-start(f32[128,1,128]{2,1,0:T(1,128)} %broadcast_in_dim.9), calls=%async_computation | async-start | bytes 131072 | tf_op jit(solution)/shard_map/all_to_all | solution.py:407
  75.0 0.0 copy-done.11
  75.0 1.1 %collective-permute-start.8 = (f32[16,512]{1,0:T(8,128)S(1)}, f32[16,512]{1,0:T(8,128)S(1)}, u32[]{:S(2)}, u32[]{:S(2)}) collective-permute-start(f32[16,512]{1,0:T(8,128)S(1)} %copy-done.11), channel_id=1, source_target_pairs={{0,4},{4,0},{8,12},{12,8},{16,20},{20,16},{24,28},{28,24},{32,36},... | collective-permute-start | bytes 98312 | tf_op jit(solution)/shard_map/ppermute | solution.py:350
  76.2 0.9 collective-permute-done.8.got
  77.0 0.0 copy-start.2
  77.0 7.8 %all-to-all-done = f32[128,1,128]{2,1,0:T(1,128)S(1)} async-done(((f32[128,1,128]{2,1,0:T(1,128)}), f32[128,1,128]{2,1,0:T(1,128)S(1)}, u32[]{:S(2)}, u32[]{:S(2)}) %all-to-all-start) | async-done | bytes 65568 | tf_op jit(solution)/shard_map/all_to_all | solution.py:407
  84.9 0.0 copy-start
  84.9 0.0 copy-done.2
  84.9 0.6 copy-done
  85.5 3.1 %shard_map.126 = (f32[128,512]{1,0:T(8,128)}, f32[128,512]{1,0:T(8,128)}) custom-call(f32[128,128]{1,0:T(8,128)} %bitcast.7, f32[8,128]{1,0:T(8,128)} %get-tuple-element.73.tau, f32[128,512]{1,0:T(8,128)} %prior.7, f32[128,512]{1,0:T(8,128)} %get-tuple-element.62.r.before.r0, f32[128,512]{1,0:T(8,128)} %get-tuple-element.81.r.before.r1, ...), custom_call_target="tpu_custom_call" | custom-call | tf_op jit(solution)/shard_map/pallas_call | solution.py:316
Async XLA Ops:
  2.5 2.5 %collective-permute-start = (f32[16,512]{1,0:T(8,128)}, f32[16,512]{1,0:T(8,128)S(1)}, u32[]{:S(2)}, u32[]{:S(2)}) collective-permute-start(f32[16,512]{1,0:T(8,128)} %get-tuple-element.50), channel_id=1, source_target_pairs={{0,4},{4,0},{8,12},{12,8},{16,20},{20,16},{24,28},{28,24},{32,36},... | collective-permute-start | bytes 98312 | tf_op jit(solution)/shard_map/ppermute | solution.py:350
  5.0 0.6 copy-start.3
  7.8 6.7 %collective-permute-start.1 = (f32[24,512]{1,0:T(8,128)}, f32[24,512]{1,0:T(8,128)S(1)}, u32[]{:S(2)}, u32[]{:S(2)}) collective-permute-start(f32[24,512]{1,0:T(8,128)} %get-tuple-element.57.sent), channel_id=1, source_target_pairs={{4,8},{12,16},{20,24},{28,32},{36,40},{44,48},{52,56},{60,64},{68,... | collective-permute-start | bytes 147464 | tf_op jit(solution)/shard_map/ppermute | solution.py:353
  14.5 0.6 copy-start.1
  17.5 1.4 %collective-permute-start.2 = (f32[16,512]{1,0:T(8,128)}, f32[16,512]{1,0:T(8,128)S(1)}, u32[]{:S(2)}, u32[]{:S(2)}) collective-permute-start(f32[16,512]{1,0:T(8,128)} %get-tuple-element.61.refs_1_), channel_id=1, source_target_pairs={{0,4},{4,0},{8,12},{12,8},{16,20},{20,16},{24,28},{28,24},{32,36},... | collective-permute-start | bytes 98312 | tf_op jit(solution)/shard_map/ppermute | solution.py:350
  18.9 0.6 copy-start.6
  21.9 6.5 %collective-permute-start.3 = (f32[16,512]{1,0:T(8,128)}, f32[16,512]{1,0:T(8,128)S(1)}, u32[]{:S(2)}, u32[]{:S(2)}) collective-permute-start(f32[16,512]{1,0:T(8,128)} %get-tuple-element.77.sent), channel_id=1, source_target_pairs={{4,8},{12,16},{20,24},{28,32},{36,40},{44,48},{52,56},{60,64},{68,... | collective-permute-start | bytes 98312 | tf_op jit(solution)/shard_map/ppermute | solution.py:353
  28.4 0.6 copy-start.7
  31.5 1.4 %collective-permute-start.4 = (f32[16,512]{1,0:T(8,128)}, f32[16,512]{1,0:T(8,128)S(1)}, u32[]{:S(2)}, u32[]{:S(2)}) collective-permute-start(f32[16,512]{1,0:T(8,128)} %get-tuple-element.80.refs_1_), channel_id=1, source_target_pairs={{0,4},{4,0},{8,12},{12,8},{16,20},{20,16},{24,28},{28,24},{32,36},... | collective-permute-start | bytes 98312 | tf_op jit(solution)/shard_map/ppermute | solution.py:350
  32.9 0.6 copy-start.4
  35.8 6.3 %collective-permute-start.5 = (f32[16,512]{1,0:T(8,128)}, f32[16,512]{1,0:T(8,128)S(1)}, u32[]{:S(2)}, u32[]{:S(2)}) collective-permute-start(f32[16,512]{1,0:T(8,128)} %get-tuple-element.85.sent), channel_id=1, source_target_pairs={{4,8},{12,16},{20,24},{28,32},{36,40},{44,48},{52,56},{60,64},{68,... | collective-permute-start | bytes 98312 | tf_op jit(solution)/shard_map/ppermute | solution.py:353
  42.1 0.6 copy-start.8
  45.2 1.4 %collective-permute-start.6 = (f32[16,512]{1,0:T(8,128)}, f32[16,512]{1,0:T(8,128)S(1)}, u32[]{:S(2)}, u32[]{:S(2)}) collective-permute-start(f32[16,512]{1,0:T(8,128)} %get-tuple-element.87.refs_1_), channel_id=1, source_target_pairs={{0,4},{4,0},{8,12},{12,8},{16,20},{20,16},{24,28},{28,24},{32,36},... | collective-permute-start | bytes 98312 | tf_op jit(solution)/shard_map/ppermute | solution.py:350
  46.6 0.6 copy-start.5
  49.5 7.7 %collective-permute-start.7 = (f32[16,512]{1,0:T(8,128)}, f32[16,512]{1,0:T(8,128)S(1)}, u32[]{:S(2)}, u32[]{:S(2)}) collective-permute-start(f32[16,512]{1,0:T(8,128)} %get-tuple-element.92.sent), channel_id=1, source_target_pairs={{4,8},{12,16},{20,24},{28,32},{36,40},{44,48},{52,56},{60,64},{68,... | collective-permute-start | bytes 98312 | tf_op jit(solution)/shard_map/ppermute | solution.py:353
  57.2 0.6 copy-start.9
  60.4 0.6 copy-start.10
  61.6 13.4 %copy-start.11 = (f32[16,512]{1,0:T(8,128)S(1)}, f32[16,512]{1,0:T(8,128)}, u32[]{:S(2)}) copy-start(f32[16,512]{1,0:T(8,128)} %get-tuple-element.95) | copy-start | bytes 98308
  61.6 23.2 %all-to-all-start = ((f32[128,1,128]{2,1,0:T(1,128)}), f32[128,1,128]{2,1,0:T(1,128)S(1)}, u32[]{:S(2)}, u32[]{:S(2)}) async-start(f32[128,1,128]{2,1,0:T(1,128)} %broadcast_in_dim.9), calls=%async_computation | async-start | bytes 131072 | tf_op jit(solution)/shard_map/all_to_all | solution.py:407
  75.0 2.0 %collective-permute-start.8 = (f32[16,512]{1,0:T(8,128)S(1)}, f32[16,512]{1,0:T(8,128)S(1)}, u32[]{:S(2)}, u32[]{:S(2)}) collective-permute-start(f32[16,512]{1,0:T(8,128)S(1)} %copy-done.11), channel_id=1, source_target_pairs={{0,4},{4,0},{8,12},{12,8},{16,20},{20,16},{24,28},{28,24},{32,36},... | collective-permute-start | bytes 98312 | tf_op jit(solution)/shard_map/ppermute | solution.py:350
  77.0 7.8 %copy-start.2 = (f32[16,512]{1,0:T(8,128)}, f32[16,512]{1,0:T(8,128)S(1)}, u32[]{:S(2)}) copy-start(f32[16,512]{1,0:T(8,128)S(1)} %collective-permute-done.8.got) | copy-start | bytes 98308
  84.9 0.6 copy-start

commit v2 on v1

--- a/solution.py
+++ b/solution.py
@@ -148,35 +148,34 @@
     msg[2 * cap :, 0:128] = match[...]
 
 
-def meet(near, gain, part, sent, got, s_a, s_b, inc, l_am, l_b, match, y_out, w_out, msg):
+def meet(near, gain, part, sent, got, s_a, s_b, inc, l_am, l_b, match, w_out, msg):
     cap = s_a.shape[0]
     y = part[...] + pick(l_b[...], got[0:cap, :])
     y_far = got[cap : 2 * cap, :] + pick(match, sent[0:cap, :])
     w = near + gain * (pick(inc[...].T, y) + pick(s_b[...].T, y_far))
-    y_out[...] = y
     w_out[...] = w
     msg[0:cap, :] = pick(l_am[...].T, y)
     msg[cap:, :] = pick(s_a[...], w)
-
-
-def meet_first(base, part, sent, got, s_a, s_b, inc, l_am, l_b, y_out, w_out, msg, match):
+    return y
+
+
+def meet_first(base, part, sent, got, s_a, s_b, inc, l_am, l_b, w_out, msg, match):
     cap = s_a.shape[0]
     match[...] = got[2 * cap :, 0:128]
-    meet(base[...], PENALTY, part, sent, got, s_a, s_b, inc, l_am, l_b, match[:, 0:cap].astype(BF16), y_out, w_out, msg)
-
-
-def meet_next(q, rvar, tau, part, sent, got, s_a, s_b, inc, l_am, l_b, match, y_out, w_out, msg):
+    meet(base[...], PENALTY, part, sent, got, s_a, s_b, inc, l_am, l_b, match[:, 0:cap].astype(BF16), w_out, msg)
+
+
+def meet_next(q, rvar, tau, part, sent, got, s_a, s_b, inc, l_am, l_b, match, w_out, msg):
     cap = s_a.shape[0]
     near = q[...] * rvar[:, 0:1]
-    meet(near, PENALTY * tau[0:1, 0:1], part, sent, got, s_a, s_b, inc, l_am, l_b, match[:, 0:cap].astype(BF16), y_out, w_out, msg)
-
-
-def meet_last(r0m, r1m, r2m, r, q, rvar, tau, part, sent, got, s_a, s_b, inc, l_am, l_b, match, w_out, msg, row, y_s):
+    meet(near, PENALTY * tau[0:1, 0:1], part, sent, got, s_a, s_b, inc, l_am, l_b, match[:, 0:cap].astype(BF16), w_out, msg)
+
+
+def meet_last(r0m, r1m, r2m, r, q, rvar, tau, part, sent, got, s_a, s_b, inc, l_am, l_b, match, w_out, msg, row):
     cap = s_a.shape[0]
     near = q[...] * rvar[:, 0:1]
     gain = PENALTY * tau[0:1, 0:1]
-    meet(near, gain, part, sent, got, s_a, s_b, inc, l_am, l_b, match[:, 0:cap].astype(BF16), y_s, w_out, msg)
-    y = y_s[...]
+    y = meet(near, gain, part, sent, got, s_a, s_b, inc, l_am, l_b, match[:, 0:cap].astype(BF16), w_out, msg)
     m5 = lanes_sum(r[...] * near) + gain * lanes_sum(y * y)
     lane = iota((1, 128), 1) // 16
     out = jnp.zeros((1, 128), F32)
@@ -185,7 +184,7 @@
         for s in (64, 32, 16):
             x = x + pltpu.roll(x, s, 1)
         out = jnp.where(lane == g, x, out)
-    row[...] = out
+    row[...] = jnp.broadcast_to(out, row.shape)
 
 
 def open_kernel(gain, w, sent, got, s_a, s_b, inc, l_am, l_b, r_out, part, msg):
@@ -310,15 +309,17 @@
     residual[...] = ((e[0] * x0 + e[1] * x1) + e[2] * x2) + e[3] * x3
 
 
-def call(kernel, outs, *args, smem=0, scratch=()):
+def call(kernel, outs, *args, smem=0, final=False):
     specs = [pl.BlockSpec(memory_space=pltpu.SMEM)] * smem
     specs += [pl.BlockSpec(memory_space=pltpu.VMEM)] * (len(args) - smem)
+    args = args[:smem] + tuple(pltpu.with_memory_space_constraint(x, pltpu.VMEM) for x in args[smem:])
+    shape = jax.ShapeDtypeStruct if final else pltpu.VMEM
     return pl.pallas_call(
         kernel,
-        out_shape=tuple(jax.ShapeDtypeStruct(s, d) for s, d in outs),
+        out_shape=tuple(shape(s, d) for s, d in outs),
         in_specs=specs,
         out_specs=tuple(pl.BlockSpec(memory_space=pltpu.VMEM) for _ in outs),
-        scratch_shapes=list(scratch),
+        compiler_params=pltpu.CompilerParams(vmem_limit_bytes=16 * 2**20),
     )(*args)
 
 
@@ -379,8 +380,8 @@
     )
     taps, (weight, base, rvar, tau) = out[:8], out[8:]
     lists = (s_a, s_b, inc, l_am, l_b)
-    y, w, msg, match = call(
-        meet_first, [heads, field, msg2, ((cap, 128), F32)], base, part, msg, got, *lists
+    w, msg, match = call(
+        meet_first, [field, msg2, ((cap, 128), F32)], base, part, msg, got, *lists
     )
     fields, sums = [], []
     for step in range(3):
@@ -397,17 +398,16 @@
         fields.append(r)
         sums.append(acc)
         if step < 2:
-            y, w, msg = call(meet_next, [heads, field, msg2], q, rvar, tau, part, msg, got, *lists, match)
+            w, msg = call(meet_next, [field, msg2], q, rvar, tau, part, msg, got, *lists, match)
     w, msg, row = call(
-        meet_last, [field, msg2, ((1, 128), F32)],
+        meet_last, [field, msg2, ((devices, 128), F32)],
         *sums, r, q, rvar, tau, part, msg, got, *lists, match,
-        scratch=[pltpu.VMEM((juncs, hours), F32)],
     )
     got = swap(msg)
     rows = lax.all_to_all(
-        jnp.broadcast_to(row[None], (devices, 1, 128)), ("net", "hour"), 0, 0, tiled=True
+        row.reshape(devices, 1, 128), ("net", "hour"), 0, 0, tiled=True
     ).reshape(devices, 128)
-    return call(finish_kernel, [field, field], rows, tau, prior_flow, *fields, w, got, s_a)
+    return call(finish_kernel, [field, field], rows, tau, prior_flow, *fields, w, got, s_a, final=True)
 
 
 def solution(mesh):

time: 89.2 us -> 66.3 us (0.74)
  Pallas kernels: 35.7 us -> 11.6 us
  starting transfers between devices: 31.3 us -> 35.9 us
  local copies, waits for them, and re-layouts: 6.75 us -> 2.27 us
  waiting for transfers between devices: 14 us -> 15.5 us
    pallas_call x14, Pallas kernels: 35.7 us -> 11.6 us  [call(): pl.pallas_call(kernel, out_shape=tuple((shape(s, d) for s, d in outs)), i...]
    unnamed x24 -> x22, local copies, waits for them, and re-layouts: 6.09 us -> 2.27 us
    all_to_all x1, starting transfers between devices: 13.4 us -> 16.9 us  [shards(): lax.all_to_all(row.reshape(devices, 1, 128), ('net', 'hour'), 0, 0, tiled...]
    ppermute x4, waiting for transfers between devices: 0.01 us -> 2.34 us  [cross(): return lax.ppermute(x, 'net', across)]
    ppermute x4, starting transfers between devices: 15.4 us -> 16.5 us  [cross(): return lax.ppermute(x, 'net', across)]
  transfers between devices with their start and end apart: 10 -> 10, of which waited for: 6 -> 10; matrix products, arithmetic and copies ran while one was open for 0% -> 0% of each run, Pallas kernels for 13% -> 5%
where the time goes in v2:
time: 66.3 us; the launch traced here: 66.1 us
  starting transfers between devices  35.9 us (54%)
  waiting for transfers between devices  15.5 us (23%)
  Pallas kernels  11.6 us (17%)
  local copies, waits for them, and re-layouts  2.27 us (3%)
  between operations  0.79 us (1%)
    all_to_all x1, starting transfers between devices, shards(): lax.all_to_all(row.reshape(devices, 1, 128), ('net', 'hour'), 0, 0, tiled...  16.9 us
    ppermute x4, starting transfers between devices, cross(): return lax.ppermute(x, 'net', across)  16.5 us
    pallas_call x14, Pallas kernels, call(): pl.pallas_call(kernel, out_shape=tuple((shape(s, d) for s, d in outs)), i...  11.6 us
    all_to_all x1, waiting for transfers between devices, shards(): lax.all_to_all(row.reshape(devices, 1, 128), ('net', 'hour'), 0, 0, tiled...  7.84 us
    ppermute x5, waiting for transfers between devices, swap(): return lax.ppermute(x, 'net', on_chip)  5.36 us
    ppermute x5, starting transfers between devices, swap(): return lax.ppermute(x, 'net', on_chip)  2.56 us
    ppermute x4, waiting for transfers between devices, cross(): return lax.ppermute(x, 'net', across)  2.34 us
    unnamed x22, local copies, waits for them, and re-layouts  2.27 us
  transfers between devices with their start and end apart: 10, of which 10 were waited for; matrix products, arithmetic and copies ran while one was open for 0% of the time, Pallas kernels for 5%

profile of v2, /device:TPU:1, one launch (start us, length us, event | category | flops | bytes accessed | tf_op | source)
XLA Modules:
  0.0 66.1 jit_solution(9048699445439784135)
XLA Ops:
  0.6 0.0 copy-start.6
  0.7 0.0 copy-start.8
  0.7 0.0 copy-start.9
  0.7 0.0 copy-start.5
  0.7 0.0 copy-start.7
  0.7 0.6 copy-done.6
  1.3 0.0 copy-done.8
  1.3 0.0 copy-done.9
  1.3 0.0 copy-done.5
  1.4 0.0 copy-done.7
  1.4 0.0 copy-start
  1.4 0.9 %copy-done = f32[128,512]{1,0:T(8,128)S(1)} copy-done((f32[128,512]{1,0:T(8,128)S(1)}, f32[128,512]{1,0:T(8,128)}, u32[]{:S(2)}) %copy-start) | copy-done | bytes 262168
  2.3 0.0 copy-start.3
  2.3 0.3 shard_map.114
  2.6 1.4 %collective-permute-start = (f32[16,512]{1,0:T(8,128)S(1)}, f32[16,512]{1,0:T(8,128)S(1)}, u32[]{:S(2)}, u32[]{:S(2)}) collective-permute-start(f32[16,512]{1,0:T(8,128)S(1)} %get-tuple-element.50), channel_id=1, source_target_pairs={{0,4},{4,0},{8,12},{12,8},{16,20},{20,16},{24,28},{28,24},{32,36},... | collective-permute-start | bytes 98312 | tf_op jit(solution)/shard_map/ppermute | solution.py:351
  4.0 0.9 %collective-permute-done.got = f32[16,512]{1,0:T(8,128)S(1)} collective-permute-done((f32[16,512]{1,0:T(8,128)S(1)}, f32[16,512]{1,0:T(8,128)S(1)}, u32[]{:S(2)}, u32[]{:S(2)}) %collective-permute-start) | collective-permute-done | bytes 32800 | tf_op jit(solution)/shard_map/ppermute | solution.py:351
  4.9 0.0 copy-done.3
  4.9 0.0 copy-start.1
  4.9 0.0 copy-start.2
  4.9 0.5 shard_map.115
  5.4 0.0 copy-start.4
  5.4 4.0 %collective-permute-start.1 = (f32[24,512]{1,0:T(8,128)S(1)}, f32[24,512]{1,0:T(8,128)S(1)}, u32[]{:S(2)}, u32[]{:S(2)}) collective-permute-start(f32[24,512]{1,0:T(8,128)S(1)} %get-tuple-element.57.sent), channel_id=1, source_target_pairs={{4,8},{12,16},{20,24},{28,32},{36,40},{44,48},{52,56},{60,64},{68,... | collective-permute-start | bytes 147464 | tf_op jit(solution)/shard_map/ppermute | solution.py:354
  9.4 0.0 copy-start.10
  9.4 0.0 copy-done.1
  9.4 0.0 copy-done.2
  9.4 0.0 copy-done.4
  9.4 0.6 copy-done.10
  10.1 1.0 %shard_map.113 = (bf16[256,256]{1,0:T(8,128)(2,1)S(1)}, bf16[256,256]{1,0:T(8,128)(2,1)S(1)}, bf16[256,256]{1,0:T(8,128)(2,1)S(1)}, bf16[256,256]{1,0:T(8,128)(2...) custom-call(f32[1,512]{1,0:T(1,128)S(1)} %bitcast.10, ...), custom_call_target="tpu_custom_call" | custom-call | tf_op jit(solution)/shard_map/pallas_call | solution.py:317
  11.1 0.1 collective-permute-done.1.got
  11.2 0.7 %shard_map.116 = (f32[128,512]{1,0:T(8,128)S(1)}, f32[16,512]{1,0:T(8,128)S(1)}, f32[8,128]{1,0:T(8,128)S(1)}) custom-call(f32[128,512]{1,0:T(8,128)S(1)} %get-tuple-element.49.base, f32[96,512]{1,0:T(8,128)S(1)} %get-tuple-element.56.part, f32[24,512]{1,0:T(8,128)S(1)} %get-tuple-element.57.sent, f32[24,512]{1,0:T(8,128)S(1)} %collective-permute-done.1.got, ...), custom_call_target="tpu_custom_call" | custom-call | tf_op jit(solution)/shard_map/pallas_call | solution.py:317
  11.9 0.0 collective-permute-start.2
  11.9 1.2 %collective-permute-done.2.refs_2_ = f32[16,512]{1,0:T(8,128)S(1)} collective-permute-done((f32[16,512]{1,0:T(8,128)S(1)}, f32[16,512]{1,0:T(8,128)S(1)}, u32[]{:S(2)}, u32[]{:S(2)}) %collective-permute-start.2) | collective-permute-done | bytes 32800 | tf_op jit(solution)/shard_map/ppermute | solution.py:351
  13.1 0.7 %shard_map.117 = (f32[128,512]{1,0:T(8,128)S(1)}, f32[96,512]{1,0:T(8,128)S(1)}, f32[16,512]{1,0:T(8,128)S(1)}) custom-call(f32[128,512]{1,0:T(8,128)S(1)} %get-tuple-element.60.refs_0_, f32[16,512]{1,0:T(8,128)S(1)} %get-tuple-element.61.refs_1_, f32[16,512]{1,0:T(8,128)S(1)} %collective-permute-done.2.refs_2_, ...), custom_call_target="tpu_custom_call" | custom-call | tf_op jit(solution)/shard_map/pallas_call | solution.py:317
  13.8 3.6 %collective-permute-start.3 = (f32[16,512]{1,0:T(8,128)S(1)}, f32[16,512]{1,0:T(8,128)S(1)}, u32[]{:S(2)}, u32[]{:S(2)}) collective-permute-start(f32[16,512]{1,0:T(8,128)S(1)} %get-tuple-element.77.sent), channel_id=1, source_target_pairs={{4,8},{12,16},{20,24},{28,32},{36,40},{44,48},{52,56},{60,64},{68,... | collective-permute-start | bytes 98312 | tf_op jit(solution)/shard_map/ppermute | solution.py:354
  17.5 0.8 %shard_map.118 = (f32[128,512]{1,0:T(8,128)S(1)}, f32[8,128]{1,0:T(8,128)S(1)}) custom-call(f32[128,512]{1,0:T(8,128)S(1)} %get-tuple-element.62.r.before.r0, f32[128,512]{1,0:T(8,128)S(1)} %get-tuple-element.63.weight, bf16[256,256]{1,0:T(8,128)(2,1)S(1)} %get-tuple-element.64.t0h, bf16[256,256]{1,0:T(8,128)(2,1)S(1)} %get-tuple-element.65.t0l, ...), custom_call_target="tpu_custom_call" | custom-call | tf_op jit(solution)/shard_map/pallas_call | solution.py:317
  18.3 0.8 %collective-permute-done.3.got = f32[16,512]{1,0:T(8,128)S(1)} collective-permute-done((f32[16,512]{1,0:T(8,128)S(1)}, f32[16,512]{1,0:T(8,128)S(1)}, u32[]{:S(2)}, u32[]{:S(2)}) %collective-permute-start.3) | collective-permute-done | bytes 32800 | tf_op jit(solution)/shard_map/ppermute | solution.py:354
  19.1 0.7 %shard_map.119 = (f32[128,512]{1,0:T(8,128)S(1)}, f32[16,512]{1,0:T(8,128)S(1)}) custom-call(f32[128,512]{1,0:T(8,128)S(1)} %get-tuple-element.74.q, f32[128,128]{1,0:T(8,128)S(1)} %get-tuple-element.75.rvar, f32[8,128]{1,0:T(8,128)S(1)} %get-tuple-element.73.tau, f32[96,512]{1,0:T(8,128)S(1)} %get-tuple-element.76.part, ...), custom_call_target="tpu_custom_call" | custom-call | tf_op jit(solution)/shard_map/pallas_call | solution.py:317
  19.8 0.0 collective-permute-start.4
  19.8 1.2 %collective-permute-done.4.refs_2_ = f32[16,512]{1,0:T(8,128)S(1)} collective-permute-done((f32[16,512]{1,0:T(8,128)S(1)}, f32[16,512]{1,0:T(8,128)S(1)}, u32[]{:S(2)}, u32[]{:S(2)}) %collective-permute-start.4) | collective-permute-done | bytes 32800 | tf_op jit(solution)/shard_map/ppermute | solution.py:351
  21.0 0.7 %shard_map.120 = (f32[128,512]{1,0:T(8,128)S(1)}, f32[96,512]{1,0:T(8,128)S(1)}, f32[16,512]{1,0:T(8,128)S(1)}) custom-call(f32[8,128]{1,0:T(8,128)S(1)} %get-tuple-element.73.tau, f32[128,512]{1,0:T(8,128)S(1)} %get-tuple-element.79.refs_0_, f32[16,512]{1,0:T(8,128)S(1)} %get-tuple-element.80.refs_1_, f32[16,512]{1,0:T(8,128)S(1)} %collective-permute-done.4.refs_2_, ...), custom_call_target="tpu_custom_call" | custom-call | tf_op jit(solution)/shard_map/pallas_call | solution.py:317
  21.8 3.6 %collective-permute-start.5 = (f32[16,512]{1,0:T(8,128)S(1)}, f32[16,512]{1,0:T(8,128)S(1)}, u32[]{:S(2)}, u32[]{:S(2)}) collective-permute-start(f32[16,512]{1,0:T(8,128)S(1)} %get-tuple-element.85.sent), channel_id=1, source_target_pairs={{4,8},{12,16},{20,24},{28,32},{36,40},{44,48},{52,56},{60,64},{68,... | collective-permute-start | bytes 98312 | tf_op jit(solution)/shard_map/ppermute | solution.py:354
  25.4 0.8 %shard_map.121 = (f32[128,512]{1,0:T(8,128)S(1)}, f32[16,128]{1,0:T(8,128)S(1)}) custom-call(f32[128,512]{1,0:T(8,128)S(1)} %get-tuple-element.81.r.before.r1, f32[128,512]{1,0:T(8,128)S(1)} %get-tuple-element.62.r.before.r0, f32[128,512]{1,0:T(8,128)S(1)} %get-tuple-element.63.weight, bf16[256,256]{1,0:T(8,128)(2,1)S(1)} %get-tuple-element.64.t0h, ...), custom_call_target="tpu_custom_call" | custom-call | tf_op jit(solution)/shard_map/pallas_call | solution.py:317
  26.2 0.8 %collective-permute-done.5.got = f32[16,512]{1,0:T(8,128)S(1)} collective-permute-done((f32[16,512]{1,0:T(8,128)S(1)}, f32[16,512]{1,0:T(8,128)S(1)}, u32[]{:S(2)}, u32[]{:S(2)}) %collective-permute-start.5) | collective-permute-done | bytes 32800 | tf_op jit(solution)/shard_map/ppermute | solution.py:354
  27.0 0.7 %shard_map.122 = (f32[128,512]{1,0:T(8,128)S(1)}, f32[16,512]{1,0:T(8,128)S(1)}) custom-call(f32[128,512]{1,0:T(8,128)S(1)} %get-tuple-element.83.q, f32[128,128]{1,0:T(8,128)S(1)} %get-tuple-element.75.rvar, f32[8,128]{1,0:T(8,128)S(1)} %get-tuple-element.73.tau, f32[96,512]{1,0:T(8,128)S(1)} %get-tuple-element.84.part, ...), custom_call_target="tpu_custom_call" | custom-call | tf_op jit(solution)/shard_map/pallas_call | solution.py:317
  27.7 0.0 collective-permute-start.6
  27.7 1.2 %collective-permute-done.6.refs_2_ = f32[16,512]{1,0:T(8,128)S(1)} collective-permute-done((f32[16,512]{1,0:T(8,128)S(1)}, f32[16,512]{1,0:T(8,128)S(1)}, u32[]{:S(2)}, u32[]{:S(2)}) %collective-permute-start.6) | collective-permute-done | bytes 32800 | tf_op jit(solution)/shard_map/ppermute | solution.py:351
  28.9 0.7 %shard_map.123 = (f32[128,512]{1,0:T(8,128)S(1)}, f32[96,512]{1,0:T(8,128)S(1)}, f32[16,512]{1,0:T(8,128)S(1)}) custom-call(f32[8,128]{1,0:T(8,128)S(1)} %get-tuple-element.73.tau, f32[128,512]{1,0:T(8,128)S(1)} %get-tuple-element.86.refs_0_, f32[16,512]{1,0:T(8,128)S(1)} %get-tuple-element.87.refs_1_, f32[16,512]{1,0:T(8,128)S(1)} %collective-permute-done.6.refs_2_, ...), custom_call_target="tpu_custom_call" | custom-call | tf_op jit(solution)/shard_map/pallas_call | solution.py:317
  29.7 5.2 %collective-permute-start.7 = (f32[16,512]{1,0:T(8,128)S(1)}, f32[16,512]{1,0:T(8,128)S(1)}, u32[]{:S(2)}, u32[]{:S(2)}) collective-permute-start(f32[16,512]{1,0:T(8,128)S(1)} %get-tuple-element.92.sent), channel_id=1, source_target_pairs={{4,8},{12,16},{20,24},{28,32},{36,40},{44,48},{52,56},{60,64},{68,... | collective-permute-start | bytes 98312 | tf_op jit(solution)/shard_map/ppermute | solution.py:354
  34.8 0.8 %shard_map.124 = (f32[128,512]{1,0:T(8,128)S(1)}, f32[16,128]{1,0:T(8,128)S(1)}) custom-call(f32[128,512]{1,0:T(8,128)S(1)} %get-tuple-element.88.r.r2, f32[128,512]{1,0:T(8,128)S(1)} %get-tuple-element.81.r.before.r1, f32[128,512]{1,0:T(8,128)S(1)} %get-tuple-element.63.weight, bf16[256,256]{1,0:T(8,128)(2,1)S(1)} %get-tuple-element.64.t0h, ...), custom_call_target="tpu_custom_call" | custom-call | tf_op jit(solution)/shard_map/pallas_call | solution.py:317
  35.7 0.8 %collective-permute-done.7.got = f32[16,512]{1,0:T(8,128)S(1)} collective-permute-done((f32[16,512]{1,0:T(8,128)S(1)}, f32[16,512]{1,0:T(8,128)S(1)}, u32[]{:S(2)}, u32[]{:S(2)}) %collective-permute-start.7) | collective-permute-done | bytes 32800 | tf_op jit(solution)/shard_map/ppermute | solution.py:354
  36.4 1.1 %shard_map.125 = (f32[128,512]{1,0:T(8,128)S(1)}, f32[16,512]{1,0:T(8,128)S(1)}, f32[128,128]{1,0:T(8,128)}) custom-call(f32[8,128]{1,0:T(8,128)S(1)} %get-tuple-element.72.r0m, f32[16,128]{1,0:T(8,128)S(1)} %get-tuple-element.82.r1m, f32[16,128]{1,0:T(8,128)S(1)} %get-tuple-element.89.r2m, f32[128,512]{1,0:T(8,128)S(1)} %get-tuple-element.88.r.r2, ...), custom_call_target="tpu_custom_call" | custom-call | tf_op jit(solution)/shard_map/pallas_call | solution.py:317
  37.6 16.9 %all-to-all-start = ((f32[128,1,128]{2,1,0:T(1,128)}), f32[128,1,128]{2,1,0:T(1,128)S(1)}, u32[]{:S(2)}, u32[]{:S(2)}) async-start(f32[128,1,128]{2,1,0:T(1,128)} %bitcast.6), calls=%async_computation | async-start | bytes 131072 | tf_op jit(solution)/shard_map/all_to_all | solution.py:407
  54.5 1.1 %collective-permute-start.8 = (f32[16,512]{1,0:T(8,128)S(1)}, f32[16,512]{1,0:T(8,128)S(1)}, u32[]{:S(2)}, u32[]{:S(2)}) collective-permute-start(f32[16,512]{1,0:T(8,128)S(1)} %get-tuple-element.95), channel_id=1, source_target_pairs={{0,4},{4,0},{8,12},{12,8},{16,20},{20,16},{24,28},{28,24},{32,36},... | collective-permute-start | bytes 98312 | tf_op jit(solution)/shard_map/ppermute | solution.py:351
  55.6 0.9 %collective-permute-done.8.got = f32[16,512]{1,0:T(8,128)S(1)} collective-permute-done((f32[16,512]{1,0:T(8,128)S(1)}, f32[16,512]{1,0:T(8,128)S(1)}, u32[]{:S(2)}, u32[]{:S(2)}) %collective-permute-start.8) | collective-permute-done | bytes 32800 | tf_op jit(solution)/shard_map/ppermute | solution.py:351
  56.5 7.8 %all-to-all-done = f32[128,1,128]{2,1,0:T(1,128)S(1)} async-done(((f32[128,1,128]{2,1,0:T(1,128)}), f32[128,1,128]{2,1,0:T(1,128)S(1)}, u32[]{:S(2)}, u32[]{:S(2)}) %all-to-all-start) | async-done | bytes 65568 | tf_op jit(solution)/shard_map/all_to_all | solution.py:407
  64.3 1.8 %shard_map.126 = (f32[128,512]{1,0:T(8,128)}, f32[128,512]{1,0:T(8,128)}) custom-call(f32[128,128]{1,0:T(8,128)S(1)} %bitcast.9, f32[8,128]{1,0:T(8,128)S(1)} %get-tuple-element.73.tau, f32[128,512]{1,0:T(8,128)S(1)} %copy-done.1, f32[128,512]{1,0:T(8,128)S(1)} %get-tuple-element.62.r.before.r0, f32[128,512]{1,0:T(8,128)S(1)} %get-tuple-element.81.r.before.r1, ...), custom_call_target="tpu_custom_call" | custom-call | tf_op jit(solution)/shard_map/pallas_call | solution.py:317
Async XLA Ops:
  0.6 0.7 %copy-start.6 = (s32[1,2,8]{2,1,0:T(2,128)S(1)}, s32[1,2,8]{2,1,0:T(2,128)}, u32[]{:S(2)}) copy-start(s32[1,2,8]{2,1,0:T(2,128)} %aj.1) | copy-start | bytes 196
  0.7 0.7 %copy-start.8 = (s32[128]{0:T(128)S(1)}, s32[128]{0:T(128)}, u32[]{:S(2)}) copy-start(s32[128]{0:T(128)} %param.16) | copy-start | bytes 1540
  0.7 0.7 %copy-start.9 = (s32[128]{0:T(128)S(1)}, s32[128]{0:T(128)}, u32[]{:S(2)}) copy-start(s32[128]{0:T(128)} %param.15) | copy-start | bytes 1540
  0.7 0.7 %copy-start.5 = (s32[1,2,8]{2,1,0:T(2,128)S(1)}, s32[1,2,8]{2,1,0:T(2,128)}, u32[]{:S(2)}) copy-start(s32[1,2,8]{2,1,0:T(2,128)} %bp.1) | copy-start | bytes 196
  0.7 0.7 %copy-start.7 = (s32[1,2]{1,0:T(1,128)S(1)}, s32[1,2]{1,0:T(1,128)}, u32[]{:S(2)}) copy-start(s32[1,2]{1,0:T(1,128)} %bc.1) | copy-start | bytes 28
  1.4 1.0 %copy-start = (f32[128,512]{1,0:T(8,128)S(1)}, f32[128,512]{1,0:T(8,128)}, u32[]{:S(2)}) copy-start(f32[128,512]{1,0:T(8,128)} %prior.7) | copy-start | bytes 786436
  2.3 2.6 %copy-start.3 = (f32[96,512]{1,0:T(8,128)S(1)}, f32[96,512]{1,0:T(8,128)}, u32[]{:S(2)}) copy-start(f32[96,512]{1,0:T(8,128)} %demand.1) | copy-start | bytes 589828
  2.6 2.3 %collective-permute-start = (f32[16,512]{1,0:T(8,128)S(1)}, f32[16,512]{1,0:T(8,128)S(1)}, u32[]{:S(2)}, u32[]{:S(2)}) collective-permute-start(f32[16,512]{1,0:T(8,128)S(1)} %get-tuple-element.50), channel_id=1, source_target_pairs={{0,4},{4,0},{8,12},{12,8},{16,20},{20,16},{24,28},{28,24},{32,36},... | collective-permute-start | bytes 98312 | tf_op jit(solution)/shard_map/ppermute | solution.py:351
  4.9 4.5 %copy-start.1 = (f32[128,512]{1,0:T(8,128)S(1)}, f32[128,512]{1,0:T(8,128)}, u32[]{:S(2)}) copy-start(f32[128,512]{1,0:T(8,128)} %prior.7) | copy-start | bytes 786436
  4.9 4.5 %copy-start.2 = (f32[128,512]{1,0:T(8,128)S(1)}, f32[128,512]{1,0:T(8,128)}, u32[]{:S(2)}) copy-start(f32[128,512]{1,0:T(8,128)} %measured.1) | copy-start | bytes 786436
  5.4 4.1 %copy-start.4 = (f32[512]{0:T(512)S(1)}, f32[512]{0:T(512)}, u32[]{:S(2)}) copy-start(f32[512]{0:T(512)} %param.14) | copy-start | bytes 6148
  5.4 5.8 %collective-permute-start.1 = (f32[24,512]{1,0:T(8,128)S(1)}, f32[24,512]{1,0:T(8,128)S(1)}, u32[]{:S(2)}, u32[]{:S(2)}) collective-permute-start(f32[24,512]{1,0:T(8,128)S(1)} %get-tuple-element.57.sent), channel_id=1, source_target_pairs={{4,8},{12,16},{20,24},{28,32},{36,40},{44,48},{52,56},{60,64},{68,... | collective-permute-start | bytes 147464 | tf_op jit(solution)/shard_map/ppermute | solution.py:354
  9.4 0.7 copy-start.10
  11.9 1.2 %collective-permute-start.2 = (f32[16,512]{1,0:T(8,128)S(1)}, f32[16,512]{1,0:T(8,128)S(1)}, u32[]{:S(2)}, u32[]{:S(2)}) collective-permute-start(f32[16,512]{1,0:T(8,128)S(1)} %get-tuple-element.61.refs_1_), channel_id=1, source_target_pairs={{0,4},{4,0},{8,12},{12,8},{16,20},{20,16},{24,28},{28,24},{32,36},... | collective-permute-start | bytes 98312 | tf_op jit(solution)/shard_map/ppermute | solution.py:351
  13.8 5.2 %collective-permute-start.3 = (f32[16,512]{1,0:T(8,128)S(1)}, f32[16,512]{1,0:T(8,128)S(1)}, u32[]{:S(2)}, u32[]{:S(2)}) collective-permute-start(f32[16,512]{1,0:T(8,128)S(1)} %get-tuple-element.77.sent), channel_id=1, source_target_pairs={{4,8},{12,16},{20,24},{28,32},{36,40},{44,48},{52,56},{60,64},{68,... | collective-permute-start | bytes 98312 | tf_op jit(solution)/shard_map/ppermute | solution.py:354
  19.8 1.2 %collective-permute-start.4 = (f32[16,512]{1,0:T(8,128)S(1)}, f32[16,512]{1,0:T(8,128)S(1)}, u32[]{:S(2)}, u32[]{:S(2)}) collective-permute-start(f32[16,512]{1,0:T(8,128)S(1)} %get-tuple-element.80.refs_1_), channel_id=1, source_target_pairs={{0,4},{4,0},{8,12},{12,8},{16,20},{20,16},{24,28},{28,24},{32,36},... | collective-permute-start | bytes 98312 | tf_op jit(solution)/shard_map/ppermute | solution.py:351
  21.8 5.2 %collective-permute-start.5 = (f32[16,512]{1,0:T(8,128)S(1)}, f32[16,512]{1,0:T(8,128)S(1)}, u32[]{:S(2)}, u32[]{:S(2)}) collective-permute-start(f32[16,512]{1,0:T(8,128)S(1)} %get-tuple-element.85.sent), channel_id=1, source_target_pairs={{4,8},{12,16},{20,24},{28,32},{36,40},{44,48},{52,56},{60,64},{68,... | collective-permute-start | bytes 98312 | tf_op jit(solution)/shard_map/ppermute | solution.py:354
  27.7 1.2 %collective-permute-start.6 = (f32[16,512]{1,0:T(8,128)S(1)}, f32[16,512]{1,0:T(8,128)S(1)}, u32[]{:S(2)}, u32[]{:S(2)}) collective-permute-start(f32[16,512]{1,0:T(8,128)S(1)} %get-tuple-element.87.refs_1_), channel_id=1, source_target_pairs={{0,4},{4,0},{8,12},{12,8},{16,20},{20,16},{24,28},{28,24},{32,36},... | collective-permute-start | bytes 98312 | tf_op jit(solution)/shard_map/ppermute | solution.py:351
  29.7 6.8 %collective-permute-start.7 = (f32[16,512]{1,0:T(8,128)S(1)}, f32[16,512]{1,0:T(8,128)S(1)}, u32[]{:S(2)}, u32[]{:S(2)}) collective-permute-start(f32[16,512]{1,0:T(8,128)S(1)} %get-tuple-element.92.sent), channel_id=1, source_target_pairs={{4,8},{12,16},{20,24},{28,32},{36,40},{44,48},{52,56},{60,64},{68,... | collective-permute-start | bytes 98312 | tf_op jit(solution)/shard_map/ppermute | solution.py:354
  37.6 26.7 %all-to-all-start = ((f32[128,1,128]{2,1,0:T(1,128)}), f32[128,1,128]{2,1,0:T(1,128)S(1)}, u32[]{:S(2)}, u32[]{:S(2)}) async-start(f32[128,1,128]{2,1,0:T(1,128)} %bitcast.6), calls=%async_computation | async-start | bytes 131072 | tf_op jit(solution)/shard_map/all_to_all | solution.py:407
  54.5 2.0 %collective-permute-start.8 = (f32[16,512]{1,0:T(8,128)S(1)}, f32[16,512]{1,0:T(8,128)S(1)}, u32[]{:S(2)}, u32[]{:S(2)}) collective-permute-start(f32[16,512]{1,0:T(8,128)S(1)} %get-tuple-element.95), channel_id=1, source_target_pairs={{0,4},{4,0},{8,12},{12,8},{16,20},{20,16},{24,28},{28,24},{32,36},... | collective-permute-start | bytes 98312 | tf_op jit(solution)/shard_map/ppermute | solution.py:351

commit v3 on v2

--- a/solution.py
+++ b/solution.py
@@ -339,19 +339,26 @@
     juncs = demand.shape[0]
     cap = boundary_pipe.shape[2]
     nets = lax.axis_size("net")
-    devices = nets * lax.axis_size("hour")
+    hour_blocks = lax.axis_size("hour")
+    devices = nets * hour_blocks
     field = ((pipes, hours), F32)
     heads = ((juncs, hours), F32)
     msg2 = ((2 * cap, hours), F32)
     half = ((hours // 2, hours // 2), BF16)
     on_chip = [(i, i ^ 1) for i in range(nets)]
-    across = [(i, i + 1) for i in range(1, nets - 1, 2)] + [(i + 1, i) for i in range(1, nets - 1, 2)]
+    across = []
+    for h in range(hour_blocks):
+        for i in range(1, nets - 1, 2):
+            a, b = i * hour_blocks + h, (i + 1) * hour_blocks + h
+            across += [(a, b), (b, a)]
+        for i in (0, nets - 1):
+            across.append((i * hour_blocks + h, i * hour_blocks + (h ^ 1)))
 
     def swap(x):
         return lax.ppermute(x, "net", on_chip)
 
     def cross(x):
-        return lax.ppermute(x, "net", across)
+        return lax.ppermute(x, ("net", "hour"), across)
 
     odd = (lax.axis_index("net") % 2).astype(jnp.int32).reshape(1, 1)
     msg, s_a, s_b, inc, l_a, l_b, own_match = call(

time: 66.3 us -> 58.6 us (0.88)
  starting transfers between devices: 35.9 us -> 26.9 us
  waiting for transfers between devices: 15.5 us -> 17 us
    ppermute x4, starting transfers between devices: 16.5 us -> 6.03 us  [cross(): return lax.ppermute(x, ('net', 'hour'), across)]
    ppermute x4, waiting for transfers between devices: 2.34 us -> 4.83 us  [cross(): return lax.ppermute(x, ('net', 'hour'), across)]
    ppermute x5, starting transfers between devices: 2.56 us -> 4.23 us  [swap(): return lax.ppermute(x, 'net', on_chip)]
    ppermute x5, waiting for transfers between devices: 5.36 us -> 4.3 us  [swap(): return lax.ppermute(x, 'net', on_chip)]
  transfers between devices with their start and end apart: 10 -> 10, of which waited for: 10 -> 10; matrix products, arithmetic and copies ran while one was open for 0% -> 0% of each run, Pallas kernels for 5% -> 6%
where the time goes in v3:
time: 58.6 us; the launch traced here: 58.4 us
  starting transfers between devices  26.9 us (46%)
  waiting for transfers between devices  17 us (29%)
  Pallas kernels  11.5 us (20%)
  local copies, waits for them, and re-layouts  2.3 us (4%)
  between operations  0.73 us (1%)
    all_to_all x1, starting transfers between devices, shards(): lax.all_to_all(row.reshape(devices, 1, 128), ('net', 'hour'), 0, 0, tiled...  16.6 us
    pallas_call x14, Pallas kernels, call(): pl.pallas_call(kernel, out_shape=tuple((shape(s, d) for s, d in outs)), i...  11.5 us
    all_to_all x1, waiting for transfers between devices, shards(): lax.all_to_all(row.reshape(devices, 1, 128), ('net', 'hour'), 0, 0, tiled...  7.84 us
    ppermute x4, starting transfers between devices, cross(): return lax.ppermute(x, ('net', 'hour'), across)  6.03 us
    ppermute x4, waiting for transfers between devices, cross(): return lax.ppermute(x, ('net', 'hour'), across)  4.83 us
    ppermute x5, waiting for transfers between devices, swap(): return lax.ppermute(x, 'net', on_chip)  4.3 us
    ppermute x5, starting transfers between devices, swap(): return lax.ppermute(x, 'net', on_chip)  4.23 us
    unnamed x22, local copies, waits for them, and re-layouts  2.3 us
  transfers between devices with their start and end apart: 10, of which 10 were waited for; matrix products, arithmetic and copies ran while one was open for 0% of the time, Pallas kernels for 6%

profile of v3, /device:TPU:1, one launch (start us, length us, event | category | flops | bytes accessed | tf_op | source)
XLA Modules:
  0.0 58.4 jit_solution(17172462164498561495)
XLA Ops:
  0.6 0.0 copy-start.6
  0.7 0.0 copy-start.8
  0.7 0.0 copy-start.9
  0.7 0.0 copy-start.5
  0.7 0.0 copy-start.7
  0.7 0.6 %copy-done.6 = s32[1,2,8]{2,1,0:T(2,128)S(1)} copy-done((s32[1,2,8]{2,1,0:T(2,128)S(1)}, s32[1,2,8]{2,1,0:T(2,128)}, u32[]{:S(2)}) %copy-start.6) | copy-done | bytes 88
  1.3 0.0 copy-done.8
  1.3 0.0 copy-done.9
  1.3 0.0 copy-done.5
  1.4 0.0 copy-done.7
  1.4 0.0 copy-start
  1.4 0.9 %copy-done = f32[128,512]{1,0:T(8,128)S(1)} copy-done((f32[128,512]{1,0:T(8,128)S(1)}, f32[128,512]{1,0:T(8,128)}, u32[]{:S(2)}) %copy-start) | copy-done | bytes 262168
  2.3 0.0 copy-start.3
  2.3 0.3 shard_map.114
  2.6 1.4 %collective-permute-start = (f32[16,512]{1,0:T(8,128)S(1)}, f32[16,512]{1,0:T(8,128)S(1)}, u32[]{:S(2)}, u32[]{:S(2)}) collective-permute-start(f32[16,512]{1,0:T(8,128)S(1)} %get-tuple-element.50), channel_id=1, source_target_pairs={{0,4},{4,0},{8,12},{12,8},{16,20},{20,16},{24,28},{28,24},{32,36},... | collective-permute-start | bytes 98312 | tf_op jit(solution)/shard_map/ppermute | solution.py:358
  4.0 0.9 %collective-permute-done.got = f32[16,512]{1,0:T(8,128)S(1)} collective-permute-done((f32[16,512]{1,0:T(8,128)S(1)}, f32[16,512]{1,0:T(8,128)S(1)}, u32[]{:S(2)}, u32[]{:S(2)}) %collective-permute-start) | collective-permute-done | bytes 32800 | tf_op jit(solution)/shard_map/ppermute | solution.py:358
  4.9 0.0 copy-done.3
  4.9 0.0 copy-start.1
  4.9 0.0 copy-start.2
  4.9 0.5 shard_map.115
  5.4 0.0 copy-start.4
  5.4 2.0 %collective-permute-start.1 = (f32[24,512]{1,0:T(8,128)S(1)}, f32[24,512]{1,0:T(8,128)S(1)}, u32[]{:S(2)}, u32[]{:S(2)}) collective-permute-start(f32[24,512]{1,0:T(8,128)S(1)} %get-tuple-element.57.sent), channel_id=1, source_target_pairs={{4,8},{8,4},{12,16},{16,12},{20,24},{24,20},{28,32},{32,28},{36,40... | collective-permute-start | bytes 147464 | tf_op jit(solution)/shard_map/ppermute | solution.py:361
  7.4 0.0 copy-start.10
  7.4 0.0 copy-done.1
  7.4 0.0 copy-done.2
  7.4 0.0 copy-done.4
  7.4 0.6 %copy-done.10 = f32[128]{0:T(128)S(1)} copy-done((f32[128]{0:T(128)S(1)}, f32[128]{0:T(128)}, u32[]{:S(2)}) %copy-start.10) | copy-done | bytes 536
  8.0 1.0 %shard_map.113 = (bf16[256,256]{1,0:T(8,128)(2,1)S(1)}, bf16[256,256]{1,0:T(8,128)(2,1)S(1)}, bf16[256,256]{1,0:T(8,128)(2,1)S(1)}, bf16[256,256]{1,0:T(8,128)(2...) custom-call(f32[1,512]{1,0:T(1,128)S(1)} %bitcast.10, ...), custom_call_target="tpu_custom_call" | custom-call | tf_op jit(solution)/shard_map/pallas_call | solution.py:317
  9.1 0.4 collective-permute-done.1.got
  9.4 0.7 %shard_map.116 = (f32[128,512]{1,0:T(8,128)S(1)}, f32[16,512]{1,0:T(8,128)S(1)}, f32[8,128]{1,0:T(8,128)S(1)}) custom-call(f32[128,512]{1,0:T(8,128)S(1)} %get-tuple-element.49.base, f32[96,512]{1,0:T(8,128)S(1)} %get-tuple-element.56.part, f32[24,512]{1,0:T(8,128)S(1)} %get-tuple-element.57.sent, f32[24,512]{1,0:T(8,128)S(1)} %collective-permute-done.1.got, ...), custom_call_target="tpu_custom_call" | custom-call | tf_op jit(solution)/shard_map/pallas_call | solution.py:317
  10.1 0.4 collective-permute-start.2
  10.5 0.9 %collective-permute-done.2.refs_2_ = f32[16,512]{1,0:T(8,128)S(1)} collective-permute-done((f32[16,512]{1,0:T(8,128)S(1)}, f32[16,512]{1,0:T(8,128)S(1)}, u32[]{:S(2)}, u32[]{:S(2)}) %collective-permute-start.2) | collective-permute-done | bytes 32800 | tf_op jit(solution)/shard_map/ppermute | solution.py:358
  11.4 0.7 %shard_map.117 = (f32[128,512]{1,0:T(8,128)S(1)}, f32[96,512]{1,0:T(8,128)S(1)}, f32[16,512]{1,0:T(8,128)S(1)}) custom-call(f32[128,512]{1,0:T(8,128)S(1)} %get-tuple-element.60.refs_0_, f32[16,512]{1,0:T(8,128)S(1)} %get-tuple-element.61.refs_1_, f32[16,512]{1,0:T(8,128)S(1)} %collective-permute-done.2.refs_2_, ...), custom_call_target="tpu_custom_call" | custom-call | tf_op jit(solution)/shard_map/pallas_call | solution.py:317
  12.1 1.4 %collective-permute-start.3 = (f32[16,512]{1,0:T(8,128)S(1)}, f32[16,512]{1,0:T(8,128)S(1)}, u32[]{:S(2)}, u32[]{:S(2)}) collective-permute-start(f32[16,512]{1,0:T(8,128)S(1)} %get-tuple-element.77.sent), channel_id=1, source_target_pairs={{4,8},{8,4},{12,16},{16,12},{20,24},{24,20},{28,32},{32,28},{36,40... | collective-permute-start | bytes 98312 | tf_op jit(solution)/shard_map/ppermute | solution.py:361
  13.5 0.8 %shard_map.118 = (f32[128,512]{1,0:T(8,128)S(1)}, f32[8,128]{1,0:T(8,128)S(1)}) custom-call(f32[128,512]{1,0:T(8,128)S(1)} %get-tuple-element.62.r.before.r0, f32[128,512]{1,0:T(8,128)S(1)} %get-tuple-element.63.weight, bf16[256,256]{1,0:T(8,128)(2,1)S(1)} %get-tuple-element.64.t0h, bf16[256,256]{1,0:T(8,128)(2,1)S(1)} %get-tuple-element.65.t0l, ...), custom_call_target="tpu_custom_call" | custom-call | tf_op jit(solution)/shard_map/pallas_call | solution.py:317
  14.4 1.4 %collective-permute-done.3.got = f32[16,512]{1,0:T(8,128)S(1)} collective-permute-done((f32[16,512]{1,0:T(8,128)S(1)}, f32[16,512]{1,0:T(8,128)S(1)}, u32[]{:S(2)}, u32[]{:S(2)}) %collective-permute-start.3) | collective-permute-done | bytes 32800 | tf_op jit(solution)/shard_map/ppermute | solution.py:361
  15.8 0.7 %shard_map.119 = (f32[128,512]{1,0:T(8,128)S(1)}, f32[16,512]{1,0:T(8,128)S(1)}) custom-call(f32[128,512]{1,0:T(8,128)S(1)} %get-tuple-element.74.q, f32[128,128]{1,0:T(8,128)S(1)} %get-tuple-element.75.rvar, f32[8,128]{1,0:T(8,128)S(1)} %get-tuple-element.73.tau, f32[96,512]{1,0:T(8,128)S(1)} %get-tuple-element.76.part, ...), custom_call_target="tpu_custom_call" | custom-call | tf_op jit(solution)/shard_map/pallas_call | solution.py:317
  16.5 0.6 %collective-permute-start.4 = (f32[16,512]{1,0:T(8,128)S(1)}, f32[16,512]{1,0:T(8,128)S(1)}, u32[]{:S(2)}, u32[]{:S(2)}) collective-permute-start(f32[16,512]{1,0:T(8,128)S(1)} %get-tuple-element.80.refs_1_), channel_id=1, source_target_pairs={{0,4},{4,0},{8,12},{12,8},{16,20},{20,16},{24,28},{28,24},{32,36},... | collective-permute-start | bytes 98312 | tf_op jit(solution)/shard_map/ppermute | solution.py:358
  17.2 0.9 %collective-permute-done.4.refs_2_ = f32[16,512]{1,0:T(8,128)S(1)} collective-permute-done((f32[16,512]{1,0:T(8,128)S(1)}, f32[16,512]{1,0:T(8,128)S(1)}, u32[]{:S(2)}, u32[]{:S(2)}) %collective-permute-start.4) | collective-permute-done | bytes 32800 | tf_op jit(solution)/shard_map/ppermute | solution.py:358
  18.0 0.7 %shard_map.120 = (f32[128,512]{1,0:T(8,128)S(1)}, f32[96,512]{1,0:T(8,128)S(1)}, f32[16,512]{1,0:T(8,128)S(1)}) custom-call(f32[8,128]{1,0:T(8,128)S(1)} %get-tuple-element.73.tau, f32[128,512]{1,0:T(8,128)S(1)} %get-tuple-element.79.refs_0_, f32[16,512]{1,0:T(8,128)S(1)} %get-tuple-element.80.refs_1_, f32[16,512]{1,0:T(8,128)S(1)} %collective-permute-done.4.refs_2_, ...), custom_call_target="tpu_custom_call" | custom-call | tf_op jit(solution)/shard_map/pallas_call | solution.py:317
  18.8 0.8 %collective-permute-start.5 = (f32[16,512]{1,0:T(8,128)S(1)}, f32[16,512]{1,0:T(8,128)S(1)}, u32[]{:S(2)}, u32[]{:S(2)}) collective-permute-start(f32[16,512]{1,0:T(8,128)S(1)} %get-tuple-element.85.sent), channel_id=1, source_target_pairs={{4,8},{8,4},{12,16},{16,12},{20,24},{24,20},{28,32},{32,28},{36,40... | collective-permute-start | bytes 98312 | tf_op jit(solution)/shard_map/ppermute | solution.py:361
  19.6 0.8 %shard_map.121 = (f32[128,512]{1,0:T(8,128)S(1)}, f32[16,128]{1,0:T(8,128)S(1)}) custom-call(f32[128,512]{1,0:T(8,128)S(1)} %get-tuple-element.81.r.before.r1, f32[128,512]{1,0:T(8,128)S(1)} %get-tuple-element.62.r.before.r0, f32[128,512]{1,0:T(8,128)S(1)} %get-tuple-element.63.weight, bf16[256,256]{1,0:T(8,128)(2,1)S(1)} %get-tuple-element.64.t0h, ...), custom_call_target="tpu_custom_call" | custom-call | tf_op jit(solution)/shard_map/pallas_call | solution.py:317
  20.4 2.0 %collective-permute-done.5.got = f32[16,512]{1,0:T(8,128)S(1)} collective-permute-done((f32[16,512]{1,0:T(8,128)S(1)}, f32[16,512]{1,0:T(8,128)S(1)}, u32[]{:S(2)}, u32[]{:S(2)}) %collective-permute-start.5) | collective-permute-done | bytes 32800 | tf_op jit(solution)/shard_map/ppermute | solution.py:361
  22.4 0.7 %shard_map.122 = (f32[128,512]{1,0:T(8,128)S(1)}, f32[16,512]{1,0:T(8,128)S(1)}) custom-call(f32[128,512]{1,0:T(8,128)S(1)} %get-tuple-element.83.q, f32[128,128]{1,0:T(8,128)S(1)} %get-tuple-element.75.rvar, f32[8,128]{1,0:T(8,128)S(1)} %get-tuple-element.73.tau, f32[96,512]{1,0:T(8,128)S(1)} %get-tuple-element.84.part, ...), custom_call_target="tpu_custom_call" | custom-call | tf_op jit(solution)/shard_map/pallas_call | solution.py:317
  23.1 0.6 %collective-permute-start.6 = (f32[16,512]{1,0:T(8,128)S(1)}, f32[16,512]{1,0:T(8,128)S(1)}, u32[]{:S(2)}, u32[]{:S(2)}) collective-permute-start(f32[16,512]{1,0:T(8,128)S(1)} %get-tuple-element.87.refs_1_), channel_id=1, source_target_pairs={{0,4},{4,0},{8,12},{12,8},{16,20},{20,16},{24,28},{28,24},{32,36},... | collective-permute-start | bytes 98312 | tf_op jit(solution)/shard_map/ppermute | solution.py:358
  23.8 0.9 %collective-permute-done.6.refs_2_ = f32[16,512]{1,0:T(8,128)S(1)} collective-permute-done((f32[16,512]{1,0:T(8,128)S(1)}, f32[16,512]{1,0:T(8,128)S(1)}, u32[]{:S(2)}, u32[]{:S(2)}) %collective-permute-start.6) | collective-permute-done | bytes 32800 | tf_op jit(solution)/shard_map/ppermute | solution.py:358
  24.6 0.7 %shard_map.123 = (f32[128,512]{1,0:T(8,128)S(1)}, f32[96,512]{1,0:T(8,128)S(1)}, f32[16,512]{1,0:T(8,128)S(1)}) custom-call(f32[8,128]{1,0:T(8,128)S(1)} %get-tuple-element.73.tau, f32[128,512]{1,0:T(8,128)S(1)} %get-tuple-element.86.refs_0_, f32[16,512]{1,0:T(8,128)S(1)} %get-tuple-element.87.refs_1_, f32[16,512]{1,0:T(8,128)S(1)} %collective-permute-done.6.refs_2_, ...), custom_call_target="tpu_custom_call" | custom-call | tf_op jit(solution)/shard_map/pallas_call | solution.py:317
  25.4 1.8 %collective-permute-start.7 = (f32[16,512]{1,0:T(8,128)S(1)}, f32[16,512]{1,0:T(8,128)S(1)}, u32[]{:S(2)}, u32[]{:S(2)}) collective-permute-start(f32[16,512]{1,0:T(8,128)S(1)} %get-tuple-element.92.sent), channel_id=1, source_target_pairs={{4,8},{8,4},{12,16},{16,12},{20,24},{24,20},{28,32},{32,28},{36,40... | collective-permute-start | bytes 98312 | tf_op jit(solution)/shard_map/ppermute | solution.py:361
  27.1 0.8 %shard_map.124 = (f32[128,512]{1,0:T(8,128)S(1)}, f32[16,128]{1,0:T(8,128)S(1)}) custom-call(f32[128,512]{1,0:T(8,128)S(1)} %get-tuple-element.88.r.r2, f32[128,512]{1,0:T(8,128)S(1)} %get-tuple-element.81.r.before.r1, f32[128,512]{1,0:T(8,128)S(1)} %get-tuple-element.63.weight, bf16[256,256]{1,0:T(8,128)(2,1)S(1)} %get-tuple-element.64.t0h, ...), custom_call_target="tpu_custom_call" | custom-call | tf_op jit(solution)/shard_map/pallas_call | solution.py:317
  28.0 1.1 %collective-permute-done.7.got = f32[16,512]{1,0:T(8,128)S(1)} collective-permute-done((f32[16,512]{1,0:T(8,128)S(1)}, f32[16,512]{1,0:T(8,128)S(1)}, u32[]{:S(2)}, u32[]{:S(2)}) %collective-permute-start.7) | collective-permute-done | bytes 32800 | tf_op jit(solution)/shard_map/ppermute | solution.py:361
  29.0 1.1 %shard_map.125 = (f32[128,512]{1,0:T(8,128)S(1)}, f32[16,512]{1,0:T(8,128)S(1)}, f32[128,128]{1,0:T(8,128)}) custom-call(f32[8,128]{1,0:T(8,128)S(1)} %get-tuple-element.72.r0m, f32[16,128]{1,0:T(8,128)S(1)} %get-tuple-element.82.r1m, f32[16,128]{1,0:T(8,128)S(1)} %get-tuple-element.89.r2m, f32[128,512]{1,0:T(8,128)S(1)} %get-tuple-element.88.r.r2, ...), custom_call_target="tpu_custom_call" | custom-call | tf_op jit(solution)/shard_map/pallas_call | solution.py:317
  30.2 16.6 %all-to-all-start = ((f32[128,1,128]{2,1,0:T(1,128)}), f32[128,1,128]{2,1,0:T(1,128)S(1)}, u32[]{:S(2)}, u32[]{:S(2)}) async-start(f32[128,1,128]{2,1,0:T(1,128)} %bitcast.6), calls=%async_computation | async-start | bytes 131072 | tf_op jit(solution)/shard_map/all_to_all | solution.py:414
  46.8 1.1 %collective-permute-start.8 = (f32[16,512]{1,0:T(8,128)S(1)}, f32[16,512]{1,0:T(8,128)S(1)}, u32[]{:S(2)}, u32[]{:S(2)}) collective-permute-start(f32[16,512]{1,0:T(8,128)S(1)} %get-tuple-element.95), channel_id=1, source_target_pairs={{0,4},{4,0},{8,12},{12,8},{16,20},{20,16},{24,28},{28,24},{32,36},... | collective-permute-start | bytes 98312 | tf_op jit(solution)/shard_map/ppermute | solution.py:358
  48.0 0.9 %collective-permute-done.8.got = f32[16,512]{1,0:T(8,128)S(1)} collective-permute-done((f32[16,512]{1,0:T(8,128)S(1)}, f32[16,512]{1,0:T(8,128)S(1)}, u32[]{:S(2)}, u32[]{:S(2)}) %collective-permute-start.8) | collective-permute-done | bytes 32800 | tf_op jit(solution)/shard_map/ppermute | solution.py:358
  48.8 7.8 %all-to-all-done = f32[128,1,128]{2,1,0:T(1,128)S(1)} async-done(((f32[128,1,128]{2,1,0:T(1,128)}), f32[128,1,128]{2,1,0:T(1,128)S(1)}, u32[]{:S(2)}, u32[]{:S(2)}) %all-to-all-start) | async-done | bytes 65568 | tf_op jit(solution)/shard_map/all_to_all | solution.py:414
  56.6 1.8 %shard_map.126 = (f32[128,512]{1,0:T(8,128)}, f32[128,512]{1,0:T(8,128)}) custom-call(f32[128,128]{1,0:T(8,128)S(1)} %bitcast.9, f32[8,128]{1,0:T(8,128)S(1)} %get-tuple-element.73.tau, f32[128,512]{1,0:T(8,128)S(1)} %copy-done.1, f32[128,512]{1,0:T(8,128)S(1)} %get-tuple-element.62.r.before.r0, f32[128,512]{1,0:T(8,128)S(1)} %get-tuple-element.81.r.before.r1, ...), custom_call_target="tpu_custom_call" | custom-call | tf_op jit(solution)/shard_map/pallas_call | solution.py:317
Async XLA Ops:
  0.6 0.7 %copy-start.6 = (s32[1,2,8]{2,1,0:T(2,128)S(1)}, s32[1,2,8]{2,1,0:T(2,128)}, u32[]{:S(2)}) copy-start(s32[1,2,8]{2,1,0:T(2,128)} %aj.1) | copy-start | bytes 196
  0.7 0.7 %copy-start.8 = (s32[128]{0:T(128)S(1)}, s32[128]{0:T(128)}, u32[]{:S(2)}) copy-start(s32[128]{0:T(128)} %param.16) | copy-start | bytes 1540
  0.7 0.7 %copy-start.9 = (s32[128]{0:T(128)S(1)}, s32[128]{0:T(128)}, u32[]{:S(2)}) copy-start(s32[128]{0:T(128)} %param.15) | copy-start | bytes 1540
  0.7 0.7 %copy-start.5 = (s32[1,2,8]{2,1,0:T(2,128)S(1)}, s32[1,2,8]{2,1,0:T(2,128)}, u32[]{:S(2)}) copy-start(s32[1,2,8]{2,1,0:T(2,128)} %bp.1) | copy-start | bytes 196
  0.7 0.7 %copy-start.7 = (s32[1,2]{1,0:T(1,128)S(1)}, s32[1,2]{1,0:T(1,128)}, u32[]{:S(2)}) copy-start(s32[1,2]{1,0:T(1,128)} %bc.1) | copy-start | bytes 28
  1.4 1.0 %copy-start = (f32[128,512]{1,0:T(8,128)S(1)}, f32[128,512]{1,0:T(8,128)}, u32[]{:S(2)}) copy-start(f32[128,512]{1,0:T(8,128)} %prior.7) | copy-start | bytes 786436
  2.3 2.6 %copy-start.3 = (f32[96,512]{1,0:T(8,128)S(1)}, f32[96,512]{1,0:T(8,128)}, u32[]{:S(2)}) copy-start(f32[96,512]{1,0:T(8,128)} %demand.1) | copy-start | bytes 589828
  2.6 2.3 %collective-permute-start = (f32[16,512]{1,0:T(8,128)S(1)}, f32[16,512]{1,0:T(8,128)S(1)}, u32[]{:S(2)}, u32[]{:S(2)}) collective-permute-start(f32[16,512]{1,0:T(8,128)S(1)} %get-tuple-element.50), channel_id=1, source_target_pairs={{0,4},{4,0},{8,12},{12,8},{16,20},{20,16},{24,28},{28,24},{32,36},... | collective-permute-start | bytes 98312 | tf_op jit(solution)/shard_map/ppermute | solution.py:358
  4.9 2.5 %copy-start.1 = (f32[128,512]{1,0:T(8,128)S(1)}, f32[128,512]{1,0:T(8,128)}, u32[]{:S(2)}) copy-start(f32[128,512]{1,0:T(8,128)} %prior.7) | copy-start | bytes 786436
  4.9 2.5 %copy-start.2 = (f32[128,512]{1,0:T(8,128)S(1)}, f32[128,512]{1,0:T(8,128)}, u32[]{:S(2)}) copy-start(f32[128,512]{1,0:T(8,128)} %measured.1) | copy-start | bytes 786436
  5.4 2.0 %copy-start.4 = (f32[512]{0:T(512)S(1)}, f32[512]{0:T(512)}, u32[]{:S(2)}) copy-start(f32[512]{0:T(512)} %param.14) | copy-start | bytes 6148
  5.4 4.0 %collective-permute-start.1 = (f32[24,512]{1,0:T(8,128)S(1)}, f32[24,512]{1,0:T(8,128)S(1)}, u32[]{:S(2)}, u32[]{:S(2)}) collective-permute-start(f32[24,512]{1,0:T(8,128)S(1)} %get-tuple-element.57.sent), channel_id=1, source_target_pairs={{4,8},{8,4},{12,16},{16,12},{20,24},{24,20},{28,32},{32,28},{36,40... | collective-permute-start | bytes 147464 | tf_op jit(solution)/shard_map/ppermute | solution.py:361
  7.4 0.7 %copy-start.10 = (f32[128]{0:T(128)S(1)}, f32[128]{0:T(128)}, u32[]{:S(2)}) copy-start(f32[128]{0:T(128)} %param.13) | copy-start | bytes 1540
  10.1 1.3 %collective-permute-start.2 = (f32[16,512]{1,0:T(8,128)S(1)}, f32[16,512]{1,0:T(8,128)S(1)}, u32[]{:S(2)}, u32[]{:S(2)}) collective-permute-start(f32[16,512]{1,0:T(8,128)S(1)} %get-tuple-element.61.refs_1_), channel_id=1, source_target_pairs={{0,4},{4,0},{8,12},{12,8},{16,20},{20,16},{24,28},{28,24},{32,36},... | collective-permute-start | bytes 98312 | tf_op jit(solution)/shard_map/ppermute | solution.py:358
  12.1 3.6 %collective-permute-start.3 = (f32[16,512]{1,0:T(8,128)S(1)}, f32[16,512]{1,0:T(8,128)S(1)}, u32[]{:S(2)}, u32[]{:S(2)}) collective-permute-start(f32[16,512]{1,0:T(8,128)S(1)} %get-tuple-element.77.sent), channel_id=1, source_target_pairs={{4,8},{8,4},{12,16},{16,12},{20,24},{24,20},{28,32},{32,28},{36,40... | collective-permute-start | bytes 98312 | tf_op jit(solution)/shard_map/ppermute | solution.py:361
  16.5 1.5 %collective-permute-start.4 = (f32[16,512]{1,0:T(8,128)S(1)}, f32[16,512]{1,0:T(8,128)S(1)}, u32[]{:S(2)}, u32[]{:S(2)}) collective-permute-start(f32[16,512]{1,0:T(8,128)S(1)} %get-tuple-element.80.refs_1_), channel_id=1, source_target_pairs={{0,4},{4,0},{8,12},{12,8},{16,20},{20,16},{24,28},{28,24},{32,36},... | collective-permute-start | bytes 98312 | tf_op jit(solution)/shard_map/ppermute | solution.py:358
  18.8 3.6 %collective-permute-start.5 = (f32[16,512]{1,0:T(8,128)S(1)}, f32[16,512]{1,0:T(8,128)S(1)}, u32[]{:S(2)}, u32[]{:S(2)}) collective-permute-start(f32[16,512]{1,0:T(8,128)S(1)} %get-tuple-element.85.sent), channel_id=1, source_target_pairs={{4,8},{8,4},{12,16},{16,12},{20,24},{24,20},{28,32},{32,28},{36,40... | collective-permute-start | bytes 98312 | tf_op jit(solution)/shard_map/ppermute | solution.py:361
  23.1 1.5 %collective-permute-start.6 = (f32[16,512]{1,0:T(8,128)S(1)}, f32[16,512]{1,0:T(8,128)S(1)}, u32[]{:S(2)}, u32[]{:S(2)}) collective-permute-start(f32[16,512]{1,0:T(8,128)S(1)} %get-tuple-element.87.refs_1_), channel_id=1, source_target_pairs={{0,4},{4,0},{8,12},{12,8},{16,20},{20,16},{24,28},{28,24},{32,36},... | collective-permute-start | bytes 98312 | tf_op jit(solution)/shard_map/ppermute | solution.py:358
  25.4 3.7 %collective-permute-start.7 = (f32[16,512]{1,0:T(8,128)S(1)}, f32[16,512]{1,0:T(8,128)S(1)}, u32[]{:S(2)}, u32[]{:S(2)}) collective-permute-start(f32[16,512]{1,0:T(8,128)S(1)} %get-tuple-element.92.sent), channel_id=1, source_target_pairs={{4,8},{8,4},{12,16},{16,12},{20,24},{24,20},{28,32},{32,28},{36,40... | collective-permute-start | bytes 98312 | tf_op jit(solution)/shard_map/ppermute | solution.py:361
  30.2 26.5 %all-to-all-start = ((f32[128,1,128]{2,1,0:T(1,128)}), f32[128,1,128]{2,1,0:T(1,128)S(1)}, u32[]{:S(2)}, u32[]{:S(2)}) async-start(f32[128,1,128]{2,1,0:T(1,128)} %bitcast.6), calls=%async_computation | async-start | bytes 131072 | tf_op jit(solution)/shard_map/all_to_all | solution.py:414
  46.8 2.0 %collective-permute-start.8 = (f32[16,512]{1,0:T(8,128)S(1)}, f32[16,512]{1,0:T(8,128)S(1)}, u32[]{:S(2)}, u32[]{:S(2)}) collective-permute-start(f32[16,512]{1,0:T(8,128)S(1)} %get-tuple-element.95), channel_id=1, source_target_pairs={{0,4},{4,0},{8,12},{12,8},{16,20},{20,16},{24,28},{28,24},{32,36},... | collective-permute-start | bytes 98312 | tf_op jit(solution)/shard_map/ppermute | solution.py:358

commit v4 on v3

v4 whole, which is shorter than its diff:
```python
import jax
import jax.numpy as jnp
from jax import lax
from jax.experimental import pallas as pl
from jax.experimental.pallas import tpu as pltpu
from jax.sharding import PartitionSpec as P

EDGE = 1.5
PENALTY = 4.0
F32 = jnp.float32
BF16 = jnp.bfloat16


def iota(shape, dim):
    return lax.broadcasted_iota(jnp.int32, shape, dim)


def thirds(v):
    a = v.astype(BF16)
    rest = v - a.astype(F32)
    b = rest.astype(BF16)
    c = (rest - b.astype(F32)).astype(BF16)
    return a, b, c


def halves(v):
    a = v.astype(BF16)
    return a, (v - a.astype(F32)).astype(BF16)


def mm(a, b):
    return jnp.dot(a, b, preferred_element_type=F32)


def pick(exact, v):
    a, b, c = thirds(v)
    return (mm(exact, c) + mm(exact, b)) + mm(exact, a)


def product(x, t_hi, t_lo):
    hi, lo = halves(x)
    return (mm(lo, t_hi) + mm(hi, t_lo)) + mm(hi, t_hi)


def forward(v, taps):
    t0h, t0l, t1h, t1l = taps
    rows = v.shape[0]
    half = v.shape[1] // 2
    both = jnp.concatenate([v[:, :half], v[:, half:]], axis=0)
    near = product(both, t0h[...], t0l[...])
    far = product(v[:, :half], t1h[...], t1l[...])
    return jnp.concatenate([near[:rows], near[rows:] + far], axis=1)


def backward(v, taps):
    t0h, t0l, t1h, t1l = taps
    rows = v.shape[0]
    half = v.shape[1] // 2
    both = jnp.concatenate([v[:, :half], v[:, half:]], axis=0)
    near = product(both, t0h[...], t0l[...])
    far = product(v[:, half:], t1h[...], t1l[...])
    return jnp.concatenate([near[:rows] + far, near[rows:]], axis=1)


def lanes_sum(v):
    rows, cols = v.shape
    total = None
    for i in range(0, rows, 8):
        for j in range(0, cols, 128):
            part = v[i : i + 8, j : j + 128]
            total = part if total is None else total + part
    return total


def column(row, n):
    return jnp.sum(jnp.where(iota((n, n), 0) == iota((n, n), 1), row, 0.0), axis=1, keepdims=True)


def stack3(v):
    a = v.astype(BF16).astype(F32)
    rest = v - a
    b = rest.astype(BF16).astype(F32)
    return jnp.concatenate([rest - b, b, a], axis=0).astype(BF16)


def thrice(m):
    return jnp.concatenate([m, m, m], axis=1).astype(BF16)


def fold(tile):
    x = jnp.sum(tile, axis=0, keepdims=True)
    for s in (64, 32, 16):
        x = x + pltpu.roll(x, s, 1)
    return x


def chosen(odd, ref, flip):
    lower, upper = ref[0, 0:1, :].astype(F32), ref[0, 1:2, :].astype(F32)
    return jnp.where(odd != flip, lower, upper)


def selectors(odd, bp, bc, pipes):
    cap = bp.shape[2]
    counts = bc[0:1, :].astype(F32)
    count_a = jnp.where(odd, counts[:, 0:1], counts[:, 1:2])
    count_b = jnp.where(odd, counts[:, 1:2], counts[:, 0:1])
    slot = iota((cap, 1), 0).astype(F32)
    live_a = jnp.where(slot < count_a, 1.0, 0.0)
    live_b = jnp.where(slot < count_b, 1.0, 0.0)
    pipe = iota((cap, pipes), 1).astype(F32)
    sel_a = jnp.where(column(chosen(odd, bp, False), cap) == pipe, live_a, 0.0)
    sel_b = jnp.where(column(chosen(odd, bp, True), cap) == pipe, live_b, 0.0)
    return sel_a, sel_b, live_a


def open_kernel(par, prior_in, *refs):
    count = 9
    ins, prior, copies = (prior_in, *refs[: count - 1]), refs[count - 1], refs[count - 1 : 2 * count - 1]
    msg, sems = refs[2 * count - 1 :]
    moves = [pltpu.make_async_copy(i, o, sems.at[k]) for k, (i, o) in enumerate(zip(ins, copies))]
    bp, bc = copies[1], copies[2]
    for m in moves:
        m.start()
    for m in moves[:3]:
        m.wait()
    cap = bp.shape[2]
    sel_a, _, live_a = selectors(par[0, 0] == 1, bp, bc, prior.shape[0])
    msg[0:cap, :] = -pick(sel_a.astype(BF16), prior[...])
    msg[cap:, :] = jnp.broadcast_to(live_a, (cap, prior.shape[1]))
    for m in moves[3:]:
        m.wait()


def lists_kernel(par, sent, prior, bp, bc, aj, head, tail, demand, s_a, s_at, inc, l_a, l_b, it_sb, out_b, out_a, mid_b, mid_a, own, gain, part, base):
    cap = bp.shape[2]
    pipes = prior.shape[0]
    juncs = inc.shape[0]
    odd = par[0, 0] == 1
    sel_a, sel_b, _ = selectors(odd, bp, bc, pipes)
    inner = 1.0 - jnp.sum(sel_a + sel_b, axis=0, keepdims=True)
    junction = iota((juncs, pipes), 0)
    heads = jnp.where(junction == head[...], inner, 0.0)
    tails = jnp.where(junction == tail[...], 1.0, 0.0)
    both = heads - tails
    land = iota((juncs, cap), 0).astype(F32)
    to_a, to_b = chosen(odd, aj, False), chosen(odd, aj, True)
    land_a = jnp.where(land == to_a, 1.0, 0.0)
    land_b = jnp.where(land == to_b, 1.0, 0.0)
    row = iota((cap, juncs), 1).astype(F32)
    land_at = jnp.where(row == column(to_a, cap), 1.0, 0.0)
    land_bt = jnp.where(row == column(to_b, cap), 1.0, 0.0)
    square = jnp.transpose(jnp.concatenate([both, jnp.zeros((pipes - juncs, pipes), F32)], axis=0))
    both_t = square[:, :juncs]
    pad = jnp.zeros((128 - 2 * cap, 128), F32)
    turned = jnp.transpose(jnp.concatenate([sel_a, sel_b, pad], axis=0))
    sel_at, sel_bt = turned[:, :cap], turned[:, cap : 2 * cap]
    both16, a16, b16 = both.astype(BF16), land_a.astype(BF16), land_b.astype(BF16)
    bt16 = land_bt.astype(BF16)
    s_a[...] = sel_a.astype(BF16)
    s_at[...] = sel_at.astype(BF16)
    inc[...] = both16
    l_a[...] = a16
    l_b[...] = b16
    it_sb[...] = jnp.concatenate([both_t, sel_bt], axis=1).astype(BF16)
    b_inc = mm(bt16, both16)
    a_inc = mm(sel_a.astype(BF16), both_t.astype(BF16))
    out_b[...] = jnp.concatenate([sel_b, b_inc], axis=0).astype(BF16)
    out_a[...] = jnp.concatenate([land_at, a_inc], axis=0).astype(BF16)
    mid_b[...] = thrice(jnp.concatenate([mm(b_inc.astype(BF16), sel_at.astype(BF16)), mm(bt16, a16)], axis=1))
    mid_a[...] = thrice(jnp.concatenate([mm(land_at.astype(BF16), b16), mm(a_inc.astype(BF16), b16)], axis=0))
    own[...] = mm(bt16, b16)
    gain[...] = jnp.full(gain.shape, PENALTY, F32)
    x = prior[...]
    p = demand[...] - pick(both16, x)
    part[...] = p
    base[0:cap, :] = -pick(sel_b.astype(BF16), x)
    base[cap:, :] = pick(bt16, p)


def across_first(got, base, mid_b, own, msg, arrived, live):
    cap = own.shape[0]
    arr = got[0:cap, :]
    arrived[...] = arr
    live[...] = got[cap:, 0:128]
    msg[0:cap, :] = base[0:cap, :]
    both = jnp.concatenate([jnp.zeros_like(arr), arr], axis=0)
    msg[cap : 2 * cap, :] = base[cap:, :] + mm(mid_b[...], stack3(both))
    msg[2 * cap :, :] = jnp.zeros((cap, msg.shape[1]), F32)
    msg[2 * cap :, 0:cap] = own[...]


def across_next(gain, sent, got, live, base, mid_b, msg, arrived):
    cap = live.shape[0]
    g = gain[0:1, 0:1]
    added = g * got[0:cap, :]
    arr = got[cap:, :] + (g * live[:, 0:1]) * sent[0:cap, :]
    arrived[...] = arr
    msg[0:cap, :] = base[0:cap, :]
    msg[cap:, :] = base[cap:, :] + mm(mid_b[...], stack3(jnp.concatenate([added, arr], axis=0)))


def back_kernel(gain, got, base, mid_a, msg):
    cap = got.shape[0] // 2 if got.shape[0] == msg.shape[0] else got.shape[0] // 3
    x = mm(mid_a[...], stack3(got[0:cap, :]))
    msg[0:cap, :] = base[0:cap, :] + x[0:cap]
    msg[cap:, :] = base[cap:, :] + gain[0:1, 0:1] * x[cap:]


def outward(gain, part, near, s_a, out_a, base):
    cap = s_a.shape[0]
    x = pick(out_a[...], part)
    base[0:cap, :] = x[0:cap]
    base[cap:, :] = gain * x[cap:] + pick(s_a[...], near)


def inside_first(
    sent, coef, sigma, measured, prior, part_in, arrived, l_a, s_a, out_a,
    t0h, t0l, t1h, t1l, u0h, u0l, u1h, u1l, weight, near, rvar, gain, part, base,
):
    length = coef.shape[1]
    half = length // 2
    c = coef[...]
    shifted = pltpu.roll(jnp.broadcast_to(c, (half, length)), 0, 1, stride=1, stride_axis=0)
    upper = iota((half, half), 1) >= iota((half, half), 0)
    t0 = jnp.where(upper, shifted[:, :half], 0.0)
    t1 = shifted[:, half:]
    for hi, lo, x in ((t0h, t0l, t0), (t1h, t1l, t1), (u0h, u0l, t0.T), (u1h, u1l, t1.T)):
        a, b = halves(x)
        hi[...] = a
        lo[...] = b
    size = jnp.sum(jnp.abs(c), axis=1, keepdims=True)
    scale = 1.0 / (4.0 * size * size + 64.0)
    gain[...] = jnp.broadcast_to(PENALTY * scale, gain.shape)
    sig = jnp.transpose(jnp.broadcast_to(sigma[...], (128, 128)))[:, 0:1]
    rsig = 1.0 / sig
    whitened = forward((measured[...] - prior[...]) * rsig, (t0h, t0l, t1h, t1l))
    h = EDGE / jnp.maximum(jnp.abs(whitened), EDGE)
    weight[...] = h
    n = backward(h * whitened, (u0h, u0l, u1h, u1l)) * rsig
    near[...] = n
    rvar[...] = jnp.broadcast_to(rsig * rsig * scale, rvar.shape)
    p = part_in[...] + pick(l_a[...], arrived[...])
    part[...] = p
    outward(PENALTY, p, n, s_a, out_a, base)


def inside(gain0, gain, sent, w, got, arrived, weight, rvar, s_a, s_at, inc, l_a, out_a, taps, r_out, part, near, base):
    cap = s_a.shape[0]
    r = w[...] + gain0[0:1, 0:1] * pick(s_at[...], got[0:cap, :])
    r_out[...] = r
    p = pick(inc[...], r) + pick(l_a[...], arrived[...])
    part[...] = p
    n = backward(weight[...] * forward(r, taps[:4]), taps[4:]) * rvar[:, 0:1]
    near[...] = n
    outward(gain[0:1, 0:1], p, n, s_a, out_a, base)
    return r, p, n


def inside_one(*refs):
    *refs, sums = refs
    r, _, _ = inside(*refs[:13], refs[13:21], *refs[21:])
    sums[...] = lanes_sum(r * r)


def inside_two(before, *refs):
    *refs, sums = refs
    r, _, _ = inside(*refs[:13], refs[13:21], *refs[21:])
    sums[0:8, :] = lanes_sum(before[...] * r)
    sums[8:16, :] = lanes_sum(r * r)


def inside_three(before, sum0, sum1, *refs):
    *refs, row = refs
    gain = refs[1]
    r, p, n = inside(*refs[:13], refs[13:21], *refs[21:])
    tiles = (
        sum0[0:8, :], sum1[0:8, :], sum1[8:16, :], lanes_sum(before[...] * r), lanes_sum(r * r),
        lanes_sum(r * n) + gain[0:1, 0:1] * lanes_sum(p * p),
    )
    lane = iota((1, 128), 1) // 16
    out = jnp.zeros((1, 128), F32)
    for k, tile in enumerate(tiles):
        out = jnp.where(lane == k, fold(tile), out)
    row[...] = jnp.broadcast_to(out, row.shape)


def close_kernel(gain, sent, got, own, row, rows):
    cap = own.shape[0]
    f = got[0:cap, :]
    extra = f * (2.0 * sent[cap : 2 * cap, :] + pick(own[...].astype(BF16), f))
    x = gain[0:1, 0:1] * fold(lanes_sum(extra))
    out = row[0:1, :] + jnp.where(iota((1, 128), 1) // 16 == 5, x, 0.0)
    rows[...] = jnp.broadcast_to(out, rows.shape)


def join(gain, sent_back, got, sent, far, part, near, l_b, it_sb, w_out):
    cap = far.shape[0]
    f = got[0:cap, :]
    y = part[...] + pick(l_b[...], f)
    y_far = got[cap : 2 * cap, :] + pick(far[...].astype(BF16), sent[0:cap, :])
    w = near[...] + gain[0:1, 0:1] * pick(it_sb[...], jnp.concatenate([y, y_far], axis=0))
    w_out[...] = w
    return w


def join_first(gain, sent_back, got, sent, part, near, l_b, it_sb, out_b, w_out, base, far):
    cap = far.shape[0]
    far[...] = got[2 * cap :, 0:cap]
    w = join(gain, sent_back, got, sent, far, part, near, l_b, it_sb, w_out)
    base[...] = pick(out_b[...], w)


def join_next(gain, sent_back, got, sent, far, part, near, l_b, it_sb, out_b, w_out, base):
    w = join(gain, sent_back, got, sent, far, part, near, l_b, it_sb, w_out)
    base[...] = pick(out_b[...], w)


def two_sum(a, b):
    s = a + b
    t = s - a
    return s, (a - (s - t)) + (b - t)


def split(a):
    t = 4097.0 * a
    hi = t - (t - a)
    return hi, a - hi


def two_prod(a, b):
    p = a * b
    ah, al = split(a)
    bh, bl = split(b)
    return p, ((ah * bh - p) + ah * bl + al * bh) + al * bl


def pair_add(x, y):
    s, e = two_sum(x[0], y[0])
    return two_sum(s, e + (x[1] + y[1]))


def finish_kernel(rows, gain, prior, r0, r1, r2, w, got, s_at, flows, residual):
    n = rows.shape[0]
    tot = (rows[0:8, :], jnp.zeros((8, 128), F32))
    for i in range(8, n, 8):
        s, e = two_sum(tot[0], rows[i : i + 8, :])
        tot = (s, tot[1] + e)
    for sh in (4, 2, 1):
        tot = pair_add(tot, tuple(pltpu.roll(t, sh, 0) for t in tot))
    for sh in (8, 4, 2, 1):
        tot = pair_add(tot, tuple(pltpu.roll(t, 128 - sh, 1) for t in tot))
    hi, lo = tot
    s0 = pltpu.roll(hi, 112, 1) / hi
    s = jnp.broadcast_to(s0[:, 0:1], (8, 128))
    mu = [hi]
    for _ in range(5):
        ph, pe = two_prod(hi, s)
        pe = pe + lo * s
        nh, nl = pltpu.roll(hi, 112, 1), pltpu.roll(lo, 112, 1)
        a, e = two_sum(nh, -ph)
        hi, lo = two_sum(a, e + (nl - pe))
        mu.append(hi)
    nu = [mu[k + 1] + s * mu[k] for k in range(5)]

    def form(u, v, m):
        total = None
        for i, a in enumerate(u):
            for j, b in enumerate(v):
                term = a * b * m[i + j]
                total = term if total is None else total + term
        return total

    def image(d):
        out = [s * x for x in d] + [jnp.zeros_like(s)]
        return [out[k] + (d[k - 1] if k else 0.0) for k in range(len(out))]

    a0 = mu[0] / nu[0]
    res1 = [mu[1] / nu[0], -a0]
    rr1 = form(res1, res1, mu)
    b0 = rr1 / mu[0]
    d1 = [res1[0] + b0, res1[1]]
    a1 = rr1 / form(d1, d1, nu)
    im1 = image(d1)
    res2 = [res1[0] - a1 * im1[0], res1[1] - a1 * im1[1], -a1 * im1[2]]
    rr2 = form(res2, res2, mu)
    b1 = rr2 / rr1
    d2 = [res2[0] + b1 * d1[0], res2[1] + b1 * d1[1], res2[2]]
    a2 = rr2 / form(d2, d2, nu)
    im2 = image(d2)
    f = [a0 + a1 * d1[0] + a2 * d2[0], a1 * d1[1] + a2 * d2[1], a2 * d2[2]]
    e = [res2[0] - a2 * im2[0], res2[1] - a2 * im2[1], res2[2] - a2 * im2[2], -a2 * im2[3]]
    ss = s * s
    f = [f[0] - s * f[1] + ss * f[2], f[1] - 2.0 * s * f[2], f[2]]
    e = [
        ((e[0] - s * e[1]) + ss * e[2]) - ss * s * e[3],
        (e[1] - 2.0 * s * e[2]) + 3.0 * ss * e[3],
        e[2] - 3.0 * s * e[3],
        e[3],
    ]
    g = gain[0:1, 0:1]
    f = [x[0:1, 0:1] * (g * (1.0 / PENALTY)) for x in f]
    e = [x[0:1, 0:1] for x in e]
    cap = s_at.shape[1]
    x0, x1, x2 = r0[...], r1[...], r2[...]
    x3 = w[...] + g * pick(s_at[...], got[0:cap, :])
    flows[...] = prior[...] + ((f[0] * x0 + f[1] * x1) + f[2] * x2)
    residual[...] = ((e[0] * x0 + e[1] * x1) + e[2] * x2) + e[3] * x3


def call(kernel, outs, *args, smem=0, final=False):
    specs = [pl.BlockSpec(memory_space=pltpu.SMEM)] * smem
    specs += [pl.BlockSpec(memory_space=pltpu.VMEM)] * (len(args) - smem)
    args = args[:smem] + tuple(pltpu.with_memory_space_constraint(x, pltpu.VMEM) for x in args[smem:])
    shape = jax.ShapeDtypeStruct if final else pltpu.VMEM
    return pl.pallas_call(
        kernel,
        out_shape=tuple(shape(s, d) for s, d in outs),
        in_specs=specs,
        out_specs=tuple(pl.BlockSpec(memory_space=pltpu.VMEM) for _ in outs),
        compiler_params=pltpu.CompilerParams(vmem_limit_bytes=16 * 2**20),
    )(*args)


def bring(odd, args, msg):
    return pl.pallas_call(
        open_kernel,
        out_shape=tuple(pltpu.VMEM(x.shape, x.dtype) for x in args) + (pltpu.VMEM(*msg),),
        in_specs=[pl.BlockSpec(memory_space=pltpu.SMEM)] + [pl.BlockSpec(memory_space=pltpu.HBM)] * len(args),
        out_specs=tuple(pl.BlockSpec(memory_space=pltpu.VMEM) for _ in range(len(args) + 1)),
        scratch_shapes=[pltpu.SemaphoreType.DMA((len(args),))],
        compiler_params=pltpu.CompilerParams(vmem_limit_bytes=16 * 2**20),
    )(odd, *(pltpu.with_memory_space_constraint(x, pltpu.HBM) for x in args))


def shards(
    measured,
    prior_flow,
    demand,
    pipe_sigma,
    whiten_coef,
    pipe_tail,
    pipe_head,
    boundary_pipe,
    boundary_count,
    arrival_junction,
):
    pipes, hours = prior_flow.shape
    juncs = demand.shape[0]
    cap = boundary_pipe.shape[2]
    nets = lax.axis_size("net")
    hour_blocks = lax.axis_size("hour")
    devices = nets * hour_blocks
    field = ((pipes, hours), F32)
    heads = ((juncs, hours), F32)
    slots = ((cap, hours), F32)
    msg2 = ((2 * cap, hours), F32)
    msg3 = ((3 * cap, hours), F32)
    tile = ((8, 128), F32)
    half = ((hours // 2, hours // 2), BF16)
    on_chip = [(i, i ^ 1) for i in range(nets)]
    across = []
    for h in range(hour_blocks):
        for i in range(1, nets - 1, 2):
            a, b = i * hour_blocks + h, (i + 1) * hour_blocks + h
            across += [(a, b), (b, a)]
        for i in (0, nets - 1):
            across.append((i * hour_blocks + h, i * hour_blocks + (h ^ 1)))

    def swap(x):
        return lax.ppermute(x, "net", on_chip)

    def cross(x):
        return lax.ppermute(x, ("net", "hour"), across)

    odd = (lax.axis_index("net") % 2).astype(jnp.int32).reshape(1, 1)
    args = (
        prior_flow, boundary_pipe, boundary_count, arrival_junction,
        pipe_head.reshape(1, pipes), pipe_tail.reshape(1, pipes), demand, measured, whiten_coef.reshape(1, hours),
    )
    prior, bp, bc, aj, head, tail, dem, meas, coef, back = bring(odd, args, msg2)
    sigma = pipe_sigma.reshape(1, pipes)
    got = swap(back)
    s_a, s_at, inc, l_a, l_b, it_sb, out_b, out_a, mid_b, mid_a, own, gain0, part, base = call(
        lists_kernel,
        [
            ((cap, pipes), BF16), ((pipes, cap), BF16), ((juncs, pipes), BF16), ((juncs, cap), BF16),
            ((juncs, cap), BF16), ((pipes, juncs + cap), BF16), ((2 * cap, pipes), BF16), ((2 * cap, juncs), BF16),
            ((cap, 6 * cap), BF16), ((2 * cap, 3 * cap), BF16), ((cap, cap), F32), tile, heads, msg2,
        ],
        odd, back, prior, bp, bc, aj, head, tail, dem,
        smem=1,
    )
    sent, arrived, live = call(across_first, [msg3, slots, tile], got, base, mid_b, own)
    got = cross(sent)
    out = call(
        inside_first,
        [half] * 8 + [field, field, ((pipes, 128), F32), tile, heads, msg2],
        sent, coef, sigma, meas, prior, part, arrived, l_a, s_a, out_a,
    )
    taps, (weight, near, rvar, gain, part, base) = out[:8], out[8:]
    (back,) = call(back_kernel, [msg2], gain0, got, base, mid_a)
    back_got = swap(back)
    w, base, far = call(
        join_first, [field, msg2, ((cap, cap), F32)], gain0, back, got, sent, part, near, l_b, it_sb, out_b
    )
    fields, sums = [], []
    for step in range(3):
        g = gain if step else gain0
        sent, arrived = call(across_next, [msg2, slots], g, back, back_got, live, base, mid_b)
        got = cross(sent)
        given = (g, gain, sent, w, back_got, arrived, weight, rvar, s_a, s_at, inc, l_a, out_a, *taps)
        gives = [field, heads, field, msg2]
        if step == 0:
            r, part, near, base, acc = call(inside_one, gives + [tile], *given)
        elif step == 1:
            r, part, near, base, acc = call(inside_two, gives + [((16, 128), F32)], fields[-1], *given)
        else:
            r, part, near, base, acc = call(inside_three, gives + [tile], fields[-1], *sums, *given)
        fields.append(r)
        sums.append(acc)
        if step == 2:
            (rows,) = call(close_kernel, [((devices, 128), F32)], gain, sent, got, own, acc)
            rows = lax.all_to_all(
                rows.reshape(devices, 1, 128), ("net", "hour"), 0, 0, tiled=True
            ).reshape(devices, 128)
        (back,) = call(back_kernel, [msg2], gain, got, base, mid_a)
        back_got = swap(back)
        w, base = call(join_next, [field, msg2], gain, back, got, sent, far, part, near, l_b, it_sb, out_b)
    return call(finish_kernel, [field, field], rows, gain, prior, *fields, w, back_got, s_at, final=True)


def solution(mesh):
    placed = (
        P("net", "hour"),
        P("net", "hour"),
        P("net", "hour"),
        P("net"),
        P(),
        P("net"),
        P("net"),
        P("net", None, None),
        P("net", None),
        P("net", None, None),
    )
    return jax.shard_map(
        shards,
        mesh=mesh,
        in_specs=placed,
        out_specs=(P("net", "hour"), P("net", "hour")),
        check_vma=False,
    )
```

time: 58.6 us -> 54.1 us (0.923)
  waiting for transfers between devices: 17 us -> 10.7 us
  Pallas kernels: 11.5 us -> 14.8 us
  local copies, waits for them, and re-layouts: 2.3 us -> 0.65 us
    ppermute x5, waiting for transfers between devices: 4.3 us -> 0.81 us  [swap(): return lax.ppermute(x, 'net', on_chip)]
    ppermute x4, waiting for transfers between devices: 4.83 us -> 2.45 us  [cross(): return lax.ppermute(x, ('net', 'hour'), across)]
    pallas_call x14 -> x19, Pallas kernels: 11.5 us -> 13.5 us  [call(): pl.pallas_call(kernel, out_shape=tuple((shape(s, d) for s, d in outs)), i...]
    unnamed x22 -> x2, local copies, waits for them, and re-layouts: 2.3 us -> 0.65 us
    pallas_call x0 -> x1, Pallas kernels: none -> 1.34 us  [bring(): pl.pallas_call(open_kernel, out_shape=tuple((pltpu.VMEM(x.shape, x.dtype)...]
  transfers between devices with their start and end apart: 10 -> 10, of which waited for: 10 -> 9; matrix products, arithmetic and copies ran while one was open for 0% -> 0% of each run, Pallas kernels for 6% -> 18%
where the time goes in v4:
time: 54.1 us; the launch traced here: 53.9 us
  starting transfers between devices  27.1 us (50%)
  Pallas kernels  14.8 us (27%)
  waiting for transfers between devices  10.7 us (20%)
  between operations  0.68 us (1%)
  local copies, waits for them, and re-layouts  0.65 us (1%)
    all_to_all x1, starting transfers between devices, shards(): lax.all_to_all(rows.reshape(devices, 1, 128), ('net', 'hour'), 0, 0, tile...  16.6 us
    pallas_call x19, Pallas kernels, call(): pl.pallas_call(kernel, out_shape=tuple((shape(s, d) for s, d in outs)), i...  13.5 us
    all_to_all x1, waiting for transfers between devices, shards(): lax.all_to_all(rows.reshape(devices, 1, 128), ('net', 'hour'), 0, 0, tile...  7.39 us
    ppermute x4, starting transfers between devices, cross(): return lax.ppermute(x, ('net', 'hour'), across)  6.3 us
    ppermute x5, starting transfers between devices, swap(): return lax.ppermute(x, 'net', on_chip)  4.18 us
    ppermute x4, waiting for transfers between devices, cross(): return lax.ppermute(x, ('net', 'hour'), across)  2.45 us
    pallas_call x1, Pallas kernels, bring(): pl.pallas_call(open_kernel, out_shape=tuple((pltpu.VMEM(x.shape, x.dtype)...  1.34 us
  transfers between devices with their start and end apart: 10, of which 9 were waited for; matrix products, arithmetic and copies ran while one was open for 0% of the time, Pallas kernels for 18%

profile of v4, /device:TPU:1, one launch (start us, length us, event | category | flops | bytes accessed | tf_op | source)
XLA Modules:
  0.0 53.9 jit_solution(3509282828402963741)
XLA Ops:
  0.6 1.3 %shard_map.113 = (f32[128,512]{1,0:T(8,128)S(1)}, s32[1,2,8]{2,1,0:T(2,128)S(1)}, s32[1,2]{1,0:T(1,128)S(1)}, s32[1,2,8]{2,1,0:T(2,128)S(1)}, s32[1,128]{1,0:T(1...) custom-call(s32[1,1]{1,0:T(1,128)} %bitcast.par, ...), custom_call_target="tpu_custom_call" | custom-call | tf_op jit(solution)/shard_map/pallas_call | solution.py:425
  2.0 1.5 %collective-permute-start = (f32[16,512]{1,0:T(8,128)S(1)}, f32[16,512]{1,0:T(8,128)S(1)}, u32[]{:S(2)}, u32[]{:S(2)}) collective-permute-start(f32[16,512]{1,0:T(8,128)S(1)} %get-tuple-element.72.sent), channel_id=1, source_target_pairs={{0,4},{4,0},{8,12},{12,8},{16,20},{20,16},{24,28},{28,24},{32,36},... | collective-permute-start | bytes 98312 | tf_op jit(solution)/shard_map/ppermute | solution.py:470
  3.5 0.7 %shard_map.114 = (bf16[8,128]{1,0:T(8,128)(2,1)S(1)}, bf16[128,8]{1,0:T(8,128)(2,1)S(1)}, bf16[96,128]{1,0:T(8,128)(2,1)S(1)}, bf16[96,8]{1,0:T(8,128)(2,1)S(1)}...) custom-call(s32[1,1]{1,0:T(1,128)} %bitcast.par, ...), custom_call_target="tpu_custom_call" | custom-call | tf_op jit(solution)/shard_map/pallas_call | solution.py:415
  4.2 0.1 collective-permute-done.got
  4.3 0.1 shard_map.115
  4.4 2.0 %collective-permute-start.1 = (f32[24,512]{1,0:T(8,128)S(1)}, f32[24,512]{1,0:T(8,128)S(1)}, u32[]{:S(2)}, u32[]{:S(2)}) collective-permute-start(f32[24,512]{1,0:T(8,128)S(1)} %get-tuple-element.83.sent), channel_id=1, source_target_pairs={{4,8},{8,4},{12,16},{16,12},{20,24},{24,20},{28,32},{32,28},{36,40... | collective-permute-start | bytes 147464 | tf_op jit(solution)/shard_map/ppermute | solution.py:473
  6.4 0.0 copy-start
  6.4 0.7 %copy-done = f32[128]{0:T(128)S(1)} copy-done((f32[128]{0:T(128)S(1)}, f32[128]{0:T(128)}, u32[]{:S(2)}) %copy-start) | copy-done | bytes 536
  7.1 1.3 %shard_map.116 = (bf16[256,256]{1,0:T(8,128)(2,1)S(1)}, bf16[256,256]{1,0:T(8,128)(2,1)S(1)}, bf16[256,256]{1,0:T(8,128)(2,1)S(1)}, bf16[256,256]{1,0:T(8,128)(2...) custom-call(f32[24,512]{1,0:T(8,128)S(1)} %get-tuple-element.83.sent, ...), custom_call_target="tpu_custom_call" | custom-call | tf_op jit(solution)/shard_map/pallas_call | solution.py:415
  8.4 0.1 collective-permute-done.1.got
  8.5 0.1 shard_map.117.sent_back.sent
  8.6 0.4 collective-permute-start.2
  9.0 0.6 %shard_map.118 = (f32[128,512]{1,0:T(8,128)S(1)}, f32[16,512]{1,0:T(8,128)S(1)}, f32[8,8]{1,0:T(8,128)S(1)}) custom-call(f32[8,128]{1,0:T(8,128)S(1)} %get-tuple-element.92.gain.refs_0_, f32[16,512]{1,0:T(8,128)S(1)} %shard_map.117.sent_back.sent, f32[24,512]{1,0:T(8,128)S(1)} %collective-permute-done.1.got, f32[24,512]{1,0:T(8,128)S(1)} %get-tuple-element.83.sent, ...), custom_call_target="tpu_custom_call" | custom-call | tf_op jit(solution)/shard_map/pallas_call | solution.py:415
  9.6 0.2 collective-permute-done.2.got.refs_4_
  9.9 0.2 shard_map.119
  10.1 1.6 %collective-permute-start.3 = (f32[16,512]{1,0:T(8,128)S(1)}, f32[16,512]{1,0:T(8,128)S(1)}, u32[]{:S(2)}, u32[]{:S(2)}) collective-permute-start(f32[16,512]{1,0:T(8,128)S(1)} %get-tuple-element.102.refs_2_.sent), channel_id=1, source_target_pairs={{4,8},{8,4},{12,16},{16,12},{20,24},{24,20},{28,32},{32,28},{36,40... | collective-permute-start | bytes 98312 | tf_op jit(solution)/shard_map/ppermute | solution.py:473
  11.6 1.4 %shard_map.120 = (f32[128,512]{1,0:T(8,128)S(1)}, f32[96,512]{1,0:T(8,128)S(1)}, f32[128,512]{1,0:T(8,128)S(1)}, f32[16,512]{1,0:T(8,128)S(1)}, f32[8,128]{1,0:T(8,128)S(1)}) custom-call(f32[8,128]{1,0:T(8,128)S(1)} %get-tuple-element.92.gain.refs_0_, f32[8,128]{1,0:T(8,128)S(1)} %get-tuple-element.91.refs_1_.gain.refs_0_, ...), custom_call_target="tpu_custom_call" | custom-call | tf_op jit(solution)/shard_map/pallas_call | solution.py:415
  13.0 0.7 %collective-permute-done.3.got = f32[16,512]{1,0:T(8,128)S(1)} collective-permute-done((f32[16,512]{1,0:T(8,128)S(1)}, f32[16,512]{1,0:T(8,128)S(1)}, u32[]{:S(2)}, u32[]{:S(2)}) %collective-permute-start.3) | collective-permute-done | bytes 32800 | tf_op jit(solution)/shard_map/ppermute | solution.py:473
  13.7 0.1 shard_map.121.sent_back.sent
  13.8 0.6 %collective-permute-start.4 = (f32[16,512]{1,0:T(8,128)S(1)}, f32[16,512]{1,0:T(8,128)S(1)}, u32[]{:S(2)}, u32[]{:S(2)}) collective-permute-start(f32[16,512]{1,0:T(8,128)S(1)} %shard_map.121.sent_back.sent), channel_id=1, source_target_pairs={{0,4},{4,0},{8,12},{12,8},{16,20},{20,16},{24,28},{28,24},{32,36},... | collective-permute-start | bytes 98312 | tf_op jit(solution)/shard_map/ppermute | solution.py:470
  14.5 0.6 %shard_map.122 = (f32[128,512]{1,0:T(8,128)S(1)}, f32[16,512]{1,0:T(8,128)S(1)}) custom-call(f32[8,128]{1,0:T(8,128)S(1)} %get-tuple-element.91.refs_1_.gain.refs_0_, f32[16,512]{1,0:T(8,128)S(1)} %shard_map.121.sent_back.sent, f32[16,512]{1,0:T(8,128)S(1)} %collective-permute-done.3.got, f32[16,512]{1,0:T(8,128)S(1)} %get-tuple-element.102.refs_2_.sent, ...), custom_call_target="tpu_custom_call" | custom-call | tf_op jit(solution)/shard_map/pallas_call | solution.py:415
  15.1 0.2 collective-permute-done.4.got.refs_4_
  15.3 0.2 shard_map.123
  15.5 1.0 %collective-permute-start.5 = (f32[16,512]{1,0:T(8,128)S(1)}, f32[16,512]{1,0:T(8,128)S(1)}, u32[]{:S(2)}, u32[]{:S(2)}) collective-permute-start(f32[16,512]{1,0:T(8,128)S(1)} %get-tuple-element.122.refs_2_.sent), channel_id=1, source_target_pairs={{4,8},{8,4},{12,16},{16,12},{20,24},{24,20},{28,32},{32,28},{36,40... | collective-permute-start | bytes 98312 | tf_op jit(solution)/shard_map/ppermute | solution.py:473
  16.5 1.4 %shard_map.124 = (f32[128,512]{1,0:T(8,128)S(1)}, f32[96,512]{1,0:T(8,128)S(1)}, f32[128,512]{1,0:T(8,128)S(1)}, f32[16,512]{1,0:T(8,128)S(1)}, f32[16,128]{1,0:T(8,128)S(1)}) custom-call(f32[128,512]{1,0:T(8,128)S(1)} %get-tuple-element.123.before.r0, f32[8,128]{1,0:T(8,128)S(1)} %get-tuple-element.91.refs_1_.gain.refs_0_, ...), custom_call_target="tpu_custom_call" | custom-call | tf_op jit(solution)/shard_map/pallas_call | solution.py:415
  17.9 1.3 %collective-permute-done.5.got = f32[16,512]{1,0:T(8,128)S(1)} collective-permute-done((f32[16,512]{1,0:T(8,128)S(1)}, f32[16,512]{1,0:T(8,128)S(1)}, u32[]{:S(2)}, u32[]{:S(2)}) %collective-permute-start.5) | collective-permute-done | bytes 32800 | tf_op jit(solution)/shard_map/ppermute | solution.py:473
  19.2 0.1 shard_map.125.sent_back.sent
  19.3 0.6 %collective-permute-start.6 = (f32[16,512]{1,0:T(8,128)S(1)}, f32[16,512]{1,0:T(8,128)S(1)}, u32[]{:S(2)}, u32[]{:S(2)}) collective-permute-start(f32[16,512]{1,0:T(8,128)S(1)} %shard_map.125.sent_back.sent), channel_id=1, source_target_pairs={{0,4},{4,0},{8,12},{12,8},{16,20},{20,16},{24,28},{28,24},{32,36},... | collective-permute-start | bytes 98312 | tf_op jit(solution)/shard_map/ppermute | solution.py:470
  19.9 0.6 %shard_map.126 = (f32[128,512]{1,0:T(8,128)S(1)}, f32[16,512]{1,0:T(8,128)S(1)}) custom-call(f32[8,128]{1,0:T(8,128)S(1)} %get-tuple-element.91.refs_1_.gain.refs_0_, f32[16,512]{1,0:T(8,128)S(1)} %shard_map.125.sent_back.sent, f32[16,512]{1,0:T(8,128)S(1)} %collective-permute-done.5.got, f32[16,512]{1,0:T(8,128)S(1)} %get-tuple-element.122.refs_2_.sent, ...), custom_call_target="tpu_custom_call" | custom-call | tf_op jit(solution)/shard_map/pallas_call | solution.py:415
  20.6 0.2 collective-permute-done.6.got.refs_4_
  20.8 0.2 shard_map.127
  21.0 1.8 %collective-permute-start.7 = (f32[16,512]{1,0:T(8,128)S(1)}, f32[16,512]{1,0:T(8,128)S(1)}, u32[]{:S(2)}, u32[]{:S(2)}) collective-permute-start(f32[16,512]{1,0:T(8,128)S(1)} %get-tuple-element.130.refs_2_.sent), channel_id=1, source_target_pairs={{4,8},{8,4},{12,16},{16,12},{20,24},{24,20},{28,32},{32,28},{36,40... | collective-permute-start | bytes 98312 | tf_op jit(solution)/shard_map/ppermute | solution.py:473
  22.8 1.5 %shard_map.128 = (f32[128,512]{1,0:T(8,128)S(1)}, f32[96,512]{1,0:T(8,128)S(1)}, f32[128,512]{1,0:T(8,128)S(1)}, f32[16,512]{1,0:T(8,128)S(1)}, f32[8,128]{1,0:T(8,128)S(1)}) custom-call(f32[128,512]{1,0:T(8,128)S(1)} %get-tuple-element.131.before.r1, f32[8,128]{1,0:T(8,128)S(1)} %get-tuple-element.132.sum0, f32[16,128]{1,0:T(8,128)S(1)} %get-tuple-element.133.sum1, ...), custom_call_target="tpu_custom_call" | custom-call | tf_op jit(solution)/shard_map/pallas_call | solution.py:415
  24.3 0.4 collective-permute-done.7.got
  24.7 1.0 %shard_map.129 = f32[128,128]{1,0:T(8,128)} custom-call(f32[8,128]{1,0:T(8,128)S(1)} %get-tuple-element.91.refs_1_.gain.refs_0_, f32[16,512]{1,0:T(8,128)S(1)} %get-tuple-element.130.refs_2_.sent, f32[16,512]{1,0:T(8,128)S(1)} %collective-permute-done.7.got, f32[8,8]{1,0:T(8,128)S(1)} %get-tuple-element.82.own, f32[8,128]{1,0:T(8,128)S(1)} %get-tuple-element.136.row), custom_call_target="tpu_custom_call" | custom-call | tf_op jit(solution)/shard_map/pallas_call | solution.py:415
  25.6 16.6 %all-to-all-start = ((f32[128,1,128]{2,1,0:T(1,128)}), f32[128,1,128]{2,1,0:T(1,128)S(1)}, u32[]{:S(2)}, u32[]{:S(2)}) async-start(f32[128,1,128]{2,1,0:T(1,128)} %bitcast.6), calls=%async_computation | async-start | bytes 131072 | tf_op jit(solution)/shard_map/all_to_all | solution.py:523
  42.3 0.1 shard_map.130.sent_back
  42.4 1.1 %collective-permute-start.8 = (f32[16,512]{1,0:T(8,128)S(1)}, f32[16,512]{1,0:T(8,128)S(1)}, u32[]{:S(2)}, u32[]{:S(2)}) collective-permute-start(f32[16,512]{1,0:T(8,128)S(1)} %shard_map.130.sent_back), channel_id=1, source_target_pairs={{0,4},{4,0},{8,12},{12,8},{16,20},{20,16},{24,28},{28,24},{32,36},... | collective-permute-start | bytes 98312 | tf_op jit(solution)/shard_map/ppermute | solution.py:470
  43.5 1.2 %shard_map.131 = (f32[128,512]{1,0:T(8,128)S(1)}, f32[16,512]{1,0:T(8,128)}) custom-call(f32[8,128]{1,0:T(8,128)S(1)} %get-tuple-element.91.refs_1_.gain.refs_0_, f32[16,512]{1,0:T(8,128)S(1)} %shard_map.130.sent_back, f32[16,512]{1,0:T(8,128)S(1)} %collective-permute-done.7.got, f32[16,512]{1,0:T(8,128)S(1)} %get-tuple-element.130.refs_2_.sent, ...), custom_call_target="tpu_custom_call" | custom-call | tf_op jit(solution)/shard_map/pallas_call | solution.py:415
  44.7 0.0 collective-permute-done.8.got
  44.7 7.4 %all-to-all-done = f32[128,1,128]{2,1,0:T(1,128)S(1)} async-done(((f32[128,1,128]{2,1,0:T(1,128)}), f32[128,1,128]{2,1,0:T(1,128)S(1)}, u32[]{:S(2)}, u32[]{:S(2)}) %all-to-all-start) | async-done | bytes 65568 | tf_op jit(solution)/shard_map/all_to_all | solution.py:523
  52.1 1.8 %shard_map.132 = (f32[128,512]{1,0:T(8,128)}, f32[128,512]{1,0:T(8,128)}) custom-call(f32[128,128]{1,0:T(8,128)S(1)} %bitcast.9, f32[8,128]{1,0:T(8,128)S(1)} %get-tuple-element.91.refs_1_.gain.refs_0_, f32[128,512]{1,0:T(8,128)S(1)} %get-tuple-element.73.prior, f32[128,512]{1,0:T(8,128)S(1)} %get-tuple-element.123.before.r0, ...), custom_call_target="tpu_custom_call" | custom-call | tf_op jit(solution)/shard_map/pallas_call | solution.py:415
Async XLA Ops:
  2.0 2.3 %collective-permute-start = (f32[16,512]{1,0:T(8,128)S(1)}, f32[16,512]{1,0:T(8,128)S(1)}, u32[]{:S(2)}, u32[]{:S(2)}) collective-permute-start(f32[16,512]{1,0:T(8,128)S(1)} %get-tuple-element.72.sent), channel_id=1, source_target_pairs={{0,4},{4,0},{8,12},{12,8},{16,20},{20,16},{24,28},{28,24},{32,36},... | collective-permute-start | bytes 98312 | tf_op jit(solution)/shard_map/ppermute | solution.py:470
  4.4 4.0 %collective-permute-start.1 = (f32[24,512]{1,0:T(8,128)S(1)}, f32[24,512]{1,0:T(8,128)S(1)}, u32[]{:S(2)}, u32[]{:S(2)}) collective-permute-start(f32[24,512]{1,0:T(8,128)S(1)} %get-tuple-element.83.sent), channel_id=1, source_target_pairs={{4,8},{8,4},{12,16},{16,12},{20,24},{24,20},{28,32},{32,28},{36,40... | collective-permute-start | bytes 147464 | tf_op jit(solution)/shard_map/ppermute | solution.py:473
  6.4 0.7 %copy-start = (f32[128]{0:T(128)S(1)}, f32[128]{0:T(128)}, u32[]{:S(2)}) copy-start(f32[128]{0:T(128)} %param.13) | copy-start | bytes 1540
  8.6 1.3 %collective-permute-start.2 = (f32[16,512]{1,0:T(8,128)S(1)}, f32[16,512]{1,0:T(8,128)S(1)}, u32[]{:S(2)}, u32[]{:S(2)}) collective-permute-start(f32[16,512]{1,0:T(8,128)S(1)} %shard_map.117.sent_back.sent), channel_id=1, source_target_pairs={{0,4},{4,0},{8,12},{12,8},{16,20},{20,16},{24,28},{28,24},{32,36},... | collective-permute-start | bytes 98312 | tf_op jit(solution)/shard_map/ppermute | solution.py:470
  10.1 3.6 %collective-permute-start.3 = (f32[16,512]{1,0:T(8,128)S(1)}, f32[16,512]{1,0:T(8,128)S(1)}, u32[]{:S(2)}, u32[]{:S(2)}) collective-permute-start(f32[16,512]{1,0:T(8,128)S(1)} %get-tuple-element.102.refs_2_.sent), channel_id=1, source_target_pairs={{4,8},{8,4},{12,16},{16,12},{20,24},{24,20},{28,32},{32,28},{36,40... | collective-permute-start | bytes 98312 | tf_op jit(solution)/shard_map/ppermute | solution.py:473
  13.8 1.5 %collective-permute-start.4 = (f32[16,512]{1,0:T(8,128)S(1)}, f32[16,512]{1,0:T(8,128)S(1)}, u32[]{:S(2)}, u32[]{:S(2)}) collective-permute-start(f32[16,512]{1,0:T(8,128)S(1)} %shard_map.121.sent_back.sent), channel_id=1, source_target_pairs={{0,4},{4,0},{8,12},{12,8},{16,20},{20,16},{24,28},{28,24},{32,36},... | collective-permute-start | bytes 98312 | tf_op jit(solution)/shard_map/ppermute | solution.py:470
  15.5 3.6 %collective-permute-start.5 = (f32[16,512]{1,0:T(8,128)S(1)}, f32[16,512]{1,0:T(8,128)S(1)}, u32[]{:S(2)}, u32[]{:S(2)}) collective-permute-start(f32[16,512]{1,0:T(8,128)S(1)} %get-tuple-element.122.refs_2_.sent), channel_id=1, source_target_pairs={{4,8},{8,4},{12,16},{16,12},{20,24},{24,20},{28,32},{32,28},{36,40... | collective-permute-start | bytes 98312 | tf_op jit(solution)/shard_map/ppermute | solution.py:473
  19.3 1.5 %collective-permute-start.6 = (f32[16,512]{1,0:T(8,128)S(1)}, f32[16,512]{1,0:T(8,128)S(1)}, u32[]{:S(2)}, u32[]{:S(2)}) collective-permute-start(f32[16,512]{1,0:T(8,128)S(1)} %shard_map.125.sent_back.sent), channel_id=1, source_target_pairs={{0,4},{4,0},{8,12},{12,8},{16,20},{20,16},{24,28},{28,24},{32,36},... | collective-permute-start | bytes 98312 | tf_op jit(solution)/shard_map/ppermute | solution.py:470
  21.0 3.7 %collective-permute-start.7 = (f32[16,512]{1,0:T(8,128)S(1)}, f32[16,512]{1,0:T(8,128)S(1)}, u32[]{:S(2)}, u32[]{:S(2)}) collective-permute-start(f32[16,512]{1,0:T(8,128)S(1)} %get-tuple-element.130.refs_2_.sent), channel_id=1, source_target_pairs={{4,8},{8,4},{12,16},{16,12},{20,24},{24,20},{28,32},{32,28},{36,40... | collective-permute-start | bytes 98312 | tf_op jit(solution)/shard_map/ppermute | solution.py:473
  25.6 26.5 %all-to-all-start = ((f32[128,1,128]{2,1,0:T(1,128)}), f32[128,1,128]{2,1,0:T(1,128)S(1)}, u32[]{:S(2)}, u32[]{:S(2)}) async-start(f32[128,1,128]{2,1,0:T(1,128)} %bitcast.6), calls=%async_computation | async-start | bytes 131072 | tf_op jit(solution)/shard_map/all_to_all | solution.py:523
  42.4 2.3 %collective-permute-start.8 = (f32[16,512]{1,0:T(8,128)S(1)}, f32[16,512]{1,0:T(8,128)S(1)}, u32[]{:S(2)}, u32[]{:S(2)}) collective-permute-start(f32[16,512]{1,0:T(8,128)S(1)} %shard_map.130.sent_back), channel_id=1, source_target_pairs={{0,4},{4,0},{8,12},{12,8},{16,20},{20,16},{24,28},{28,24},{32,36},... | collective-permute-start | bytes 98312 | tf_op jit(solution)/shard_map/ppermute | solution.py:470

commit v5 on v4

--- a/solution.py
+++ b/solution.py
@@ -88,10 +88,12 @@
 
 
 def fold(tile):
-    x = jnp.sum(tile, axis=0, keepdims=True)
-    for s in (64, 32, 16):
-        x = x + pltpu.roll(x, s, 1)
-    return x
+    hi, lo = tile, jnp.zeros_like(tile)
+    for axis, shifts in ((0, (4, 2, 1)), (1, (64, 32, 16, 8, 4, 2, 1))):
+        for s in shifts:
+            hi, e = two_sum(hi, pltpu.roll(hi, s, axis))
+            lo = (lo + pltpu.roll(lo, s, axis)) + e
+    return hi[0:1, :], lo[0:1, :]
 
 
 def chosen(odd, ref, flip):
@@ -110,33 +112,40 @@
     pipe = iota((cap, pipes), 1).astype(F32)
     sel_a = jnp.where(column(chosen(odd, bp, False), cap) == pipe, live_a, 0.0)
     sel_b = jnp.where(column(chosen(odd, bp, True), cap) == pipe, live_b, 0.0)
-    return sel_a, sel_b, live_a
-
-
-def open_kernel(par, prior_in, *refs):
+    return sel_a, sel_b
+
+
+def is_odd():
+    return lax.rem(lax.axis_index("net"), 2) == 1
+
+
+def open_kernel(prior_in, *refs):
     count = 9
     ins, prior, copies = (prior_in, *refs[: count - 1]), refs[count - 1], refs[count - 1 : 2 * count - 1]
-    msg, sems = refs[2 * count - 1 :]
-    moves = [pltpu.make_async_copy(i, o, sems.at[k]) for k, (i, o) in enumerate(zip(ins, copies))]
-    bp, bc = copies[1], copies[2]
+    msg, sems, pipe_of, count_of = refs[2 * count - 1 :]
+    moves = [pltpu.make_async_copy(ins[1], pipe_of, sems.at[count]), pltpu.make_async_copy(ins[2], count_of, sems.at[count + 1])]
+    moves += [pltpu.make_async_copy(i, o, sems.at[k]) for k, (i, o) in enumerate(zip(ins, copies))]
     for m in moves:
         m.start()
     for m in moves[:3]:
         m.wait()
-    cap = bp.shape[2]
-    sel_a, _, live_a = selectors(par[0, 0] == 1, bp, bc, prior.shape[0])
-    msg[0:cap, :] = -pick(sel_a.astype(BF16), prior[...])
-    msg[cap:, :] = jnp.broadcast_to(live_a, (cap, prior.shape[1]))
+    cap = pipe_of.shape[2]
+    side = jnp.where(is_odd(), 0, 1)
+    live = count_of[0, side]
+    for k in range(cap):
+        row = prior[pl.ds(pipe_of[0, side, k], 1), :]
+        msg[k : k + 1, :] = jnp.where(k < live, -row, 0.0)
+    msg[cap:, :] = jnp.where(iota((cap, prior.shape[1]), 0) < live, 1.0, 0.0)
     for m in moves[3:]:
         m.wait()
 
 
-def lists_kernel(par, sent, prior, bp, bc, aj, head, tail, demand, s_a, s_at, inc, l_a, l_b, it_sb, out_b, out_a, mid_b, mid_a, own, gain, part, base):
+def lists_kernel(sent, prior, bp, bc, aj, head, tail, demand, s_a, s_at, inc, l_a, l_b, it_sb, out_b, out_a, mid_b, mid_a, own, gain, part, base):
     cap = bp.shape[2]
     pipes = prior.shape[0]
     juncs = inc.shape[0]
-    odd = par[0, 0] == 1
-    sel_a, sel_b, _ = selectors(odd, bp, bc, pipes)
+    odd = is_odd()
+    sel_a, sel_b = selectors(odd, bp, bc, pipes)
     inner = 1.0 - jnp.sum(sel_a + sel_b, axis=0, keepdims=True)
     junction = iota((juncs, pipes), 0)
     heads = jnp.where(junction == head[...], inner, 0.0)
@@ -199,6 +208,11 @@
     msg[cap:, :] = base[cap:, :] + mm(mid_b[...], stack3(jnp.concatenate([added, arr], axis=0)))
 
 
+def whole_kernel(gain, w, got, s_at, r_out):
+    cap = s_at.shape[1]
+    r_out[...] = w[...] + gain[0:1, 0:1] * pick(s_at[...], got[0:cap, :])
+
+
 def back_kernel(gain, got, base, mid_a, msg):
     cap = got.shape[0] // 2 if got.shape[0] == msg.shape[0] else got.shape[0] // 3
     x = mm(mid_a[...], stack3(got[0:cap, :]))
@@ -277,10 +291,11 @@
         sum0[0:8, :], sum1[0:8, :], sum1[8:16, :], lanes_sum(before[...] * r), lanes_sum(r * r),
         lanes_sum(r * n) + gain[0:1, 0:1] * lanes_sum(p * p),
     )
-    lane = iota((1, 128), 1) // 16
+    lane = iota((1, 128), 1)
     out = jnp.zeros((1, 128), F32)
     for k, tile in enumerate(tiles):
-        out = jnp.where(lane == k, fold(tile), out)
+        hi, lo = fold(tile)
+        out = jnp.where(lane == 2 * k, hi, jnp.where(lane == 2 * k + 1, lo, out))
     row[...] = jnp.broadcast_to(out, row.shape)
 
 
@@ -288,8 +303,9 @@
     cap = own.shape[0]
     f = got[0:cap, :]
     extra = f * (2.0 * sent[cap : 2 * cap, :] + pick(own[...].astype(BF16), f))
-    x = gain[0:1, 0:1] * fold(lanes_sum(extra))
-    out = row[0:1, :] + jnp.where(iota((1, 128), 1) // 16 == 5, x, 0.0)
+    x = gain[0:1, 0:1] * jnp.sum(lanes_sum(extra), axis=0, keepdims=True)
+    x = x + pltpu.roll(x, 64, 1)
+    out = jnp.where(iota((1, 128), 1) < 64, row[0:1, :], x)
     rows[...] = jnp.broadcast_to(out, rows.shape)
 
 
@@ -321,45 +337,46 @@
     return s, (a - (s - t)) + (b - t)
 
 
-def split(a):
-    t = 4097.0 * a
-    hi = t - (t - a)
-    return hi, a - hi
-
-
-def two_prod(a, b):
-    p = a * b
-    ah, al = split(a)
-    bh, bl = split(b)
-    return p, ((ah * bh - p) + ah * bl + al * bh) + al * bl
-
-
-def pair_add(x, y):
-    s, e = two_sum(x[0], y[0])
-    return two_sum(s, e + (x[1] + y[1]))
-
-
-def finish_kernel(rows, gain, prior, r0, r1, r2, w, got, s_at, flows, residual):
+def finish_kernel(rows, gain, prior, r0, r1, r2, r3, flows, residual, x_s, e_s, sems):
     n = rows.shape[0]
-    tot = (rows[0:8, :], jnp.zeros((8, 128), F32))
-    for i in range(8, n, 8):
-        s, e = two_sum(tot[0], rows[i : i + 8, :])
-        tot = (s, tot[1] + e)
+    tots = [(rows[i : i + 8, :], None) for i in range(0, n, 8)]
+    while len(tots) > 1:
+        pairs = []
+        for (a, ae), (b, be) in zip(tots[::2], tots[1::2]):
+            t, e = two_sum(a, b)
+            pairs.append((t, e if ae is None else (ae + be) + e))
+        tots = pairs
+    hi, lo = tots[0]
     for sh in (4, 2, 1):
-        tot = pair_add(tot, tuple(pltpu.roll(t, sh, 0) for t in tot))
-    for sh in (8, 4, 2, 1):
-        tot = pair_add(tot, tuple(pltpu.roll(t, 128 - sh, 1) for t in tot))
-    hi, lo = tot
-    s0 = pltpu.roll(hi, 112, 1) / hi
-    s = jnp.broadcast_to(s0[:, 0:1], (8, 128))
-    mu = [hi]
+        hi, e = two_sum(hi, pltpu.roll(hi, sh, 0))
+        lo = (lo + pltpu.roll(lo, sh, 0)) + e
+    cut, cut_e = hi, lo
+    for sh in (32, 16, 8, 4, 2, 1):
+        cut, e = two_sum(cut, pltpu.roll(cut, 128 - sh, 1))
+        cut_e = (cut_e + pltpu.roll(cut_e, 128 - sh, 1)) + e
+
+    def lane(v, k):
+        return jnp.broadcast_to(v[:, k : k + 1], (8, 128))
+
+    m = []
+    for k in range(6):
+        low = lane(lo, 2 * k) + (lane(hi, 2 * k + 1) + lane(lo, 2 * k + 1))
+        high = lane(hi, 2 * k)
+        if k == 5:
+            high, e = two_sum(high, lane(cut, 64))
+            low = (low + lane(cut_e, 64)) + e
+        m.append(two_sum(high, low))
+    s = (m[1][0] / m[0][0]).astype(BF16).astype(F32)
+    mu = [m[0][0]]
     for _ in range(5):
-        ph, pe = two_prod(hi, s)
-        pe = pe + lo * s
-        nh, nl = pltpu.roll(hi, 112, 1), pltpu.roll(lo, 112, 1)
-        a, e = two_sum(nh, -ph)
-        hi, lo = two_sum(a, e + (nl - pe))
-        mu.append(hi)
+        level = []
+        for (h0, l0), (h1, l1) in zip(m[:-1], m[1:]):
+            top = h0.astype(BF16).astype(F32)
+            a, e = two_sum(h1, -(s * top))
+            b, e2 = two_sum(a, -(s * (h0 - top)))
+            level.append((b, (e + e2) + (l1 - s * l0)))
+        m = level
+        mu.append(m[0][0] + m[0][1])
     nu = [mu[k + 1] + s * mu[k] for k in range(5)]
 
     def form(u, v, m):
@@ -397,39 +414,56 @@
         e[2] - 3.0 * s * e[3],
         e[3],
     ]
-    g = gain[0:1, 0:1]
-    f = [x[0:1, 0:1] * (g * (1.0 / PENALTY)) for x in f]
+    g = jnp.broadcast_to(gain[0:1, 0:1], (8, 128)) * (1.0 / PENALTY)
+    f = [x[0:1, 0:1] * g[0:1, 0:1] for x in f]
     e = [x[0:1, 0:1] for x in e]
-    cap = s_at.shape[1]
-    x0, x1, x2 = r0[...], r1[...], r2[...]
-    x3 = w[...] + g * pick(s_at[...], got[0:cap, :])
-    flows[...] = prior[...] + ((f[0] * x0 + f[1] * x1) + f[2] * x2)
-    residual[...] = ((e[0] * x0 + e[1] * x1) + e[2] * x2) + e[3] * x3
-
-
-def call(kernel, outs, *args, smem=0, final=False):
-    specs = [pl.BlockSpec(memory_space=pltpu.SMEM)] * smem
-    specs += [pl.BlockSpec(memory_space=pltpu.VMEM)] * (len(args) - smem)
-    args = args[:smem] + tuple(pltpu.with_memory_space_constraint(x, pltpu.VMEM) for x in args[smem:])
-    shape = jax.ShapeDtypeStruct if final else pltpu.VMEM
+    moves = []
+    step = prior.shape[0] // 4
+    for i in range(4):
+        at = slice(i * step, (i + 1) * step)
+        x0, x1, x2 = r0[at, :], r1[at, :], r2[at, :]
+        x_s[at, :] = prior[at, :] + ((f[0] * x0 + f[1] * x1) + f[2] * x2)
+        e_s[at, :] = ((e[0] * x0 + e[1] * x1) + e[2] * x2) + e[3] * r3[at, :]
+        for k, (src, dst) in enumerate(((x_s, flows), (e_s, residual))):
+            moves.append(pltpu.make_async_copy(src.at[pl.ds(i * step, step), :], dst.at[pl.ds(i * step, step), :], sems.at[2 * i + k]))
+            moves[-1].start()
+    for m in moves:
+        m.wait()
+
+
+def call(kernel, outs, *args):
     return pl.pallas_call(
         kernel,
-        out_shape=tuple(shape(s, d) for s, d in outs),
-        in_specs=specs,
+        out_shape=tuple(pltpu.VMEM(s, d) for s, d in outs),
+        in_specs=[pl.BlockSpec(memory_space=pltpu.VMEM)] * len(args),
         out_specs=tuple(pl.BlockSpec(memory_space=pltpu.VMEM) for _ in outs),
         compiler_params=pltpu.CompilerParams(vmem_limit_bytes=16 * 2**20),
-    )(*args)
-
-
-def bring(odd, args, msg):
+    )(*(pltpu.with_memory_space_constraint(x, pltpu.VMEM) for x in args))
+
+
+def bring(args, msg):
+    lists = (args[1], args[2])
     return pl.pallas_call(
         open_kernel,
         out_shape=tuple(pltpu.VMEM(x.shape, x.dtype) for x in args) + (pltpu.VMEM(*msg),),
-        in_specs=[pl.BlockSpec(memory_space=pltpu.SMEM)] + [pl.BlockSpec(memory_space=pltpu.HBM)] * len(args),
+        in_specs=[pl.BlockSpec(memory_space=pltpu.HBM)] * len(args),
         out_specs=tuple(pl.BlockSpec(memory_space=pltpu.VMEM) for _ in range(len(args) + 1)),
-        scratch_shapes=[pltpu.SemaphoreType.DMA((len(args),))],
+        scratch_shapes=[pltpu.SemaphoreType.DMA((len(args) + 2,))] + [pltpu.SMEM(x.shape, x.dtype) for x in lists],
         compiler_params=pltpu.CompilerParams(vmem_limit_bytes=16 * 2**20),
-    )(odd, *(pltpu.with_memory_space_constraint(x, pltpu.HBM) for x in args))
+    )(*(pltpu.with_memory_space_constraint(x, pltpu.HBM) for x in args))
+
+
+def finish(rows, *args):
+    field = args[1]
+    args = (rows, *args)
+    return pl.pallas_call(
+        finish_kernel,
+        out_shape=(jax.ShapeDtypeStruct(field.shape, F32),) * 2,
+        in_specs=[pl.BlockSpec(memory_space=pltpu.VMEM)] * len(args),
+        out_specs=(pl.BlockSpec(memory_space=pltpu.HBM),) * 2,
+        scratch_shapes=[pltpu.VMEM(field.shape, F32)] * 2 + [pltpu.SemaphoreType.DMA((8,))],
+        compiler_params=pltpu.CompilerParams(vmem_limit_bytes=16 * 2**20),
+    )(*(pltpu.with_memory_space_constraint(x, pltpu.VMEM) for x in args))
 
 
 def shards(
@@ -472,12 +506,11 @@
     def cross(x):
         return lax.ppermute(x, ("net", "hour"), across)
 
-    odd = (lax.axis_index("net") % 2).astype(jnp.int32).reshape(1, 1)
     args = (
         prior_flow, boundary_pipe, boundary_count, arrival_junction,
         pipe_head.reshape(1, pipes), pipe_tail.reshape(1, pipes), demand, measured, whiten_coef.reshape(1, hours),
     )
-    prior, bp, bc, aj, head, tail, dem, meas, coef, back = bring(odd, args, msg2)
+    prior, bp, bc, aj, head, tail, dem, meas, coef, back = bring(args, msg2)
     sigma = pipe_sigma.reshape(1, pipes)
     got = swap(back)
     s_a, s_at, inc, l_a, l_b, it_sb, out_b, out_a, mid_b, mid_a, own, gain0, part, base = call(
@@ -487,8 +520,7 @@
             ((juncs, cap), BF16), ((pipes, juncs + cap), BF16), ((2 * cap, pipes), BF16), ((2 * cap, juncs), BF16),
             ((cap, 6 * cap), BF16), ((2 * cap, 3 * cap), BF16), ((cap, cap), F32), tile, heads, msg2,
         ],
-        odd, back, prior, bp, bc, aj, head, tail, dem,
-        smem=1,
+        back, prior, bp, bc, aj, head, tail, dem,
     )
     sent, arrived, live = call(across_first, [msg3, slots, tile], got, base, mid_b, own)
     got = cross(sent)
@@ -526,7 +558,8 @@
         (back,) = call(back_kernel, [msg2], gain, got, base, mid_a)
         back_got = swap(back)
         w, base = call(join_next, [field, msg2], gain, back, got, sent, far, part, near, l_b, it_sb, out_b)
-    return call(finish_kernel, [field, field], rows, gain, prior, *fields, w, back_got, s_at, final=True)
+    (last,) = call(whole_kernel, [field], gain, w, back_got, s_at)
+    return finish(rows, gain, prior, *fields, last)
 
 
 def solution(mesh):

time: 54.1 us -> 53.5 us (0.989)
  waiting for transfers between devices: 10.7 us -> 10.1 us
    pallas_call x19 -> x20, Pallas kernels: 13.5 us -> 13.5 us  [the longest x19 12.1 us: call(): pl.pallas_call(kernel, out_shape=tuple((pltpu.VMEM(s, d) for s, d in outs...]
  transfers between devices with their start and end apart: 10 -> 10, of which waited for: 9 -> 9; matrix products, arithmetic and copies ran while one was open for 0% -> 0% of each run, Pallas kernels for 18% -> 19%
where the time goes in v5:
time: 53.5 us; the launch traced here: 53.4 us
  starting transfers between devices  27.1 us (51%)
  Pallas kernels  14.8 us (28%)
  waiting for transfers between devices  10.1 us (19%)
  between operations  0.68 us (1%)
  local copies, waits for them, and re-layouts  0.65 us (1%)
    all_to_all x1, starting transfers between devices, shards(): lax.all_to_all(rows.reshape(devices, 1, 128), ('net', 'hour'), 0, 0, tile...  16.6 us
    pallas_call x19, Pallas kernels, call(): pl.pallas_call(kernel, out_shape=tuple((pltpu.VMEM(s, d) for s, d in outs...  12.1 us
    all_to_all x1, waiting for transfers between devices, shards(): lax.all_to_all(rows.reshape(devices, 1, 128), ('net', 'hour'), 0, 0, tile...  7.15 us
    ppermute x4, starting transfers between devices, cross(): return lax.ppermute(x, ('net', 'hour'), across)  6.31 us
    ppermute x5, starting transfers between devices, swap(): return lax.ppermute(x, 'net', on_chip)  4.18 us
    ppermute x4, waiting for transfers between devices, cross(): return lax.ppermute(x, ('net', 'hour'), across)  2.12 us
    pallas_call x1, Pallas kernels, finish(): pl.pallas_call(finish_kernel, out_shape=(jax.ShapeDtypeStruct(field.shape...  1.43 us
    pallas_call x1, Pallas kernels, bring(): pl.pallas_call(open_kernel, out_shape=tuple((pltpu.VMEM(x.shape, x.dtype)...  1.31 us
  transfers between devices with their start and end apart: 10, of which 9 were waited for; matrix products, arithmetic and copies ran while one was open for 0% of the time, Pallas kernels for 19%

profile of v5, /device:TPU:1, one launch (start us, length us, event | category | flops | bytes accessed | tf_op | source)
XLA Modules:
  0.0 53.4 jit_solution(17419904700421860127)
XLA Ops:
  0.6 1.3 %shard_map.113 = (f32[128,512]{1,0:T(8,128)S(1)}, s32[1,2,8]{2,1,0:T(2,128)S(1)}, s32[1,2]{1,0:T(1,128)S(1)}, s32[1,2,8]{2,1,0:T(2,128)S(1)}, s32[1,128]{1,0:T(1...) custom-call(f32[128,512]{1,0:T(8,128)} %prior_in.1, ...), custom_call_target="tpu_custom_call" | custom-call | tf_op jit(solution)/shard_map/pallas_call | solution.py:446
  2.0 1.5 %collective-permute-start = (f32[16,512]{1,0:T(8,128)S(1)}, f32[16,512]{1,0:T(8,128)S(1)}, u32[]{:S(2)}, u32[]{:S(2)}) collective-permute-start(f32[16,512]{1,0:T(8,128)S(1)} %get-tuple-element.72.sent), channel_id=1, source_target_pairs={{0,4},{4,0},{8,12},{12,8},{16,20},{20,16},{24,28},{28,24},{32,36},... | collective-permute-start | bytes 98312 | tf_op jit(solution)/shard_map/ppermute | solution.py:504
  3.4 0.7 %shard_map.114 = (bf16[8,128]{1,0:T(8,128)(2,1)S(1)}, bf16[128,8]{1,0:T(8,128)(2,1)S(1)}, bf16[96,128]{1,0:T(8,128)(2,1)S(1)}, bf16[96,8]{1,0:T(8,128)(2,1)S(1)}...) custom-call(f32[16,512]{1,0:T(8,128)S(1)} %get-tuple-element.72.sent, ...), custom_call_target="tpu_custom_call" | custom-call | tf_op jit(solution)/shard_map/pallas_call | solution.py:435
  4.2 0.1 collective-permute-done.got
  4.3 0.1 shard_map.115
  4.4 2.0 %collective-permute-start.1 = (f32[24,512]{1,0:T(8,128)S(1)}, f32[24,512]{1,0:T(8,128)S(1)}, u32[]{:S(2)}, u32[]{:S(2)}) collective-permute-start(f32[24,512]{1,0:T(8,128)S(1)} %get-tuple-element.83.sent), channel_id=1, source_target_pairs={{4,8},{8,4},{12,16},{16,12},{20,24},{24,20},{28,32},{32,28},{36,40... | collective-permute-start | bytes 147464 | tf_op jit(solution)/shard_map/ppermute | solution.py:507
  6.4 0.0 copy-start
  6.4 0.7 %copy-done = f32[128]{0:T(128)S(1)} copy-done((f32[128]{0:T(128)S(1)}, f32[128]{0:T(128)}, u32[]{:S(2)}) %copy-start) | copy-done | bytes 536
  7.0 1.3 %shard_map.116 = (bf16[256,256]{1,0:T(8,128)(2,1)S(1)}, bf16[256,256]{1,0:T(8,128)(2,1)S(1)}, bf16[256,256]{1,0:T(8,128)(2,1)S(1)}, bf16[256,256]{1,0:T(8,128)(2...) custom-call(f32[24,512]{1,0:T(8,128)S(1)} %get-tuple-element.83.sent, ...), custom_call_target="tpu_custom_call" | custom-call | tf_op jit(solution)/shard_map/pallas_call | solution.py:435
  8.3 0.1 collective-permute-done.1.got
  8.4 0.1 shard_map.117.sent_back.sent
  8.6 0.4 collective-permute-start.2
  9.0 0.6 %shard_map.118 = (f32[128,512]{1,0:T(8,128)S(1)}, f32[16,512]{1,0:T(8,128)S(1)}, f32[8,8]{1,0:T(8,128)S(1)}) custom-call(f32[8,128]{1,0:T(8,128)S(1)} %get-tuple-element.92.gain.refs_0_, f32[16,512]{1,0:T(8,128)S(1)} %shard_map.117.sent_back.sent, f32[24,512]{1,0:T(8,128)S(1)} %collective-permute-done.1.got, f32[24,512]{1,0:T(8,128)S(1)} %get-tuple-element.83.sent, ...), custom_call_target="tpu_custom_call" | custom-call | tf_op jit(solution)/shard_map/pallas_call | solution.py:435
  9.6 0.2 collective-permute-done.2.got.refs_4_
  9.8 0.2 shard_map.119
  10.0 1.6 %collective-permute-start.3 = (f32[16,512]{1,0:T(8,128)S(1)}, f32[16,512]{1,0:T(8,128)S(1)}, u32[]{:S(2)}, u32[]{:S(2)}) collective-permute-start(f32[16,512]{1,0:T(8,128)S(1)} %get-tuple-element.102.refs_2_.sent), channel_id=1, source_target_pairs={{4,8},{8,4},{12,16},{16,12},{20,24},{24,20},{28,32},{32,28},{36,40... | collective-permute-start | bytes 98312 | tf_op jit(solution)/shard_map/ppermute | solution.py:507
  11.6 1.4 %shard_map.120 = (f32[128,512]{1,0:T(8,128)S(1)}, f32[96,512]{1,0:T(8,128)S(1)}, f32[128,512]{1,0:T(8,128)S(1)}, f32[16,512]{1,0:T(8,128)S(1)}, f32[8,128]{1,0:T(8,128)S(1)}) custom-call(f32[8,128]{1,0:T(8,128)S(1)} %get-tuple-element.92.gain.refs_0_, f32[8,128]{1,0:T(8,128)S(1)} %get-tuple-element.91.refs_1_.gain.refs_0_, ...), custom_call_target="tpu_custom_call" | custom-call | tf_op jit(solution)/shard_map/pallas_call | solution.py:435
  13.0 0.7 %collective-permute-done.3.got = f32[16,512]{1,0:T(8,128)S(1)} collective-permute-done((f32[16,512]{1,0:T(8,128)S(1)}, f32[16,512]{1,0:T(8,128)S(1)}, u32[]{:S(2)}, u32[]{:S(2)}) %collective-permute-start.3) | collective-permute-done | bytes 32800 | tf_op jit(solution)/shard_map/ppermute | solution.py:507
  13.7 0.1 shard_map.121.sent_back.sent
  13.8 0.6 %collective-permute-start.4 = (f32[16,512]{1,0:T(8,128)S(1)}, f32[16,512]{1,0:T(8,128)S(1)}, u32[]{:S(2)}, u32[]{:S(2)}) collective-permute-start(f32[16,512]{1,0:T(8,128)S(1)} %shard_map.121.sent_back.sent), channel_id=1, source_target_pairs={{0,4},{4,0},{8,12},{12,8},{16,20},{20,16},{24,28},{28,24},{32,36},... | collective-permute-start | bytes 98312 | tf_op jit(solution)/shard_map/ppermute | solution.py:504
  14.4 0.6 %shard_map.122 = (f32[128,512]{1,0:T(8,128)S(1)}, f32[16,512]{1,0:T(8,128)S(1)}) custom-call(f32[8,128]{1,0:T(8,128)S(1)} %get-tuple-element.91.refs_1_.gain.refs_0_, f32[16,512]{1,0:T(8,128)S(1)} %shard_map.121.sent_back.sent, f32[16,512]{1,0:T(8,128)S(1)} %collective-permute-done.3.got, f32[16,512]{1,0:T(8,128)S(1)} %get-tuple-element.102.refs_2_.sent, ...), custom_call_target="tpu_custom_call" | custom-call | tf_op jit(solution)/shard_map/pallas_call | solution.py:435
  15.1 0.2 collective-permute-done.4.got.refs_4_
  15.3 0.2 shard_map.123
  15.5 1.0 %collective-permute-start.5 = (f32[16,512]{1,0:T(8,128)S(1)}, f32[16,512]{1,0:T(8,128)S(1)}, u32[]{:S(2)}, u32[]{:S(2)}) collective-permute-start(f32[16,512]{1,0:T(8,128)S(1)} %get-tuple-element.122.refs_2_.sent), channel_id=1, source_target_pairs={{4,8},{8,4},{12,16},{16,12},{20,24},{24,20},{28,32},{32,28},{36,40... | collective-permute-start | bytes 98312 | tf_op jit(solution)/shard_map/ppermute | solution.py:507
  16.5 1.4 %shard_map.124 = (f32[128,512]{1,0:T(8,128)S(1)}, f32[96,512]{1,0:T(8,128)S(1)}, f32[128,512]{1,0:T(8,128)S(1)}, f32[16,512]{1,0:T(8,128)S(1)}, f32[16,128]{1,0:T(8,128)S(1)}) custom-call(f32[128,512]{1,0:T(8,128)S(1)} %get-tuple-element.123.before.r0, f32[8,128]{1,0:T(8,128)S(1)} %get-tuple-element.91.refs_1_.gain.refs_0_, ...), custom_call_target="tpu_custom_call" | custom-call | tf_op jit(solution)/shard_map/pallas_call | solution.py:435
  17.9 1.2 %collective-permute-done.5.got = f32[16,512]{1,0:T(8,128)S(1)} collective-permute-done((f32[16,512]{1,0:T(8,128)S(1)}, f32[16,512]{1,0:T(8,128)S(1)}, u32[]{:S(2)}, u32[]{:S(2)}) %collective-permute-start.5) | collective-permute-done | bytes 32800 | tf_op jit(solution)/shard_map/ppermute | solution.py:507
  19.1 0.1 shard_map.125.sent_back.sent
  19.3 0.6 %collective-permute-start.6 = (f32[16,512]{1,0:T(8,128)S(1)}, f32[16,512]{1,0:T(8,128)S(1)}, u32[]{:S(2)}, u32[]{:S(2)}) collective-permute-start(f32[16,512]{1,0:T(8,128)S(1)} %shard_map.125.sent_back.sent), channel_id=1, source_target_pairs={{0,4},{4,0},{8,12},{12,8},{16,20},{20,16},{24,28},{28,24},{32,36},... | collective-permute-start | bytes 98312 | tf_op jit(solution)/shard_map/ppermute | solution.py:504
  19.9 0.6 %shard_map.126 = (f32[128,512]{1,0:T(8,128)S(1)}, f32[16,512]{1,0:T(8,128)S(1)}) custom-call(f32[8,128]{1,0:T(8,128)S(1)} %get-tuple-element.91.refs_1_.gain.refs_0_, f32[16,512]{1,0:T(8,128)S(1)} %shard_map.125.sent_back.sent, f32[16,512]{1,0:T(8,128)S(1)} %collective-permute-done.5.got, f32[16,512]{1,0:T(8,128)S(1)} %get-tuple-element.122.refs_2_.sent, ...), custom_call_target="tpu_custom_call" | custom-call | tf_op jit(solution)/shard_map/pallas_call | solution.py:435
  20.5 0.2 collective-permute-done.6.got.refs_4_
  20.8 0.2 shard_map.127
  21.0 1.8 %collective-permute-start.7 = (f32[16,512]{1,0:T(8,128)S(1)}, f32[16,512]{1,0:T(8,128)S(1)}, u32[]{:S(2)}, u32[]{:S(2)}) collective-permute-start(f32[16,512]{1,0:T(8,128)S(1)} %get-tuple-element.130.refs_2_.sent), channel_id=1, source_target_pairs={{4,8},{8,4},{12,16},{16,12},{20,24},{24,20},{28,32},{32,28},{36,40... | collective-permute-start | bytes 98312 | tf_op jit(solution)/shard_map/ppermute | solution.py:507
  22.7 1.8 %shard_map.128 = (f32[128,512]{1,0:T(8,128)S(1)}, f32[96,512]{1,0:T(8,128)S(1)}, f32[128,512]{1,0:T(8,128)S(1)}, f32[16,512]{1,0:T(8,128)S(1)}, f32[8,128]{1,0:T(8,128)S(1)}) custom-call(f32[128,512]{1,0:T(8,128)S(1)} %get-tuple-element.131.before.r1, f32[8,128]{1,0:T(8,128)S(1)} %get-tuple-element.132.sum0, f32[16,128]{1,0:T(8,128)S(1)} %get-tuple-element.133.sum1, ...), custom_call_target="tpu_custom_call" | custom-call | tf_op jit(solution)/shard_map/pallas_call | solution.py:435
  24.6 0.1 collective-permute-done.7.got
  24.6 0.8 %shard_map.129 = f32[128,128]{1,0:T(8,128)} custom-call(f32[8,128]{1,0:T(8,128)S(1)} %get-tuple-element.91.refs_1_.gain.refs_0_, f32[16,512]{1,0:T(8,128)S(1)} %get-tuple-element.130.refs_2_.sent, f32[16,512]{1,0:T(8,128)S(1)} %collective-permute-done.7.got, f32[8,8]{1,0:T(8,128)S(1)} %get-tuple-element.82.own, f32[8,128]{1,0:T(8,128)S(1)} %get-tuple-element.136.row), custom_call_target="tpu_custom_call" | custom-call | tf_op jit(solution)/shard_map/pallas_call | solution.py:435
  25.5 16.6 %all-to-all-start = ((f32[128,1,128]{2,1,0:T(1,128)}), f32[128,1,128]{2,1,0:T(1,128)S(1)}, u32[]{:S(2)}, u32[]{:S(2)}) async-start(f32[128,1,128]{2,1,0:T(1,128)} %bitcast.5), calls=%async_computation | async-start | bytes 131072 | tf_op jit(solution)/shard_map/all_to_all | solution.py:555
  42.1 0.1 shard_map.130.sent_back
  42.2 1.1 %collective-permute-start.8 = (f32[16,512]{1,0:T(8,128)S(1)}, f32[16,512]{1,0:T(8,128)S(1)}, u32[]{:S(2)}, u32[]{:S(2)}) collective-permute-start(f32[16,512]{1,0:T(8,128)S(1)} %shard_map.130.sent_back), channel_id=1, source_target_pairs={{0,4},{4,0},{8,12},{12,8},{16,20},{20,16},{24,28},{28,24},{32,36},... | collective-permute-start | bytes 98312 | tf_op jit(solution)/shard_map/ppermute | solution.py:504
  43.3 1.2 %shard_map.131 = (f32[128,512]{1,0:T(8,128)S(1)}, f32[16,512]{1,0:T(8,128)}) custom-call(f32[8,128]{1,0:T(8,128)S(1)} %get-tuple-element.91.refs_1_.gain.refs_0_, f32[16,512]{1,0:T(8,128)S(1)} %shard_map.130.sent_back, f32[16,512]{1,0:T(8,128)S(1)} %collective-permute-done.7.got, f32[16,512]{1,0:T(8,128)S(1)} %get-tuple-element.130.refs_2_.sent, ...), custom_call_target="tpu_custom_call" | custom-call | tf_op jit(solution)/shard_map/pallas_call | solution.py:435
  44.5 0.0 collective-permute-done.8.got
  44.5 0.2 shard_map.132.r3
  44.8 7.2 %all-to-all-done = f32[128,1,128]{2,1,0:T(1,128)S(1)} async-done(((f32[128,1,128]{2,1,0:T(1,128)}), f32[128,1,128]{2,1,0:T(1,128)S(1)}, u32[]{:S(2)}, u32[]{:S(2)}) %all-to-all-start) | async-done | bytes 65568 | tf_op jit(solution)/shard_map/all_to_all | solution.py:555
  51.9 1.4 %shard_map.133 = (f32[128,512]{1,0:T(8,128)}, f32[128,512]{1,0:T(8,128)}) custom-call(f32[128,128]{1,0:T(8,128)S(1)} %bitcast.8, f32[8,128]{1,0:T(8,128)S(1)} %get-tuple-element.91.refs_1_.gain.refs_0_, f32[128,512]{1,0:T(8,128)S(1)} %get-tuple-element.73.prior, f32[128,512]{1,0:T(8,128)S(1)} %get-tuple-element.123.before.r0, ...), custom_call_target="tpu_custom_call" | custom-call | tf_op jit(solution)/shard_map/pallas_call | solution.py:459
Async XLA Ops:
  2.0 2.3 %collective-permute-start = (f32[16,512]{1,0:T(8,128)S(1)}, f32[16,512]{1,0:T(8,128)S(1)}, u32[]{:S(2)}, u32[]{:S(2)}) collective-permute-start(f32[16,512]{1,0:T(8,128)S(1)} %get-tuple-element.72.sent), channel_id=1, source_target_pairs={{0,4},{4,0},{8,12},{12,8},{16,20},{20,16},{24,28},{28,24},{32,36},... | collective-permute-start | bytes 98312 | tf_op jit(solution)/shard_map/ppermute | solution.py:504
  4.4 4.0 %collective-permute-start.1 = (f32[24,512]{1,0:T(8,128)S(1)}, f32[24,512]{1,0:T(8,128)S(1)}, u32[]{:S(2)}, u32[]{:S(2)}) collective-permute-start(f32[24,512]{1,0:T(8,128)S(1)} %get-tuple-element.83.sent), channel_id=1, source_target_pairs={{4,8},{8,4},{12,16},{16,12},{20,24},{24,20},{28,32},{32,28},{36,40... | collective-permute-start | bytes 147464 | tf_op jit(solution)/shard_map/ppermute | solution.py:507
  6.4 0.7 %copy-start = (f32[128]{0:T(128)S(1)}, f32[128]{0:T(128)}, u32[]{:S(2)}) copy-start(f32[128]{0:T(128)} %param.13) | copy-start | bytes 1540
  8.6 1.3 %collective-permute-start.2 = (f32[16,512]{1,0:T(8,128)S(1)}, f32[16,512]{1,0:T(8,128)S(1)}, u32[]{:S(2)}, u32[]{:S(2)}) collective-permute-start(f32[16,512]{1,0:T(8,128)S(1)} %shard_map.117.sent_back.sent), channel_id=1, source_target_pairs={{0,4},{4,0},{8,12},{12,8},{16,20},{20,16},{24,28},{28,24},{32,36},... | collective-permute-start | bytes 98312 | tf_op jit(solution)/shard_map/ppermute | solution.py:504
  10.0 3.6 %collective-permute-start.3 = (f32[16,512]{1,0:T(8,128)S(1)}, f32[16,512]{1,0:T(8,128)S(1)}, u32[]{:S(2)}, u32[]{:S(2)}) collective-permute-start(f32[16,512]{1,0:T(8,128)S(1)} %get-tuple-element.102.refs_2_.sent), channel_id=1, source_target_pairs={{4,8},{8,4},{12,16},{16,12},{20,24},{24,20},{28,32},{32,28},{36,40... | collective-permute-start | bytes 98312 | tf_op jit(solution)/shard_map/ppermute | solution.py:507
  13.8 1.5 %collective-permute-start.4 = (f32[16,512]{1,0:T(8,128)S(1)}, f32[16,512]{1,0:T(8,128)S(1)}, u32[]{:S(2)}, u32[]{:S(2)}) collective-permute-start(f32[16,512]{1,0:T(8,128)S(1)} %shard_map.121.sent_back.sent), channel_id=1, source_target_pairs={{0,4},{4,0},{8,12},{12,8},{16,20},{20,16},{24,28},{28,24},{32,36},... | collective-permute-start | bytes 98312 | tf_op jit(solution)/shard_map/ppermute | solution.py:504
  15.5 3.6 %collective-permute-start.5 = (f32[16,512]{1,0:T(8,128)S(1)}, f32[16,512]{1,0:T(8,128)S(1)}, u32[]{:S(2)}, u32[]{:S(2)}) collective-permute-start(f32[16,512]{1,0:T(8,128)S(1)} %get-tuple-element.122.refs_2_.sent), channel_id=1, source_target_pairs={{4,8},{8,4},{12,16},{16,12},{20,24},{24,20},{28,32},{32,28},{36,40... | collective-permute-start | bytes 98312 | tf_op jit(solution)/shard_map/ppermute | solution.py:507
  19.3 1.5 %collective-permute-start.6 = (f32[16,512]{1,0:T(8,128)S(1)}, f32[16,512]{1,0:T(8,128)S(1)}, u32[]{:S(2)}, u32[]{:S(2)}) collective-permute-start(f32[16,512]{1,0:T(8,128)S(1)} %shard_map.125.sent_back.sent), channel_id=1, source_target_pairs={{0,4},{4,0},{8,12},{12,8},{16,20},{20,16},{24,28},{28,24},{32,36},... | collective-permute-start | bytes 98312 | tf_op jit(solution)/shard_map/ppermute | solution.py:504
  21.0 3.7 %collective-permute-start.7 = (f32[16,512]{1,0:T(8,128)S(1)}, f32[16,512]{1,0:T(8,128)S(1)}, u32[]{:S(2)}, u32[]{:S(2)}) collective-permute-start(f32[16,512]{1,0:T(8,128)S(1)} %get-tuple-element.130.refs_2_.sent), channel_id=1, source_target_pairs={{4,8},{8,4},{12,16},{16,12},{20,24},{24,20},{28,32},{32,28},{36,40... | collective-permute-start | bytes 98312 | tf_op jit(solution)/shard_map/ppermute | solution.py:507
  25.5 26.5 %all-to-all-start = ((f32[128,1,128]{2,1,0:T(1,128)}), f32[128,1,128]{2,1,0:T(1,128)S(1)}, u32[]{:S(2)}, u32[]{:S(2)}) async-start(f32[128,1,128]{2,1,0:T(1,128)} %bitcast.5), calls=%async_computation | async-start | bytes 131072 | tf_op jit(solution)/shard_map/all_to_all | solution.py:555
  42.2 2.3 %collective-permute-start.8 = (f32[16,512]{1,0:T(8,128)S(1)}, f32[16,512]{1,0:T(8,128)S(1)}, u32[]{:S(2)}, u32[]{:S(2)}) collective-permute-start(f32[16,512]{1,0:T(8,128)S(1)} %shard_map.130.sent_back), channel_id=1, source_target_pairs={{0,4},{4,0},{8,12},{12,8},{16,20},{20,16},{24,28},{28,24},{32,36},... | collective-permute-start | bytes 98312 | tf_op jit(solution)/shard_map/ppermute | solution.py:504

commit v6 on v5

--- a/solution.py
+++ b/solution.py
@@ -120,7 +120,7 @@
 
 
 def open_kernel(prior_in, *refs):
-    count = 9
+    count = 8
     ins, prior, copies = (prior_in, *refs[: count - 1]), refs[count - 1], refs[count - 1 : 2 * count - 1]
     msg, sems, pipe_of, count_of = refs[2 * count - 1 :]
     moves = [pltpu.make_async_copy(ins[1], pipe_of, sems.at[count]), pltpu.make_async_copy(ins[2], count_of, sems.at[count + 1])]
@@ -188,21 +188,26 @@
 
 def across_first(got, base, mid_b, own, msg, arrived, live):
     cap = own.shape[0]
+    hours = base.shape[1]
     arr = got[0:cap, :]
     arrived[...] = arr
     live[...] = got[cap:, 0:128]
-    msg[0:cap, :] = base[0:cap, :]
+    msg[0:cap, 0:hours] = base[0:cap, :]
     both = jnp.concatenate([jnp.zeros_like(arr), arr], axis=0)
-    msg[cap : 2 * cap, :] = base[cap:, :] + mm(mid_b[...], stack3(both))
-    msg[2 * cap :, :] = jnp.zeros((cap, msg.shape[1]), F32)
-    msg[2 * cap :, 0:cap] = own[...]
+    msg[cap:, 0:hours] = base[cap:, :] + mm(mid_b[...], stack3(both))
+    msg[:, hours:] = jnp.zeros((2 * cap, msg.shape[1] - hours), F32)
+    msg[0:cap, hours : hours + cap] = own[...]
+
+
+def wide(tile, v):
+    return jnp.concatenate([tile] * (v.shape[1] // 128), axis=1)
 
 
 def across_next(gain, sent, got, live, base, mid_b, msg, arrived):
     cap = live.shape[0]
-    g = gain[0:1, 0:1]
-    added = g * got[0:cap, :]
-    arr = got[cap:, :] + (g * live[:, 0:1]) * sent[0:cap, :]
+    g = gain[...]
+    added = wide(g, sent) * got[0:cap, :]
+    arr = got[cap:, :] + wide(g * live[...], sent) * sent[0:cap, :]
     arrived[...] = arr
     msg[0:cap, :] = base[0:cap, :]
     msg[cap:, :] = base[cap:, :] + mm(mid_b[...], stack3(jnp.concatenate([added, arr], axis=0)))
@@ -214,10 +219,10 @@
 
 
 def back_kernel(gain, got, base, mid_a, msg):
-    cap = got.shape[0] // 2 if got.shape[0] == msg.shape[0] else got.shape[0] // 3
-    x = mm(mid_a[...], stack3(got[0:cap, :]))
+    cap, hours = msg.shape[0] // 2, msg.shape[1]
+    x = mm(mid_a[...], stack3(got[0:cap, 0:hours]))
     msg[0:cap, :] = base[0:cap, :] + x[0:cap]
-    msg[cap:, :] = base[cap:, :] + gain[0:1, 0:1] * x[cap:]
+    msg[cap:, :] = base[cap:, :] + wide(gain[...], msg) * x[cap:]
 
 
 def outward(gain, part, near, s_a, out_a, base):
@@ -310,10 +315,9 @@
 
 
 def join(gain, sent_back, got, sent, far, part, near, l_b, it_sb, w_out):
-    cap = far.shape[0]
-    f = got[0:cap, :]
-    y = part[...] + pick(l_b[...], f)
-    y_far = got[cap : 2 * cap, :] + pick(far[...].astype(BF16), sent[0:cap, :])
+    cap, hours = far.shape[0], part.shape[1]
+    y = part[...] + pick(l_b[...], got[0:cap, 0:hours])
+    y_far = got[cap:, 0:hours] + pick(far[...].astype(BF16), sent[0:cap, 0:hours])
     w = near[...] + gain[0:1, 0:1] * pick(it_sb[...], jnp.concatenate([y, y_far], axis=0))
     w_out[...] = w
     return w
@@ -321,7 +325,8 @@
 
 def join_first(gain, sent_back, got, sent, part, near, l_b, it_sb, out_b, w_out, base, far):
     cap = far.shape[0]
-    far[...] = got[2 * cap :, 0:cap]
+    hours = part.shape[1]
+    far[...] = got[0:cap, hours : hours + cap]
     w = join(gain, sent_back, got, sent, far, part, near, l_b, it_sb, w_out)
     base[...] = pick(out_b[...], w)
 
@@ -350,22 +355,16 @@
     for sh in (4, 2, 1):
         hi, e = two_sum(hi, pltpu.roll(hi, sh, 0))
         lo = (lo + pltpu.roll(lo, sh, 0)) + e
-    cut, cut_e = hi, lo
-    for sh in (32, 16, 8, 4, 2, 1):
-        cut, e = two_sum(cut, pltpu.roll(cut, 128 - sh, 1))
-        cut_e = (cut_e + pltpu.roll(cut_e, 128 - sh, 1)) + e
+    at = iota((8, 128), 1)
+    cut = jnp.sum(jnp.where(at >= 64, hi + lo, 0.0), axis=1, keepdims=True)
+    low = lo + (pltpu.roll(hi, 127, 1) + pltpu.roll(lo, 127, 1))
+    hi, e = two_sum(hi, jnp.where(at == 10, cut, 0.0))
+    hi, lo = two_sum(hi, low + e)
 
     def lane(v, k):
         return jnp.broadcast_to(v[:, k : k + 1], (8, 128))
 
-    m = []
-    for k in range(6):
-        low = lane(lo, 2 * k) + (lane(hi, 2 * k + 1) + lane(lo, 2 * k + 1))
-        high = lane(hi, 2 * k)
-        if k == 5:
-            high, e = two_sum(high, lane(cut, 64))
-            low = (low + lane(cut_e, 64)) + e
-        m.append(two_sum(high, low))
+    m = [(lane(hi, 2 * k), lane(lo, 2 * k)) for k in range(6)]
     s = (m[1][0] / m[0][0]).astype(BF16).astype(F32)
     mu = [m[0][0]]
     for _ in range(5):
@@ -488,7 +487,7 @@
     heads = ((juncs, hours), F32)
     slots = ((cap, hours), F32)
     msg2 = ((2 * cap, hours), F32)
-    msg3 = ((3 * cap, hours), F32)
+    wide = ((2 * cap, hours + 128), F32)
     tile = ((8, 128), F32)
     half = ((hours // 2, hours // 2), BF16)
     on_chip = [(i, i ^ 1) for i in range(nets)]
@@ -508,10 +507,9 @@
 
     args = (
         prior_flow, boundary_pipe, boundary_count, arrival_junction,
-        pipe_head.reshape(1, pipes), pipe_tail.reshape(1, pipes), demand, measured, whiten_coef.reshape(1, hours),
-    )
-    prior, bp, bc, aj, head, tail, dem, meas, coef, back = bring(args, msg2)
-    sigma = pipe_sigma.reshape(1, pipes)
+        pipe_head.reshape(1, pipes), pipe_tail.reshape(1, pipes), whiten_coef.reshape(1, hours), pipe_sigma.reshape(1, pipes),
+    )
+    prior, bp, bc, aj, head, tail, coef, sigma, back = bring(args, msg2)
     got = swap(back)
     s_a, s_at, inc, l_a, l_b, it_sb, out_b, out_a, mid_b, mid_a, own, gain0, part, base = call(
         lists_kernel,
@@ -520,14 +518,14 @@
             ((juncs, cap), BF16), ((pipes, juncs + cap), BF16), ((2 * cap, pipes), BF16), ((2 * cap, juncs), BF16),
             ((cap, 6 * cap), BF16), ((2 * cap, 3 * cap), BF16), ((cap, cap), F32), tile, heads, msg2,
         ],
-        back, prior, bp, bc, aj, head, tail, dem,
-    )
-    sent, arrived, live = call(across_first, [msg3, slots, tile], got, base, mid_b, own)
+        back, prior, bp, bc, aj, head, tail, demand,
+    )
+    sent, arrived, live = call(across_first, [wide, slots, tile], got, base, mid_b, own)
     got = cross(sent)
     out = call(
         inside_first,
         [half] * 8 + [field, field, ((pipes, 128), F32), tile, heads, msg2],
-        sent, coef, sigma, meas, prior, part, arrived, l_a, s_a, out_a,
+        sent, coef, sigma, measured, prior, part, arrived, l_a, s_a, out_a,
     )
     taps, (weight, near, rvar, gain, part, base) = out[:8], out[8:]
     (back,) = call(back_kernel, [msg2], gain0, got, base, mid_a)

time: 53.5 us -> 52.8 us (0.987)
  waiting for transfers between devices: 10.1 us -> 11 us
  Pallas kernels: 14.8 us -> 14.1 us
  local copies, waits for them, and re-layouts: 0.65 us -> 0.01 us
    ppermute x4, waiting for transfers between devices: 2.12 us -> 3.01 us  [cross(): return lax.ppermute(x, ('net', 'hour'), across)]
    unnamed x2 -> x4, local copies, waits for them, and re-layouts: 0.65 us -> 0.01 us
where the time goes in v6:
time: 52.8 us; the launch traced here: 52.6 us
  starting transfers between devices  26.8 us (51%)
  Pallas kernels  14.1 us (27%)
  waiting for transfers between devices  11 us (21%)
  between operations  0.69 us (1%)
    all_to_all x1, starting transfers between devices, shards(): lax.all_to_all(rows.reshape(devices, 1, 128), ('net', 'hour'), 0, 0, tile...  16.6 us
    pallas_call x19, Pallas kernels, call(): pl.pallas_call(kernel, out_shape=tuple((pltpu.VMEM(s, d) for s, d in outs...  11.9 us
    all_to_all x1, waiting for transfers between devices, shards(): lax.all_to_all(rows.reshape(devices, 1, 128), ('net', 'hour'), 0, 0, tile...  7.15 us
    ppermute x4, starting transfers between devices, cross(): return lax.ppermute(x, ('net', 'hour'), across)  6 us
    ppermute x5, starting transfers between devices, swap(): return lax.ppermute(x, 'net', on_chip)  4.19 us
    ppermute x4, waiting for transfers between devices, cross(): return lax.ppermute(x, ('net', 'hour'), across)  3.01 us
    pallas_call x1, Pallas kernels, finish(): pl.pallas_call(finish_kernel, out_shape=(jax.ShapeDtypeStruct(field.shape...  1.14 us
    pallas_call x1, Pallas kernels, bring(): pl.pallas_call(open_kernel, out_shape=tuple((pltpu.VMEM(x.shape, x.dtype)...  1.12 us
  transfers between devices with their start and end apart: 10, of which 9 were waited for; matrix products, arithmetic and copies ran while one was open for 0% of the time, Pallas kernels for 19%

profile of v6, /device:TPU:1, one launch (start us, length us, event | category | flops | bytes accessed | tf_op | source)
XLA Modules:
  0.0 52.6 jit_solution(10136040114216979979)
XLA Ops:
  0.6 0.0 copy-start.1
  0.6 1.1 %shard_map.113 = (f32[128,512]{1,0:T(8,128)S(1)}, s32[1,2,8]{2,1,0:T(2,128)S(1)}, s32[1,2]{1,0:T(1,128)S(1)}, s32[1,2,8]{2,1,0:T(2,128)S(1)}, s32[1,128]{1,0:T(1...) custom-call(f32[128,512]{1,0:T(8,128)} %prior_in.1, ...), custom_call_target="tpu_custom_call" | custom-call | tf_op jit(solution)/shard_map/pallas_call | solution.py:445
  1.8 1.5 %collective-permute-start = (f32[16,512]{1,0:T(8,128)S(1)}, f32[16,512]{1,0:T(8,128)S(1)}, u32[]{:S(2)}, u32[]{:S(2)}) collective-permute-start(f32[16,512]{1,0:T(8,128)S(1)} %get-tuple-element.71.sent), channel_id=1, source_target_pairs={{0,4},{4,0},{8,12},{12,8},{16,20},{20,16},{24,28},{28,24},{32,36},... | collective-permute-start | bytes 98312 | tf_op jit(solution)/shard_map/ppermute | solution.py:503
  3.2 0.0 copy-done.1
  3.2 0.0 copy-start
  3.2 0.7 %shard_map.114 = (bf16[8,128]{1,0:T(8,128)(2,1)S(1)}, bf16[128,8]{1,0:T(8,128)(2,1)S(1)}, bf16[96,128]{1,0:T(8,128)(2,1)S(1)}, bf16[96,8]{1,0:T(8,128)(2,1)S(1)}...) custom-call(f32[16,512]{1,0:T(8,128)S(1)} %get-tuple-element.71.sent, ...), custom_call_target="tpu_custom_call" | custom-call | tf_op jit(solution)/shard_map/pallas_call | solution.py:434
  4.0 0.1 collective-permute-done.got
  4.1 0.1 shard_map.115
  4.2 2.0 %collective-permute-start.1 = (f32[16,640]{1,0:T(8,128)S(1)}, f32[16,640]{1,0:T(8,128)S(1)}, u32[]{:S(2)}, u32[]{:S(2)}) collective-permute-start(f32[16,640]{1,0:T(8,128)S(1)} %get-tuple-element.81.sent), channel_id=1, source_target_pairs={{4,8},{8,4},{12,16},{16,12},{20,24},{24,20},{28,32},{32,28},{36,40... | collective-permute-start | bytes 122888 | tf_op jit(solution)/shard_map/ppermute | solution.py:506
  6.2 0.0 copy-done
  6.2 1.3 %shard_map.116 = (bf16[256,256]{1,0:T(8,128)(2,1)S(1)}, bf16[256,256]{1,0:T(8,128)(2,1)S(1)}, bf16[256,256]{1,0:T(8,128)(2,1)S(1)}, bf16[256,256]{1,0:T(8,128)(2...) custom-call(f32[16,640]{1,0:T(8,128)S(1)} %get-tuple-element.81.sent, ...), custom_call_target="tpu_custom_call" | custom-call | tf_op jit(solution)/shard_map/pallas_call | solution.py:434
  7.5 0.7 %collective-permute-done.1.got = f32[16,640]{1,0:T(8,128)S(1)} collective-permute-done((f32[16,640]{1,0:T(8,128)S(1)}, f32[16,640]{1,0:T(8,128)S(1)}, u32[]{:S(2)}, u32[]{:S(2)}) %collective-permute-start.1) | collective-permute-done | bytes 40992 | tf_op jit(solution)/shard_map/ppermute | solution.py:506
  8.2 0.1 shard_map.117.sent_back.sent
  8.3 0.4 collective-permute-start.2
  8.7 0.6 %shard_map.118 = (f32[128,512]{1,0:T(8,128)S(1)}, f32[16,512]{1,0:T(8,128)S(1)}, f32[8,8]{1,0:T(8,128)S(1)}) custom-call(f32[8,128]{1,0:T(8,128)S(1)} %get-tuple-element.90.gain.refs_0_, f32[16,512]{1,0:T(8,128)S(1)} %shard_map.117.sent_back.sent, f32[16,640]{1,0:T(8,128)S(1)} %collective-permute-done.1.got, f32[16,640]{1,0:T(8,128)S(1)} %get-tuple-element.81.sent, ...), custom_call_target="tpu_custom_call" | custom-call | tf_op jit(solution)/shard_map/pallas_call | solution.py:434
  9.3 0.2 collective-permute-done.2.got.refs_4_
  9.6 0.1 shard_map.119
  9.7 1.4 %collective-permute-start.3 = (f32[16,512]{1,0:T(8,128)S(1)}, f32[16,512]{1,0:T(8,128)S(1)}, u32[]{:S(2)}, u32[]{:S(2)}) collective-permute-start(f32[16,512]{1,0:T(8,128)S(1)} %get-tuple-element.100.refs_2_.sent), channel_id=1, source_target_pairs={{4,8},{8,4},{12,16},{16,12},{20,24},{24,20},{28,32},{32,28},{36,40... | collective-permute-start | bytes 98312 | tf_op jit(solution)/shard_map/ppermute | solution.py:506
  11.1 1.4 %shard_map.120 = (f32[128,512]{1,0:T(8,128)S(1)}, f32[96,512]{1,0:T(8,128)S(1)}, f32[128,512]{1,0:T(8,128)S(1)}, f32[16,512]{1,0:T(8,128)S(1)}, f32[8,128]{1,0:T(8,128)S(1)}) custom-call(f32[8,128]{1,0:T(8,128)S(1)} %get-tuple-element.90.gain.refs_0_, f32[8,128]{1,0:T(8,128)S(1)} %get-tuple-element.89.refs_1_.gain.refs_0_, ...), custom_call_target="tpu_custom_call" | custom-call | tf_op jit(solution)/shard_map/pallas_call | solution.py:434
  12.5 0.9 %collective-permute-done.3.got = f32[16,512]{1,0:T(8,128)S(1)} collective-permute-done((f32[16,512]{1,0:T(8,128)S(1)}, f32[16,512]{1,0:T(8,128)S(1)}, u32[]{:S(2)}, u32[]{:S(2)}) %collective-permute-start.3) | collective-permute-done | bytes 32800 | tf_op jit(solution)/shard_map/ppermute | solution.py:506
  13.3 0.1 shard_map.121.sent_back.sent
  13.5 0.6 %collective-permute-start.4 = (f32[16,512]{1,0:T(8,128)S(1)}, f32[16,512]{1,0:T(8,128)S(1)}, u32[]{:S(2)}, u32[]{:S(2)}) collective-permute-start(f32[16,512]{1,0:T(8,128)S(1)} %shard_map.121.sent_back.sent), channel_id=1, source_target_pairs={{0,4},{4,0},{8,12},{12,8},{16,20},{20,16},{24,28},{28,24},{32,36},... | collective-permute-start | bytes 98312 | tf_op jit(solution)/shard_map/ppermute | solution.py:503
  14.1 0.6 %shard_map.122 = (f32[128,512]{1,0:T(8,128)S(1)}, f32[16,512]{1,0:T(8,128)S(1)}) custom-call(f32[8,128]{1,0:T(8,128)S(1)} %get-tuple-element.89.refs_1_.gain.refs_0_, f32[16,512]{1,0:T(8,128)S(1)} %shard_map.121.sent_back.sent, f32[16,512]{1,0:T(8,128)S(1)} %collective-permute-done.3.got, f32[16,512]{1,0:T(8,128)S(1)} %get-tuple-element.100.refs_2_.sent, ...), custom_call_target="tpu_custom_call" | custom-call | tf_op jit(solution)/shard_map/pallas_call | solution.py:434
  14.7 0.2 collective-permute-done.4.got.refs_4_
  15.0 0.1 shard_map.123
  15.1 0.8 %collective-permute-start.5 = (f32[16,512]{1,0:T(8,128)S(1)}, f32[16,512]{1,0:T(8,128)S(1)}, u32[]{:S(2)}, u32[]{:S(2)}) collective-permute-start(f32[16,512]{1,0:T(8,128)S(1)} %get-tuple-element.120.refs_2_.sent), channel_id=1, source_target_pairs={{4,8},{8,4},{12,16},{16,12},{20,24},{24,20},{28,32},{32,28},{36,40... | collective-permute-start | bytes 98312 | tf_op jit(solution)/shard_map/ppermute | solution.py:506
  15.9 1.4 %shard_map.124 = (f32[128,512]{1,0:T(8,128)S(1)}, f32[96,512]{1,0:T(8,128)S(1)}, f32[128,512]{1,0:T(8,128)S(1)}, f32[16,512]{1,0:T(8,128)S(1)}, f32[16,128]{1,0:T(8,128)S(1)}) custom-call(f32[128,512]{1,0:T(8,128)S(1)} %get-tuple-element.121.before.r0, f32[8,128]{1,0:T(8,128)S(1)} %get-tuple-element.89.refs_1_.gain.refs_0_, ...), custom_call_target="tpu_custom_call" | custom-call | tf_op jit(solution)/shard_map/pallas_call | solution.py:434
  17.3 1.4 %collective-permute-done.5.got = f32[16,512]{1,0:T(8,128)S(1)} collective-permute-done((f32[16,512]{1,0:T(8,128)S(1)}, f32[16,512]{1,0:T(8,128)S(1)}, u32[]{:S(2)}, u32[]{:S(2)}) %collective-permute-start.5) | collective-permute-done | bytes 32800 | tf_op jit(solution)/shard_map/ppermute | solution.py:506
  18.7 0.1 shard_map.125.sent_back.sent
  18.9 0.6 %collective-permute-start.6 = (f32[16,512]{1,0:T(8,128)S(1)}, f32[16,512]{1,0:T(8,128)S(1)}, u32[]{:S(2)}, u32[]{:S(2)}) collective-permute-start(f32[16,512]{1,0:T(8,128)S(1)} %shard_map.125.sent_back.sent), channel_id=1, source_target_pairs={{0,4},{4,0},{8,12},{12,8},{16,20},{20,16},{24,28},{28,24},{32,36},... | collective-permute-start | bytes 98312 | tf_op jit(solution)/shard_map/ppermute | solution.py:503
  19.5 0.6 %shard_map.126 = (f32[128,512]{1,0:T(8,128)S(1)}, f32[16,512]{1,0:T(8,128)S(1)}) custom-call(f32[8,128]{1,0:T(8,128)S(1)} %get-tuple-element.89.refs_1_.gain.refs_0_, f32[16,512]{1,0:T(8,128)S(1)} %shard_map.125.sent_back.sent, f32[16,512]{1,0:T(8,128)S(1)} %collective-permute-done.5.got, f32[16,512]{1,0:T(8,128)S(1)} %get-tuple-element.120.refs_2_.sent, ...), custom_call_target="tpu_custom_call" | custom-call | tf_op jit(solution)/shard_map/pallas_call | solution.py:434
  20.1 0.2 collective-permute-done.6.got.refs_4_
  20.4 0.1 shard_map.127
  20.5 1.8 %collective-permute-start.7 = (f32[16,512]{1,0:T(8,128)S(1)}, f32[16,512]{1,0:T(8,128)S(1)}, u32[]{:S(2)}, u32[]{:S(2)}) collective-permute-start(f32[16,512]{1,0:T(8,128)S(1)} %get-tuple-element.128.refs_2_.sent), channel_id=1, source_target_pairs={{4,8},{8,4},{12,16},{16,12},{20,24},{24,20},{28,32},{32,28},{36,40... | collective-permute-start | bytes 98312 | tf_op jit(solution)/shard_map/ppermute | solution.py:506
  22.3 1.8 %shard_map.128 = (f32[128,512]{1,0:T(8,128)S(1)}, f32[96,512]{1,0:T(8,128)S(1)}, f32[128,512]{1,0:T(8,128)S(1)}, f32[16,512]{1,0:T(8,128)S(1)}, f32[8,128]{1,0:T(8,128)S(1)}) custom-call(f32[128,512]{1,0:T(8,128)S(1)} %get-tuple-element.129.before.r1, f32[8,128]{1,0:T(8,128)S(1)} %get-tuple-element.130.sum0, f32[16,128]{1,0:T(8,128)S(1)} %get-tuple-element.131.sum1, ...), custom_call_target="tpu_custom_call" | custom-call | tf_op jit(solution)/shard_map/pallas_call | solution.py:434
  24.1 0.1 collective-permute-done.7.got
  24.2 0.8 %shard_map.129 = f32[128,128]{1,0:T(8,128)} custom-call(f32[8,128]{1,0:T(8,128)S(1)} %get-tuple-element.89.refs_1_.gain.refs_0_, f32[16,512]{1,0:T(8,128)S(1)} %get-tuple-element.128.refs_2_.sent, f32[16,512]{1,0:T(8,128)S(1)} %collective-permute-done.7.got, f32[8,8]{1,0:T(8,128)S(1)} %get-tuple-element.80.own, f32[8,128]{1,0:T(8,128)S(1)} %get-tuple-element.134.row), custom_call_target="tpu_custom_call" | custom-call | tf_op jit(solution)/shard_map/pallas_call | solution.py:434
  25.0 16.6 %all-to-all-start = ((f32[128,1,128]{2,1,0:T(1,128)}), f32[128,1,128]{2,1,0:T(1,128)S(1)}, u32[]{:S(2)}, u32[]{:S(2)}) async-start(f32[128,1,128]{2,1,0:T(1,128)} %bitcast.5), calls=%async_computation | async-start | bytes 131072 | tf_op jit(solution)/shard_map/all_to_all | solution.py:553
  41.6 0.1 shard_map.130.sent_back
  41.7 1.1 %collective-permute-start.8 = (f32[16,512]{1,0:T(8,128)S(1)}, f32[16,512]{1,0:T(8,128)S(1)}, u32[]{:S(2)}, u32[]{:S(2)}) collective-permute-start(f32[16,512]{1,0:T(8,128)S(1)} %shard_map.130.sent_back), channel_id=1, source_target_pairs={{0,4},{4,0},{8,12},{12,8},{16,20},{20,16},{24,28},{28,24},{32,36},... | collective-permute-start | bytes 98312 | tf_op jit(solution)/shard_map/ppermute | solution.py:503
  42.8 1.2 %shard_map.131 = (f32[128,512]{1,0:T(8,128)S(1)}, f32[16,512]{1,0:T(8,128)}) custom-call(f32[8,128]{1,0:T(8,128)S(1)} %get-tuple-element.89.refs_1_.gain.refs_0_, f32[16,512]{1,0:T(8,128)S(1)} %shard_map.130.sent_back, f32[16,512]{1,0:T(8,128)S(1)} %collective-permute-done.7.got, f32[16,512]{1,0:T(8,128)S(1)} %get-tuple-element.128.refs_2_.sent, ...), custom_call_target="tpu_custom_call" | custom-call | tf_op jit(solution)/shard_map/pallas_call | solution.py:434
  44.1 0.0 collective-permute-done.8.got
  44.1 0.2 shard_map.132.r3
  44.3 7.2 %all-to-all-done = f32[128,1,128]{2,1,0:T(1,128)S(1)} async-done(((f32[128,1,128]{2,1,0:T(1,128)}), f32[128,1,128]{2,1,0:T(1,128)S(1)}, u32[]{:S(2)}, u32[]{:S(2)}) %all-to-all-start) | async-done | bytes 65568 | tf_op jit(solution)/shard_map/all_to_all | solution.py:553
  51.5 1.1 %shard_map.133 = (f32[128,512]{1,0:T(8,128)}, f32[128,512]{1,0:T(8,128)}) custom-call(f32[128,128]{1,0:T(8,128)S(1)} %bitcast.8, f32[8,128]{1,0:T(8,128)S(1)} %get-tuple-element.89.refs_1_.gain.refs_0_, f32[128,512]{1,0:T(8,128)S(1)} %get-tuple-element.72.prior, f32[128,512]{1,0:T(8,128)S(1)} %get-tuple-element.121.before.r0, ...), custom_call_target="tpu_custom_call" | custom-call | tf_op jit(solution)/shard_map/pallas_call | solution.py:458
Async XLA Ops:
  0.6 2.6 %copy-start.1 = (f32[96,512]{1,0:T(8,128)S(1)}, f32[96,512]{1,0:T(8,128)}, u32[]{:S(2)}) copy-start(f32[96,512]{1,0:T(8,128)} %demand.1) | copy-start | bytes 589828
  1.8 2.3 %collective-permute-start = (f32[16,512]{1,0:T(8,128)S(1)}, f32[16,512]{1,0:T(8,128)S(1)}, u32[]{:S(2)}, u32[]{:S(2)}) collective-permute-start(f32[16,512]{1,0:T(8,128)S(1)} %get-tuple-element.71.sent), channel_id=1, source_target_pairs={{0,4},{4,0},{8,12},{12,8},{16,20},{20,16},{24,28},{28,24},{32,36},... | collective-permute-start | bytes 98312 | tf_op jit(solution)/shard_map/ppermute | solution.py:503
  3.2 3.0 %copy-start = (f32[128,512]{1,0:T(8,128)S(1)}, f32[128,512]{1,0:T(8,128)}, u32[]{:S(2)}) copy-start(f32[128,512]{1,0:T(8,128)} %measured.1) | copy-start | bytes 786436
  4.2 4.0 %collective-permute-start.1 = (f32[16,640]{1,0:T(8,128)S(1)}, f32[16,640]{1,0:T(8,128)S(1)}, u32[]{:S(2)}, u32[]{:S(2)}) collective-permute-start(f32[16,640]{1,0:T(8,128)S(1)} %get-tuple-element.81.sent), channel_id=1, source_target_pairs={{4,8},{8,4},{12,16},{16,12},{20,24},{24,20},{28,32},{32,28},{36,40... | collective-permute-start | bytes 122888 | tf_op jit(solution)/shard_map/ppermute | solution.py:506
  8.3 1.3 %collective-permute-start.2 = (f32[16,512]{1,0:T(8,128)S(1)}, f32[16,512]{1,0:T(8,128)S(1)}, u32[]{:S(2)}, u32[]{:S(2)}) collective-permute-start(f32[16,512]{1,0:T(8,128)S(1)} %shard_map.117.sent_back.sent), channel_id=1, source_target_pairs={{0,4},{4,0},{8,12},{12,8},{16,20},{20,16},{24,28},{28,24},{32,36},... | collective-permute-start | bytes 98312 | tf_op jit(solution)/shard_map/ppermute | solution.py:503
  9.7 3.6 %collective-permute-start.3 = (f32[16,512]{1,0:T(8,128)S(1)}, f32[16,512]{1,0:T(8,128)S(1)}, u32[]{:S(2)}, u32[]{:S(2)}) collective-permute-start(f32[16,512]{1,0:T(8,128)S(1)} %get-tuple-element.100.refs_2_.sent), channel_id=1, source_target_pairs={{4,8},{8,4},{12,16},{16,12},{20,24},{24,20},{28,32},{32,28},{36,40... | collective-permute-start | bytes 98312 | tf_op jit(solution)/shard_map/ppermute | solution.py:506
  13.5 1.5 %collective-permute-start.4 = (f32[16,512]{1,0:T(8,128)S(1)}, f32[16,512]{1,0:T(8,128)S(1)}, u32[]{:S(2)}, u32[]{:S(2)}) collective-permute-start(f32[16,512]{1,0:T(8,128)S(1)} %shard_map.121.sent_back.sent), channel_id=1, source_target_pairs={{0,4},{4,0},{8,12},{12,8},{16,20},{20,16},{24,28},{28,24},{32,36},... | collective-permute-start | bytes 98312 | tf_op jit(solution)/shard_map/ppermute | solution.py:503
  15.1 3.6 %collective-permute-start.5 = (f32[16,512]{1,0:T(8,128)S(1)}, f32[16,512]{1,0:T(8,128)S(1)}, u32[]{:S(2)}, u32[]{:S(2)}) collective-permute-start(f32[16,512]{1,0:T(8,128)S(1)} %get-tuple-element.120.refs_2_.sent), channel_id=1, source_target_pairs={{4,8},{8,4},{12,16},{16,12},{20,24},{24,20},{28,32},{32,28},{36,40... | collective-permute-start | bytes 98312 | tf_op jit(solution)/shard_map/ppermute | solution.py:506
  18.9 1.5 %collective-permute-start.6 = (f32[16,512]{1,0:T(8,128)S(1)}, f32[16,512]{1,0:T(8,128)S(1)}, u32[]{:S(2)}, u32[]{:S(2)}) collective-permute-start(f32[16,512]{1,0:T(8,128)S(1)} %shard_map.125.sent_back.sent), channel_id=1, source_target_pairs={{0,4},{4,0},{8,12},{12,8},{16,20},{20,16},{24,28},{28,24},{32,36},... | collective-permute-start | bytes 98312 | tf_op jit(solution)/shard_map/ppermute | solution.py:503
  20.5 3.7 %collective-permute-start.7 = (f32[16,512]{1,0:T(8,128)S(1)}, f32[16,512]{1,0:T(8,128)S(1)}, u32[]{:S(2)}, u32[]{:S(2)}) collective-permute-start(f32[16,512]{1,0:T(8,128)S(1)} %get-tuple-element.128.refs_2_.sent), channel_id=1, source_target_pairs={{4,8},{8,4},{12,16},{16,12},{20,24},{24,20},{28,32},{32,28},{36,40... | collective-permute-start | bytes 98312 | tf_op jit(solution)/shard_map/ppermute | solution.py:506
  25.0 26.5 %all-to-all-start = ((f32[128,1,128]{2,1,0:T(1,128)}), f32[128,1,128]{2,1,0:T(1,128)S(1)}, u32[]{:S(2)}, u32[]{:S(2)}) async-start(f32[128,1,128]{2,1,0:T(1,128)} %bitcast.5), calls=%async_computation | async-start | bytes 131072 | tf_op jit(solution)/shard_map/all_to_all | solution.py:553
  41.7 2.3 %collective-permute-start.8 = (f32[16,512]{1,0:T(8,128)S(1)}, f32[16,512]{1,0:T(8,128)S(1)}, u32[]{:S(2)}, u32[]{:S(2)}) collective-permute-start(f32[16,512]{1,0:T(8,128)S(1)} %shard_map.130.sent_back), channel_id=1, source_target_pairs={{0,4},{4,0},{8,12},{12,8},{16,20},{20,16},{24,28},{28,24},{32,36},... | collective-permute-start | bytes 98312 | tf_op jit(solution)/shard_map/ppermute | solution.py:503

commit v7 on v6

--- a/solution.py
+++ b/solution.py
@@ -3,8 +3,9 @@
 from jax import lax
 from jax.experimental import pallas as pl
 from jax.experimental.pallas import tpu as pltpu
-from jax.sharding import PartitionSpec as P
-
+from jax.sharding import Mesh, PartitionSpec as P
+
+NET = ("y", "z", "core")
 EDGE = 1.5
 PENALTY = 4.0
 F32 = jnp.float32
@@ -116,7 +117,7 @@
 
 
 def is_odd():
-    return lax.rem(lax.axis_index("net"), 2) == 1
+    return lax.axis_index("core") == 1
 
 
 def open_kernel(prior_in, *refs):
@@ -124,10 +125,14 @@
     ins, prior, copies = (prior_in, *refs[: count - 1]), refs[count - 1], refs[count - 1 : 2 * count - 1]
     msg, sems, pipe_of, count_of = refs[2 * count - 1 :]
     moves = [pltpu.make_async_copy(ins[1], pipe_of, sems.at[count]), pltpu.make_async_copy(ins[2], count_of, sems.at[count + 1])]
-    moves += [pltpu.make_async_copy(i, o, sems.at[k]) for k, (i, o) in enumerate(zip(ins, copies))]
+    piece = prior.shape[0] // 4
+    for k in range(4):
+        rows = pl.ds(k * piece, piece)
+        moves.append(pltpu.make_async_copy(prior_in.at[rows, :], prior.at[rows, :], sems.at[count + 2 + k]))
+    moves += [pltpu.make_async_copy(i, o, sems.at[k]) for k, (i, o) in enumerate(zip(ins, copies)) if k]
     for m in moves:
         m.start()
-    for m in moves[:3]:
+    for m in moves[:6]:
         m.wait()
     cap = pipe_of.shape[2]
     side = jnp.where(is_odd(), 0, 1)
@@ -136,7 +141,7 @@
         row = prior[pl.ds(pipe_of[0, side, k], 1), :]
         msg[k : k + 1, :] = jnp.where(k < live, -row, 0.0)
     msg[cap:, :] = jnp.where(iota((cap, prior.shape[1]), 0) < live, 1.0, 0.0)
-    for m in moves[3:]:
+    for m in moves[6:]:
         m.wait()
 
 
@@ -447,7 +452,7 @@
         out_shape=tuple(pltpu.VMEM(x.shape, x.dtype) for x in args) + (pltpu.VMEM(*msg),),
         in_specs=[pl.BlockSpec(memory_space=pltpu.HBM)] * len(args),
         out_specs=tuple(pl.BlockSpec(memory_space=pltpu.VMEM) for _ in range(len(args) + 1)),
-        scratch_shapes=[pltpu.SemaphoreType.DMA((len(args) + 2,))] + [pltpu.SMEM(x.shape, x.dtype) for x in lists],
+        scratch_shapes=[pltpu.SemaphoreType.DMA((len(args) + 6,))] + [pltpu.SMEM(x.shape, x.dtype) for x in lists],
         compiler_params=pltpu.CompilerParams(vmem_limit_bytes=16 * 2**20),
     )(*(pltpu.with_memory_space_constraint(x, pltpu.HBM) for x in args))
 
@@ -480,7 +485,7 @@
     pipes, hours = prior_flow.shape
     juncs = demand.shape[0]
     cap = boundary_pipe.shape[2]
-    nets = lax.axis_size("net")
+    nets = lax.axis_size(NET)
     hour_blocks = lax.axis_size("hour")
     devices = nets * hour_blocks
     field = ((pipes, hours), F32)
@@ -500,10 +505,10 @@
             across.append((i * hour_blocks + h, i * hour_blocks + (h ^ 1)))
 
     def swap(x):
-        return lax.ppermute(x, "net", on_chip)
+        return lax.ppermute(x, NET, on_chip)
 
     def cross(x):
-        return lax.ppermute(x, ("net", "hour"), across)
+        return lax.ppermute(x, (*NET, "hour"), across)
 
     args = (
         prior_flow, boundary_pipe, boundary_count, arrival_junction,
@@ -551,7 +556,7 @@
         if step == 2:
             (rows,) = call(close_kernel, [((devices, 128), F32)], gain, sent, got, own, acc)
             rows = lax.all_to_all(
-                rows.reshape(devices, 1, 128), ("net", "hour"), 0, 0, tiled=True
+                rows.reshape(devices, 1, 128), ("core", "z", "y", "hour"), 0, 0, tiled=True
             ).reshape(devices, 128)
         (back,) = call(back_kernel, [msg2], gain, got, base, mid_a)
         back_got = swap(back)
@@ -561,22 +566,24 @@
 
 
 def solution(mesh):
+    nets, hours = mesh.devices.shape
+    fine = Mesh(mesh.devices.reshape(nets // 8, 4, 2, hours), (*NET, "hour"))
     placed = (
-        P("net", "hour"),
-        P("net", "hour"),
-        P("net", "hour"),
-        P("net"),
+        P(NET, "hour"),
+        P(NET, "hour"),
+        P(NET, "hour"),
+        P(NET),
         P(),
-        P("net"),
-        P("net"),
-        P("net", None, None),
-        P("net", None),
-        P("net", None, None),
+        P(NET),
+        P(NET),
+        P(NET, None, None),
+        P(NET, None),
+        P(NET, None, None),
     )
     return jax.shard_map(
         shards,
-        mesh=mesh,
+        mesh=fine,
         in_specs=placed,
-        out_specs=(P("net", "hour"), P("net", "hour")),
+        out_specs=(P(NET, "hour"), P(NET, "hour")),
         check_vma=False,
     )

time: 52.8 us -> 52.4 us (level)
  no operation moved by 1% of the time
where the time goes in v7:
time: 52.4 us; the launch traced here: 52.2 us
  starting transfers between devices  26.8 us (51%)
  Pallas kernels  14.2 us (27%)
  waiting for transfers between devices  10.6 us (20%)
  between operations  0.69 us (1%)
    all_to_all x1, starting transfers between devices, shards(): lax.all_to_all(rows.reshape(devices, 1, 128), ('core', 'z', 'y', 'hour'),...  16.6 us
    pallas_call x19, Pallas kernels, call(): pl.pallas_call(kernel, out_shape=tuple((pltpu.VMEM(s, d) for s, d in outs...  11.9 us
    all_to_all x1, waiting for transfers between devices, shards(): lax.all_to_all(rows.reshape(devices, 1, 128), ('core', 'z', 'y', 'hour'),...  6.77 us
    ppermute x4, starting transfers between devices, cross(): return lax.ppermute(x, (*NET, 'hour'), across)  6 us
    ppermute x5, starting transfers between devices, swap(): return lax.ppermute(x, NET, on_chip)  4.19 us
    ppermute x4, waiting for transfers between devices, cross(): return lax.ppermute(x, (*NET, 'hour'), across)  3.01 us
    pallas_call x1, Pallas kernels, finish(): pl.pallas_call(finish_kernel, out_shape=(jax.ShapeDtypeStruct(field.shape...  1.14 us
    pallas_call x1, Pallas kernels, bring(): pl.pallas_call(open_kernel, out_shape=tuple((pltpu.VMEM(x.shape, x.dtype)...  1.14 us
  transfers between devices with their start and end apart: 10, of which 9 were waited for; matrix products, arithmetic and copies ran while one was open for 0% of the time, Pallas kernels for 19%

profile of v7, /device:TPU:1, one launch (start us, length us, event | category | flops | bytes accessed | tf_op | source)
XLA Modules:
  0.0 52.2 jit_solution(10015434297271243007)
XLA Ops:
  0.6 0.0 copy-start.1
  0.6 1.1 %shard_map.113 = (f32[128,512]{1,0:T(8,128)S(1)}, s32[1,2,8]{2,1,0:T(2,128)S(1)}, s32[1,2]{1,0:T(1,128)S(1)}, s32[1,2,8]{2,1,0:T(2,128)S(1)}, s32[1,128]{1,0:T(1...) custom-call(f32[128,512]{1,0:T(8,128)} %prior_in.1, ...), custom_call_target="tpu_custom_call" | custom-call | tf_op jit(solution)/shard_map/pallas_call | solution.py:450
  1.8 1.5 %collective-permute-start = (f32[16,512]{1,0:T(8,128)S(1)}, f32[16,512]{1,0:T(8,128)S(1)}, u32[]{:S(2)}, u32[]{:S(2)}) collective-permute-start(f32[16,512]{1,0:T(8,128)S(1)} %get-tuple-element.71.sent), channel_id=1, source_target_pairs={{0,4},{4,0},{8,12},{12,8},{16,20},{20,16},{24,28},{28,24},{32,36},... | collective-permute-start | bytes 98312 | tf_op jit(solution)/shard_map/ppermute | solution.py:508
  3.2 0.0 copy-done.1
  3.3 0.0 copy-start
  3.3 0.7 %shard_map.114 = (bf16[8,128]{1,0:T(8,128)(2,1)S(1)}, bf16[128,8]{1,0:T(8,128)(2,1)S(1)}, bf16[96,128]{1,0:T(8,128)(2,1)S(1)}, bf16[96,8]{1,0:T(8,128)(2,1)S(1)}...) custom-call(f32[16,512]{1,0:T(8,128)S(1)} %get-tuple-element.71.sent, ...), custom_call_target="tpu_custom_call" | custom-call | tf_op jit(solution)/shard_map/pallas_call | solution.py:439
  4.0 0.1 collective-permute-done.got
  4.1 0.1 shard_map.115
  4.2 2.0 %collective-permute-start.1 = (f32[16,640]{1,0:T(8,128)S(1)}, f32[16,640]{1,0:T(8,128)S(1)}, u32[]{:S(2)}, u32[]{:S(2)}) collective-permute-start(f32[16,640]{1,0:T(8,128)S(1)} %get-tuple-element.81.sent), channel_id=1, source_target_pairs={{4,8},{8,4},{12,16},{16,12},{20,24},{24,20},{28,32},{32,28},{36,40... | collective-permute-start | bytes 122888 | tf_op jit(solution)/shard_map/ppermute | solution.py:511
  6.2 0.0 copy-done
  6.2 1.3 %shard_map.116 = (bf16[256,256]{1,0:T(8,128)(2,1)S(1)}, bf16[256,256]{1,0:T(8,128)(2,1)S(1)}, bf16[256,256]{1,0:T(8,128)(2,1)S(1)}, bf16[256,256]{1,0:T(8,128)(2...) custom-call(f32[16,640]{1,0:T(8,128)S(1)} %get-tuple-element.81.sent, ...), custom_call_target="tpu_custom_call" | custom-call | tf_op jit(solution)/shard_map/pallas_call | solution.py:439
  7.5 0.7 %collective-permute-done.1.got = f32[16,640]{1,0:T(8,128)S(1)} collective-permute-done((f32[16,640]{1,0:T(8,128)S(1)}, f32[16,640]{1,0:T(8,128)S(1)}, u32[]{:S(2)}, u32[]{:S(2)}) %collective-permute-start.1) | collective-permute-done | bytes 40992 | tf_op jit(solution)/shard_map/ppermute | solution.py:511
  8.2 0.1 shard_map.117.sent_back.sent
  8.3 0.4 collective-permute-start.2
  8.7 0.6 %shard_map.118 = (f32[128,512]{1,0:T(8,128)S(1)}, f32[16,512]{1,0:T(8,128)S(1)}, f32[8,8]{1,0:T(8,128)S(1)}) custom-call(f32[8,128]{1,0:T(8,128)S(1)} %get-tuple-element.90.gain.refs_0_, f32[16,512]{1,0:T(8,128)S(1)} %shard_map.117.sent_back.sent, f32[16,640]{1,0:T(8,128)S(1)} %collective-permute-done.1.got, f32[16,640]{1,0:T(8,128)S(1)} %get-tuple-element.81.sent, ...), custom_call_target="tpu_custom_call" | custom-call | tf_op jit(solution)/shard_map/pallas_call | solution.py:439
  9.4 0.2 collective-permute-done.2.got.refs_4_
  9.6 0.1 shard_map.119
  9.7 1.4 %collective-permute-start.3 = (f32[16,512]{1,0:T(8,128)S(1)}, f32[16,512]{1,0:T(8,128)S(1)}, u32[]{:S(2)}, u32[]{:S(2)}) collective-permute-start(f32[16,512]{1,0:T(8,128)S(1)} %get-tuple-element.100.refs_2_.sent), channel_id=1, source_target_pairs={{4,8},{8,4},{12,16},{16,12},{20,24},{24,20},{28,32},{32,28},{36,40... | collective-permute-start | bytes 98312 | tf_op jit(solution)/shard_map/ppermute | solution.py:511
  11.1 1.4 %shard_map.120 = (f32[128,512]{1,0:T(8,128)S(1)}, f32[96,512]{1,0:T(8,128)S(1)}, f32[128,512]{1,0:T(8,128)S(1)}, f32[16,512]{1,0:T(8,128)S(1)}, f32[8,128]{1,0:T(8,128)S(1)}) custom-call(f32[8,128]{1,0:T(8,128)S(1)} %get-tuple-element.90.gain.refs_0_, f32[8,128]{1,0:T(8,128)S(1)} %get-tuple-element.89.refs_1_.gain.refs_0_, ...), custom_call_target="tpu_custom_call" | custom-call | tf_op jit(solution)/shard_map/pallas_call | solution.py:439
  12.5 0.9 %collective-permute-done.3.got = f32[16,512]{1,0:T(8,128)S(1)} collective-permute-done((f32[16,512]{1,0:T(8,128)S(1)}, f32[16,512]{1,0:T(8,128)S(1)}, u32[]{:S(2)}, u32[]{:S(2)}) %collective-permute-start.3) | collective-permute-done | bytes 32800 | tf_op jit(solution)/shard_map/ppermute | solution.py:511
  13.4 0.1 shard_map.121.sent_back.sent
  13.5 0.6 %collective-permute-start.4 = (f32[16,512]{1,0:T(8,128)S(1)}, f32[16,512]{1,0:T(8,128)S(1)}, u32[]{:S(2)}, u32[]{:S(2)}) collective-permute-start(f32[16,512]{1,0:T(8,128)S(1)} %shard_map.121.sent_back.sent), channel_id=1, source_target_pairs={{0,4},{4,0},{8,12},{12,8},{16,20},{20,16},{24,28},{28,24},{32,36},... | collective-permute-start | bytes 98312 | tf_op jit(solution)/shard_map/ppermute | solution.py:508
  14.1 0.6 %shard_map.122 = (f32[128,512]{1,0:T(8,128)S(1)}, f32[16,512]{1,0:T(8,128)S(1)}) custom-call(f32[8,128]{1,0:T(8,128)S(1)} %get-tuple-element.89.refs_1_.gain.refs_0_, f32[16,512]{1,0:T(8,128)S(1)} %shard_map.121.sent_back.sent, f32[16,512]{1,0:T(8,128)S(1)} %collective-permute-done.3.got, f32[16,512]{1,0:T(8,128)S(1)} %get-tuple-element.100.refs_2_.sent, ...), custom_call_target="tpu_custom_call" | custom-call | tf_op jit(solution)/shard_map/pallas_call | solution.py:439
  14.7 0.2 collective-permute-done.4.got.refs_4_
  15.0 0.1 shard_map.123
  15.1 0.8 %collective-permute-start.5 = (f32[16,512]{1,0:T(8,128)S(1)}, f32[16,512]{1,0:T(8,128)S(1)}, u32[]{:S(2)}, u32[]{:S(2)}) collective-permute-start(f32[16,512]{1,0:T(8,128)S(1)} %get-tuple-element.120.refs_2_.sent), channel_id=1, source_target_pairs={{4,8},{8,4},{12,16},{16,12},{20,24},{24,20},{28,32},{32,28},{36,40... | collective-permute-start | bytes 98312 | tf_op jit(solution)/shard_map/ppermute | solution.py:511
  15.9 1.4 %shard_map.124 = (f32[128,512]{1,0:T(8,128)S(1)}, f32[96,512]{1,0:T(8,128)S(1)}, f32[128,512]{1,0:T(8,128)S(1)}, f32[16,512]{1,0:T(8,128)S(1)}, f32[16,128]{1,0:T(8,128)S(1)}) custom-call(f32[128,512]{1,0:T(8,128)S(1)} %get-tuple-element.121.before.r0, f32[8,128]{1,0:T(8,128)S(1)} %get-tuple-element.89.refs_1_.gain.refs_0_, ...), custom_call_target="tpu_custom_call" | custom-call | tf_op jit(solution)/shard_map/pallas_call | solution.py:439
  17.3 1.4 %collective-permute-done.5.got = f32[16,512]{1,0:T(8,128)S(1)} collective-permute-done((f32[16,512]{1,0:T(8,128)S(1)}, f32[16,512]{1,0:T(8,128)S(1)}, u32[]{:S(2)}, u32[]{:S(2)}) %collective-permute-start.5) | collective-permute-done | bytes 32800 | tf_op jit(solution)/shard_map/ppermute | solution.py:511
  18.7 0.1 shard_map.125.sent_back.sent
  18.9 0.6 %collective-permute-start.6 = (f32[16,512]{1,0:T(8,128)S(1)}, f32[16,512]{1,0:T(8,128)S(1)}, u32[]{:S(2)}, u32[]{:S(2)}) collective-permute-start(f32[16,512]{1,0:T(8,128)S(1)} %shard_map.125.sent_back.sent), channel_id=1, source_target_pairs={{0,4},{4,0},{8,12},{12,8},{16,20},{20,16},{24,28},{28,24},{32,36},... | collective-permute-start | bytes 98312 | tf_op jit(solution)/shard_map/ppermute | solution.py:508
  19.5 0.6 %shard_map.126 = (f32[128,512]{1,0:T(8,128)S(1)}, f32[16,512]{1,0:T(8,128)S(1)}) custom-call(f32[8,128]{1,0:T(8,128)S(1)} %get-tuple-element.89.refs_1_.gain.refs_0_, f32[16,512]{1,0:T(8,128)S(1)} %shard_map.125.sent_back.sent, f32[16,512]{1,0:T(8,128)S(1)} %collective-permute-done.5.got, f32[16,512]{1,0:T(8,128)S(1)} %get-tuple-element.120.refs_2_.sent, ...), custom_call_target="tpu_custom_call" | custom-call | tf_op jit(solution)/shard_map/pallas_call | solution.py:439
  20.1 0.2 collective-permute-done.6.got.refs_4_
  20.4 0.1 shard_map.127
  20.5 1.8 %collective-permute-start.7 = (f32[16,512]{1,0:T(8,128)S(1)}, f32[16,512]{1,0:T(8,128)S(1)}, u32[]{:S(2)}, u32[]{:S(2)}) collective-permute-start(f32[16,512]{1,0:T(8,128)S(1)} %get-tuple-element.128.refs_2_.sent), channel_id=1, source_target_pairs={{4,8},{8,4},{12,16},{16,12},{20,24},{24,20},{28,32},{32,28},{36,40... | collective-permute-start | bytes 98312 | tf_op jit(solution)/shard_map/ppermute | solution.py:511
  22.3 1.8 %shard_map.128 = (f32[128,512]{1,0:T(8,128)S(1)}, f32[96,512]{1,0:T(8,128)S(1)}, f32[128,512]{1,0:T(8,128)S(1)}, f32[16,512]{1,0:T(8,128)S(1)}, f32[8,128]{1,0:T(8,128)S(1)}) custom-call(f32[128,512]{1,0:T(8,128)S(1)} %get-tuple-element.129.before.r1, f32[8,128]{1,0:T(8,128)S(1)} %get-tuple-element.130.sum0, f32[16,128]{1,0:T(8,128)S(1)} %get-tuple-element.131.sum1, ...), custom_call_target="tpu_custom_call" | custom-call | tf_op jit(solution)/shard_map/pallas_call | solution.py:439
  24.1 0.1 collective-permute-done.7.got
  24.2 0.8 %shard_map.129 = f32[128,128]{1,0:T(8,128)} custom-call(f32[8,128]{1,0:T(8,128)S(1)} %get-tuple-element.89.refs_1_.gain.refs_0_, f32[16,512]{1,0:T(8,128)S(1)} %get-tuple-element.128.refs_2_.sent, f32[16,512]{1,0:T(8,128)S(1)} %collective-permute-done.7.got, f32[8,8]{1,0:T(8,128)S(1)} %get-tuple-element.80.own, f32[8,128]{1,0:T(8,128)S(1)} %get-tuple-element.134.row), custom_call_target="tpu_custom_call" | custom-call | tf_op jit(solution)/shard_map/pallas_call | solution.py:439
  25.0 16.6 %all-to-all-start = ((f32[128,1,128]{2,1,0:T(1,128)}), f32[128,1,128]{2,1,0:T(1,128)S(1)}, u32[]{:S(2)}, u32[]{:S(2)}) async-start(f32[128,1,128]{2,1,0:T(1,128)} %bitcast.5), calls=%async_computation | async-start | bytes 131072 | tf_op jit(solution)/shard_map/all_to_all | solution.py:558
  41.6 0.1 shard_map.130.sent_back
  41.8 1.1 %collective-permute-start.8 = (f32[16,512]{1,0:T(8,128)S(1)}, f32[16,512]{1,0:T(8,128)S(1)}, u32[]{:S(2)}, u32[]{:S(2)}) collective-permute-start(f32[16,512]{1,0:T(8,128)S(1)} %shard_map.130.sent_back), channel_id=1, source_target_pairs={{0,4},{4,0},{8,12},{12,8},{16,20},{20,16},{24,28},{28,24},{32,36},... | collective-permute-start | bytes 98312 | tf_op jit(solution)/shard_map/ppermute | solution.py:508
  42.8 1.2 %shard_map.131 = (f32[128,512]{1,0:T(8,128)S(1)}, f32[16,512]{1,0:T(8,128)}) custom-call(f32[8,128]{1,0:T(8,128)S(1)} %get-tuple-element.89.refs_1_.gain.refs_0_, f32[16,512]{1,0:T(8,128)S(1)} %shard_map.130.sent_back, f32[16,512]{1,0:T(8,128)S(1)} %collective-permute-done.7.got, f32[16,512]{1,0:T(8,128)S(1)} %get-tuple-element.128.refs_2_.sent, ...), custom_call_target="tpu_custom_call" | custom-call | tf_op jit(solution)/shard_map/pallas_call | solution.py:439
  44.1 0.0 collective-permute-done.8.got
  44.1 0.2 shard_map.132.r3
  44.3 6.8 %all-to-all-done = f32[128,1,128]{2,1,0:T(1,128)S(1)} async-done(((f32[128,1,128]{2,1,0:T(1,128)}), f32[128,1,128]{2,1,0:T(1,128)S(1)}, u32[]{:S(2)}, u32[]{:S(2)}) %all-to-all-start) | async-done | bytes 65568 | tf_op jit(solution)/shard_map/all_to_all | solution.py:558
  51.1 1.1 %shard_map.133 = (f32[128,512]{1,0:T(8,128)}, f32[128,512]{1,0:T(8,128)}) custom-call(f32[128,128]{1,0:T(8,128)S(1)} %bitcast.8, f32[8,128]{1,0:T(8,128)S(1)} %get-tuple-element.89.refs_1_.gain.refs_0_, f32[128,512]{1,0:T(8,128)S(1)} %get-tuple-element.72.prior, f32[128,512]{1,0:T(8,128)S(1)} %get-tuple-element.121.before.r0, ...), custom_call_target="tpu_custom_call" | custom-call | tf_op jit(solution)/shard_map/pallas_call | solution.py:463
Async XLA Ops:
  0.6 2.6 %copy-start.1 = (f32[96,512]{1,0:T(8,128)S(1)}, f32[96,512]{1,0:T(8,128)}, u32[]{:S(2)}) copy-start(f32[96,512]{1,0:T(8,128)} %demand.1) | copy-start | bytes 589828
  1.8 2.3 %collective-permute-start = (f32[16,512]{1,0:T(8,128)S(1)}, f32[16,512]{1,0:T(8,128)S(1)}, u32[]{:S(2)}, u32[]{:S(2)}) collective-permute-start(f32[16,512]{1,0:T(8,128)S(1)} %get-tuple-element.71.sent), channel_id=1, source_target_pairs={{0,4},{4,0},{8,12},{12,8},{16,20},{20,16},{24,28},{28,24},{32,36},... | collective-permute-start | bytes 98312 | tf_op jit(solution)/shard_map/ppermute | solution.py:508
  3.3 3.0 %copy-start = (f32[128,512]{1,0:T(8,128)S(1)}, f32[128,512]{1,0:T(8,128)}, u32[]{:S(2)}) copy-start(f32[128,512]{1,0:T(8,128)} %measured.1) | copy-start | bytes 786436
  4.2 4.0 %collective-permute-start.1 = (f32[16,640]{1,0:T(8,128)S(1)}, f32[16,640]{1,0:T(8,128)S(1)}, u32[]{:S(2)}, u32[]{:S(2)}) collective-permute-start(f32[16,640]{1,0:T(8,128)S(1)} %get-tuple-element.81.sent), channel_id=1, source_target_pairs={{4,8},{8,4},{12,16},{16,12},{20,24},{24,20},{28,32},{32,28},{36,40... | collective-permute-start | bytes 122888 | tf_op jit(solution)/shard_map/ppermute | solution.py:511
  8.3 1.3 %collective-permute-start.2 = (f32[16,512]{1,0:T(8,128)S(1)}, f32[16,512]{1,0:T(8,128)S(1)}, u32[]{:S(2)}, u32[]{:S(2)}) collective-permute-start(f32[16,512]{1,0:T(8,128)S(1)} %shard_map.117.sent_back.sent), channel_id=1, source_target_pairs={{0,4},{4,0},{8,12},{12,8},{16,20},{20,16},{24,28},{28,24},{32,36},... | collective-permute-start | bytes 98312 | tf_op jit(solution)/shard_map/ppermute | solution.py:508
  9.7 3.6 %collective-permute-start.3 = (f32[16,512]{1,0:T(8,128)S(1)}, f32[16,512]{1,0:T(8,128)S(1)}, u32[]{:S(2)}, u32[]{:S(2)}) collective-permute-start(f32[16,512]{1,0:T(8,128)S(1)} %get-tuple-element.100.refs_2_.sent), channel_id=1, source_target_pairs={{4,8},{8,4},{12,16},{16,12},{20,24},{24,20},{28,32},{32,28},{36,40... | collective-permute-start | bytes 98312 | tf_op jit(solution)/shard_map/ppermute | solution.py:511
  13.5 1.5 %collective-permute-start.4 = (f32[16,512]{1,0:T(8,128)S(1)}, f32[16,512]{1,0:T(8,128)S(1)}, u32[]{:S(2)}, u32[]{:S(2)}) collective-permute-start(f32[16,512]{1,0:T(8,128)S(1)} %shard_map.121.sent_back.sent), channel_id=1, source_target_pairs={{0,4},{4,0},{8,12},{12,8},{16,20},{20,16},{24,28},{28,24},{32,36},... | collective-permute-start | bytes 98312 | tf_op jit(solution)/shard_map/ppermute | solution.py:508
  15.1 3.6 %collective-permute-start.5 = (f32[16,512]{1,0:T(8,128)S(1)}, f32[16,512]{1,0:T(8,128)S(1)}, u32[]{:S(2)}, u32[]{:S(2)}) collective-permute-start(f32[16,512]{1,0:T(8,128)S(1)} %get-tuple-element.120.refs_2_.sent), channel_id=1, source_target_pairs={{4,8},{8,4},{12,16},{16,12},{20,24},{24,20},{28,32},{32,28},{36,40... | collective-permute-start | bytes 98312 | tf_op jit(solution)/shard_map/ppermute | solution.py:511
  18.9 1.5 %collective-permute-start.6 = (f32[16,512]{1,0:T(8,128)S(1)}, f32[16,512]{1,0:T(8,128)S(1)}, u32[]{:S(2)}, u32[]{:S(2)}) collective-permute-start(f32[16,512]{1,0:T(8,128)S(1)} %shard_map.125.sent_back.sent), channel_id=1, source_target_pairs={{0,4},{4,0},{8,12},{12,8},{16,20},{20,16},{24,28},{28,24},{32,36},... | collective-permute-start | bytes 98312 | tf_op jit(solution)/shard_map/ppermute | solution.py:508
  20.5 3.7 %collective-permute-start.7 = (f32[16,512]{1,0:T(8,128)S(1)}, f32[16,512]{1,0:T(8,128)S(1)}, u32[]{:S(2)}, u32[]{:S(2)}) collective-permute-start(f32[16,512]{1,0:T(8,128)S(1)} %get-tuple-element.128.refs_2_.sent), channel_id=1, source_target_pairs={{4,8},{8,4},{12,16},{16,12},{20,24},{24,20},{28,32},{32,28},{36,40... | collective-permute-start | bytes 98312 | tf_op jit(solution)/shard_map/ppermute | solution.py:511
  25.0 26.1 %all-to-all-start = ((f32[128,1,128]{2,1,0:T(1,128)}), f32[128,1,128]{2,1,0:T(1,128)S(1)}, u32[]{:S(2)}, u32[]{:S(2)}) async-start(f32[128,1,128]{2,1,0:T(1,128)} %bitcast.5), calls=%async_computation | async-start | bytes 131072 | tf_op jit(solution)/shard_map/all_to_all | solution.py:558
  41.8 2.3 %collective-permute-start.8 = (f32[16,512]{1,0:T(8,128)S(1)}, f32[16,512]{1,0:T(8,128)S(1)}, u32[]{:S(2)}, u32[]{:S(2)}) collective-permute-start(f32[16,512]{1,0:T(8,128)S(1)} %shard_map.130.sent_back), channel_id=1, source_target_pairs={{0,4},{4,0},{8,12},{12,8},{16,20},{20,16},{24,28},{28,24},{32,36},... | collective-permute-start | bytes 98312 | tf_op jit(solution)/shard_map/ppermute | solution.py:508

commit v8 on v7

--- a/solution.py
+++ b/solution.py
@@ -24,11 +24,6 @@
     return a, b, c
 
 
-def halves(v):
-    a = v.astype(BF16)
-    return a, (v - a.astype(F32)).astype(BF16)
-
-
 def mm(a, b):
     return jnp.dot(a, b, preferred_element_type=F32)
 
@@ -38,28 +33,25 @@
     return (mm(exact, c) + mm(exact, b)) + mm(exact, a)
 
 
-def product(x, t_hi, t_lo):
-    hi, lo = halves(x)
-    return (mm(lo, t_hi) + mm(hi, t_lo)) + mm(hi, t_hi)
+def product(x, taps):
+    a, b, c = thirds(x)
+    h, m, l = (t[...] for t in taps)
+    return ((mm(c, h) + mm(a, l)) + mm(b, m)) + (mm(b, h) + mm(a, m)) + mm(a, h)
 
 
 def forward(v, taps):
-    t0h, t0l, t1h, t1l = taps
     rows = v.shape[0]
     half = v.shape[1] // 2
-    both = jnp.concatenate([v[:, :half], v[:, half:]], axis=0)
-    near = product(both, t0h[...], t0l[...])
-    far = product(v[:, :half], t1h[...], t1l[...])
+    near = product(jnp.concatenate([v[:, :half], v[:, half:]], axis=0), taps[:3])
+    far = product(v[:, :half], taps[3:])
     return jnp.concatenate([near[:rows], near[rows:] + far], axis=1)
 
 
 def backward(v, taps):
-    t0h, t0l, t1h, t1l = taps
     rows = v.shape[0]
     half = v.shape[1] // 2
-    both = jnp.concatenate([v[:, :half], v[:, half:]], axis=0)
-    near = product(both, t0h[...], t0l[...])
-    far = product(v[:, half:], t1h[...], t1l[...])
+    near = product(jnp.concatenate([v[:, :half], v[:, half:]], axis=0), taps[:3])
+    far = product(v[:, half:], taps[3:])
     return jnp.concatenate([near[:rows] + far, near[rows:]], axis=1)
 
 
@@ -238,9 +230,9 @@
 
 
 def inside_first(
-    sent, coef, sigma, measured, prior, part_in, arrived, l_a, s_a, out_a,
-    t0h, t0l, t1h, t1l, u0h, u0l, u1h, u1l, weight, near, rvar, gain, part, base,
+    sent, coef, sigma, measured, prior, part_in, arrived, l_a, s_a, out_a, *outs,
 ):
+    taps, (weight, near, rvar, gain, part, base) = outs[:12], outs[12:]
     length = coef.shape[1]
     half = length // 2
     c = coef[...]
@@ -248,19 +240,18 @@
     upper = iota((half, half), 1) >= iota((half, half), 0)
     t0 = jnp.where(upper, shifted[:, :half], 0.0)
     t1 = shifted[:, half:]
-    for hi, lo, x in ((t0h, t0l, t0), (t1h, t1l, t1), (u0h, u0l, t0.T), (u1h, u1l, t1.T)):
-        a, b = halves(x)
-        hi[...] = a
-        lo[...] = b
+    for k, x in enumerate((t0, t1, t0.T, t1.T)):
+        for ref, term in zip(taps[3 * k : 3 * k + 3], thirds(x)):
+            ref[...] = term
     size = jnp.sum(jnp.abs(c), axis=1, keepdims=True)
     scale = 1.0 / (4.0 * size * size + 64.0)
     gain[...] = jnp.broadcast_to(PENALTY * scale, gain.shape)
     sig = jnp.transpose(jnp.broadcast_to(sigma[...], (128, 128)))[:, 0:1]
     rsig = 1.0 / sig
-    whitened = forward((measured[...] - prior[...]) * rsig, (t0h, t0l, t1h, t1l))
+    whitened = forward((measured[...] - prior[...]) * rsig, taps[:6])
     h = EDGE / jnp.maximum(jnp.abs(whitened), EDGE)
     weight[...] = h
-    n = backward(h * whitened, (u0h, u0l, u1h, u1l)) * rsig
+    n = backward(h * whitened, taps[6:]) * rsig
     near[...] = n
     rvar[...] = jnp.broadcast_to(rsig * rsig * scale, rvar.shape)
     p = part_in[...] + pick(l_a[...], arrived[...])
@@ -274,7 +265,7 @@
     r_out[...] = r
     p = pick(inc[...], r) + pick(l_a[...], arrived[...])
     part[...] = p
-    n = backward(weight[...] * forward(r, taps[:4]), taps[4:]) * rvar[:, 0:1]
+    n = backward(weight[...] * forward(r, taps[:6]), taps[6:]) * rvar[:, 0:1]
     near[...] = n
     outward(gain[0:1, 0:1], p, n, s_a, out_a, base)
     return r, p, n
@@ -282,13 +273,13 @@
 
 def inside_one(*refs):
     *refs, sums = refs
-    r, _, _ = inside(*refs[:13], refs[13:21], *refs[21:])
+    r, _, _ = inside(*refs[:13], refs[13:25], *refs[25:])
     sums[...] = lanes_sum(r * r)
 
 
 def inside_two(before, *refs):
     *refs, sums = refs
-    r, _, _ = inside(*refs[:13], refs[13:21], *refs[21:])
+    r, _, _ = inside(*refs[:13], refs[13:25], *refs[25:])
     sums[0:8, :] = lanes_sum(before[...] * r)
     sums[8:16, :] = lanes_sum(r * r)
 
@@ -296,7 +287,7 @@
 def inside_three(before, sum0, sum1, *refs):
     *refs, row = refs
     gain = refs[1]
-    r, p, n = inside(*refs[:13], refs[13:21], *refs[21:])
+    r, p, n = inside(*refs[:13], refs[13:25], *refs[25:])
     tiles = (
         sum0[0:8, :], sum1[0:8, :], sum1[8:16, :], lanes_sum(before[...] * r), lanes_sum(r * r),
         lanes_sum(r * n) + gain[0:1, 0:1] * lanes_sum(p * p),
@@ -529,10 +520,10 @@
     got = cross(sent)
     out = call(
         inside_first,
-        [half] * 8 + [field, field, ((pipes, 128), F32), tile, heads, msg2],
+        [half] * 12 + [field, field, ((pipes, 128), F32), tile, heads, msg2],
         sent, coef, sigma, measured, prior, part, arrived, l_a, s_a, out_a,
     )
-    taps, (weight, near, rvar, gain, part, base) = out[:8], out[8:]
+    taps, (weight, near, rvar, gain, part, base) = out[:12], out[12:]
     (back,) = call(back_kernel, [msg2], gain0, got, base, mid_a)
     back_got = swap(back)
     w, base, far = call(

time: 52.4 us -> 52.4 us (level)
  waiting for transfers between devices: 10.6 us -> 8.03 us
  Pallas kernels: 14.2 us -> 16.7 us
    ppermute x4, waiting for transfers between devices: 3.01 us -> 0.44 us  [cross(): return lax.ppermute(x, (*NET, 'hour'), across)]
    pallas_call x19, Pallas kernels: 11.9 us -> 14.4 us  [call(): pl.pallas_call(kernel, out_shape=tuple((pltpu.VMEM(s, d) for s, d in outs...]
    ppermute x4, starting transfers between devices: 6 us -> 7.48 us  [cross(): return lax.ppermute(x, (*NET, 'hour'), across)]
    all_to_all x1, starting transfers between devices: 16.6 us -> 15.2 us  [shards(): lax.all_to_all(rows.reshape(devices, 1, 128), ('core', 'z', 'y', 'hour'),...]
  transfers between devices with their start and end apart: 10 -> 10, of which waited for: 9 -> 6; matrix products, arithmetic and copies ran while one was open for 0% -> 0% of each run, Pallas kernels for 19% -> 24%
where the time goes in v8:
time: 52.4 us; the launch traced here: 52.2 us
  starting transfers between devices  26.8 us (51%)
  Pallas kernels  16.7 us (32%)
  waiting for transfers between devices  8.03 us (15%)
  between operations  0.7 us (1%)
    all_to_all x1, starting transfers between devices, shards(): lax.all_to_all(rows.reshape(devices, 1, 128), ('core', 'z', 'y', 'hour'),...  15.2 us
    pallas_call x19, Pallas kernels, call(): pl.pallas_call(kernel, out_shape=tuple((pltpu.VMEM(s, d) for s, d in outs...  14.4 us
    ppermute x4, starting transfers between devices, cross(): return lax.ppermute(x, (*NET, 'hour'), across)  7.48 us
    all_to_all x1, waiting for transfers between devices, shards(): lax.all_to_all(rows.reshape(devices, 1, 128), ('core', 'z', 'y', 'hour'),...  6.77 us
    ppermute x5, starting transfers between devices, swap(): return lax.ppermute(x, NET, on_chip)  4.12 us
    pallas_call x1, Pallas kernels, finish(): pl.pallas_call(finish_kernel, out_shape=(jax.ShapeDtypeStruct(field.shape...  1.14 us
    pallas_call x1, Pallas kernels, bring(): pl.pallas_call(open_kernel, out_shape=tuple((pltpu.VMEM(x.shape, x.dtype)...  1.14 us
  transfers between devices with their start and end apart: 10, of which 6 were waited for; matrix products, arithmetic and copies ran while one was open for 0% of the time, Pallas kernels for 24%

profile of v8, /device:TPU:1, one launch (start us, length us, event | category | flops | bytes accessed | tf_op | source)
XLA Modules:
  0.0 52.2 jit_solution(10574508066590078161)
XLA Ops:
  0.6 0.0 copy-start.1
  0.6 1.1 %shard_map.113 = (f32[128,512]{1,0:T(8,128)S(1)}, s32[1,2,8]{2,1,0:T(2,128)S(1)}, s32[1,2]{1,0:T(1,128)S(1)}, s32[1,2,8]{2,1,0:T(2,128)S(1)}, s32[1,128]{1,0:T(1...) custom-call(f32[128,512]{1,0:T(8,128)} %prior_in.1, ...), custom_call_target="tpu_custom_call" | custom-call | tf_op jit(solution)/shard_map/pallas_call | solution.py:441
  1.8 1.5 %collective-permute-start = (f32[16,512]{1,0:T(8,128)S(1)}, f32[16,512]{1,0:T(8,128)S(1)}, u32[]{:S(2)}, u32[]{:S(2)}) collective-permute-start(f32[16,512]{1,0:T(8,128)S(1)} %get-tuple-element.75.sent), channel_id=1, source_target_pairs={{0,4},{4,0},{8,12},{12,8},{16,20},{20,16},{24,28},{28,24},{32,36},... | collective-permute-start | bytes 98312 | tf_op jit(solution)/shard_map/ppermute | solution.py:499
  3.2 0.0 copy-done.1
  3.3 0.0 copy-start
  3.3 0.7 %shard_map.114 = (bf16[8,128]{1,0:T(8,128)(2,1)S(1)}, bf16[128,8]{1,0:T(8,128)(2,1)S(1)}, bf16[96,128]{1,0:T(8,128)(2,1)S(1)}, bf16[96,8]{1,0:T(8,128)(2,1)S(1)}...) custom-call(f32[16,512]{1,0:T(8,128)S(1)} %get-tuple-element.75.sent, ...), custom_call_target="tpu_custom_call" | custom-call | tf_op jit(solution)/shard_map/pallas_call | solution.py:430
  4.0 0.1 collective-permute-done.got
  4.1 0.1 shard_map.115
  4.2 2.0 %collective-permute-start.1 = (f32[16,640]{1,0:T(8,128)S(1)}, f32[16,640]{1,0:T(8,128)S(1)}, u32[]{:S(2)}, u32[]{:S(2)}) collective-permute-start(f32[16,640]{1,0:T(8,128)S(1)} %get-tuple-element.85.sent), channel_id=1, source_target_pairs={{4,8},{8,4},{12,16},{16,12},{20,24},{24,20},{28,32},{32,28},{36,40... | collective-permute-start | bytes 122888 | tf_op jit(solution)/shard_map/ppermute | solution.py:502
  6.2 0.0 copy-done
  6.2 2.0 %shard_map.116 = (bf16[256,256]{1,0:T(8,128)(2,1)S(1)}, bf16[256,256]{1,0:T(8,128)(2,1)S(1)}, bf16[256,256]{1,0:T(8,128)(2,1)S(1)}, bf16[256,256]{1,0:T(8,128)(2...) custom-call(f32[16,640]{1,0:T(8,128)S(1)} %get-tuple-element.85.sent, ...), custom_call_target="tpu_custom_call" | custom-call | tf_op jit(solution)/shard_map/pallas_call | solution.py:430
  8.2 0.0 collective-permute-done.1.got
  8.2 0.2 shard_map.117.sent_back.sent
  8.3 0.4 collective-permute-start.2
  8.7 0.6 %shard_map.118 = (f32[128,512]{1,0:T(8,128)S(1)}, f32[16,512]{1,0:T(8,128)S(1)}, f32[8,8]{1,0:T(8,128)S(1)}) custom-call(f32[8,128]{1,0:T(8,128)S(1)} %get-tuple-element.94.gain.refs_0_, f32[16,512]{1,0:T(8,128)S(1)} %shard_map.117.sent_back.sent, f32[16,640]{1,0:T(8,128)S(1)} %collective-permute-done.1.got, f32[16,640]{1,0:T(8,128)S(1)} %get-tuple-element.85.sent, ...), custom_call_target="tpu_custom_call" | custom-call | tf_op jit(solution)/shard_map/pallas_call | solution.py:430
  9.4 0.2 collective-permute-done.2.got.refs_4_
  9.6 0.1 shard_map.119
  9.7 1.7 %collective-permute-start.3 = (f32[16,512]{1,0:T(8,128)S(1)}, f32[16,512]{1,0:T(8,128)S(1)}, u32[]{:S(2)}, u32[]{:S(2)}) collective-permute-start(f32[16,512]{1,0:T(8,128)S(1)} %get-tuple-element.104.refs_2_.sent), channel_id=1, source_target_pairs={{4,8},{8,4},{12,16},{16,12},{20,24},{24,20},{28,32},{32,28},{36,40... | collective-permute-start | bytes 98312 | tf_op jit(solution)/shard_map/ppermute | solution.py:502
  11.4 2.0 %shard_map.120 = (f32[128,512]{1,0:T(8,128)S(1)}, f32[96,512]{1,0:T(8,128)S(1)}, f32[128,512]{1,0:T(8,128)S(1)}, f32[16,512]{1,0:T(8,128)S(1)}, f32[8,128]{1,0:T(8,128)S(1)}) custom-call(f32[8,128]{1,0:T(8,128)S(1)} %get-tuple-element.94.gain.refs_0_, f32[8,128]{1,0:T(8,128)S(1)} %get-tuple-element.93.refs_1_.gain.refs_0_, ...), custom_call_target="tpu_custom_call" | custom-call | tf_op jit(solution)/shard_map/pallas_call | solution.py:430
  13.4 0.0 collective-permute-done.3.got
  13.4 0.2 shard_map.121.sent_back.sent
  13.5 0.6 %collective-permute-start.4 = (f32[16,512]{1,0:T(8,128)S(1)}, f32[16,512]{1,0:T(8,128)S(1)}, u32[]{:S(2)}, u32[]{:S(2)}) collective-permute-start(f32[16,512]{1,0:T(8,128)S(1)} %shard_map.121.sent_back.sent), channel_id=1, source_target_pairs={{0,4},{4,0},{8,12},{12,8},{16,20},{20,16},{24,28},{28,24},{32,36},... | collective-permute-start | bytes 98312 | tf_op jit(solution)/shard_map/ppermute | solution.py:499
  14.1 0.6 %shard_map.122 = (f32[128,512]{1,0:T(8,128)S(1)}, f32[16,512]{1,0:T(8,128)S(1)}) custom-call(f32[8,128]{1,0:T(8,128)S(1)} %get-tuple-element.93.refs_1_.gain.refs_0_, f32[16,512]{1,0:T(8,128)S(1)} %shard_map.121.sent_back.sent, f32[16,512]{1,0:T(8,128)S(1)} %collective-permute-done.3.got, f32[16,512]{1,0:T(8,128)S(1)} %get-tuple-element.104.refs_2_.sent, ...), custom_call_target="tpu_custom_call" | custom-call | tf_op jit(solution)/shard_map/pallas_call | solution.py:430
  14.7 0.2 collective-permute-done.4.got.refs_4_
  15.0 0.1 shard_map.123
  15.1 1.2 %collective-permute-start.5 = (f32[16,512]{1,0:T(8,128)S(1)}, f32[16,512]{1,0:T(8,128)S(1)}, u32[]{:S(2)}, u32[]{:S(2)}) collective-permute-start(f32[16,512]{1,0:T(8,128)S(1)} %get-tuple-element.128.refs_2_.sent), channel_id=1, source_target_pairs={{4,8},{8,4},{12,16},{16,12},{20,24},{24,20},{28,32},{32,28},{36,40... | collective-permute-start | bytes 98312 | tf_op jit(solution)/shard_map/ppermute | solution.py:502
  16.3 2.0 %shard_map.124 = (f32[128,512]{1,0:T(8,128)S(1)}, f32[96,512]{1,0:T(8,128)S(1)}, f32[128,512]{1,0:T(8,128)S(1)}, f32[16,512]{1,0:T(8,128)S(1)}, f32[16,128]{1,0:T(8,128)S(1)}) custom-call(f32[128,512]{1,0:T(8,128)S(1)} %get-tuple-element.129.before.r0, f32[8,128]{1,0:T(8,128)S(1)} %get-tuple-element.93.refs_1_.gain.refs_0_, ...), custom_call_target="tpu_custom_call" | custom-call | tf_op jit(solution)/shard_map/pallas_call | solution.py:430
  18.3 0.4 collective-permute-done.5.got
  18.7 0.1 shard_map.125.sent_back.sent
  18.9 0.6 %collective-permute-start.6 = (f32[16,512]{1,0:T(8,128)S(1)}, f32[16,512]{1,0:T(8,128)S(1)}, u32[]{:S(2)}, u32[]{:S(2)}) collective-permute-start(f32[16,512]{1,0:T(8,128)S(1)} %shard_map.125.sent_back.sent), channel_id=1, source_target_pairs={{0,4},{4,0},{8,12},{12,8},{16,20},{20,16},{24,28},{28,24},{32,36},... | collective-permute-start | bytes 98312 | tf_op jit(solution)/shard_map/ppermute | solution.py:499
  19.5 0.6 %shard_map.126 = (f32[128,512]{1,0:T(8,128)S(1)}, f32[16,512]{1,0:T(8,128)S(1)}) custom-call(f32[8,128]{1,0:T(8,128)S(1)} %get-tuple-element.93.refs_1_.gain.refs_0_, f32[16,512]{1,0:T(8,128)S(1)} %shard_map.125.sent_back.sent, f32[16,512]{1,0:T(8,128)S(1)} %collective-permute-done.5.got, f32[16,512]{1,0:T(8,128)S(1)} %get-tuple-element.128.refs_2_.sent, ...), custom_call_target="tpu_custom_call" | custom-call | tf_op jit(solution)/shard_map/pallas_call | solution.py:430
  20.1 0.2 collective-permute-done.6.got.refs_4_
  20.4 0.1 shard_map.127
  20.5 2.6 %collective-permute-start.7 = (f32[16,512]{1,0:T(8,128)S(1)}, f32[16,512]{1,0:T(8,128)S(1)}, u32[]{:S(2)}, u32[]{:S(2)}) collective-permute-start(f32[16,512]{1,0:T(8,128)S(1)} %get-tuple-element.136.refs_2_.sent), channel_id=1, source_target_pairs={{4,8},{8,4},{12,16},{16,12},{20,24},{24,20},{28,32},{32,28},{36,40... | collective-permute-start | bytes 98312 | tf_op jit(solution)/shard_map/ppermute | solution.py:502
  23.1 2.4 %shard_map.128 = (f32[128,512]{1,0:T(8,128)S(1)}, f32[96,512]{1,0:T(8,128)S(1)}, f32[128,512]{1,0:T(8,128)S(1)}, f32[16,512]{1,0:T(8,128)S(1)}, f32[8,128]{1,0:T(8,128)S(1)}) custom-call(f32[128,512]{1,0:T(8,128)S(1)} %get-tuple-element.137.before.r1, f32[8,128]{1,0:T(8,128)S(1)} %get-tuple-element.138.sum0, f32[16,128]{1,0:T(8,128)S(1)} %get-tuple-element.139.sum1, ...), custom_call_target="tpu_custom_call" | custom-call | tf_op jit(solution)/shard_map/pallas_call | solution.py:430
  25.6 0.0 collective-permute-done.7.got
  25.6 0.8 %shard_map.129 = f32[128,128]{1,0:T(8,128)} custom-call(f32[8,128]{1,0:T(8,128)S(1)} %get-tuple-element.93.refs_1_.gain.refs_0_, f32[16,512]{1,0:T(8,128)S(1)} %get-tuple-element.136.refs_2_.sent, f32[16,512]{1,0:T(8,128)S(1)} %collective-permute-done.7.got, f32[8,8]{1,0:T(8,128)S(1)} %get-tuple-element.84.own, f32[8,128]{1,0:T(8,128)S(1)} %get-tuple-element.142.row), custom_call_target="tpu_custom_call" | custom-call | tf_op jit(solution)/shard_map/pallas_call | solution.py:430
  26.4 15.2 %all-to-all-start = ((f32[128,1,128]{2,1,0:T(1,128)}), f32[128,1,128]{2,1,0:T(1,128)S(1)}, u32[]{:S(2)}, u32[]{:S(2)}) async-start(f32[128,1,128]{2,1,0:T(1,128)} %bitcast.5), calls=%async_computation | async-start | bytes 131072 | tf_op jit(solution)/shard_map/all_to_all | solution.py:549
  41.6 0.1 shard_map.130.sent_back
  41.8 1.1 %collective-permute-start.8 = (f32[16,512]{1,0:T(8,128)S(1)}, f32[16,512]{1,0:T(8,128)S(1)}, u32[]{:S(2)}, u32[]{:S(2)}) collective-permute-start(f32[16,512]{1,0:T(8,128)S(1)} %shard_map.130.sent_back), channel_id=1, source_target_pairs={{0,4},{4,0},{8,12},{12,8},{16,20},{20,16},{24,28},{28,24},{32,36},... | collective-permute-start | bytes 98312 | tf_op jit(solution)/shard_map/ppermute | solution.py:499
  42.8 1.2 %shard_map.131 = (f32[128,512]{1,0:T(8,128)S(1)}, f32[16,512]{1,0:T(8,128)}) custom-call(f32[8,128]{1,0:T(8,128)S(1)} %get-tuple-element.93.refs_1_.gain.refs_0_, f32[16,512]{1,0:T(8,128)S(1)} %shard_map.130.sent_back, f32[16,512]{1,0:T(8,128)S(1)} %collective-permute-done.7.got, f32[16,512]{1,0:T(8,128)S(1)} %get-tuple-element.136.refs_2_.sent, ...), custom_call_target="tpu_custom_call" | custom-call | tf_op jit(solution)/shard_map/pallas_call | solution.py:430
  44.1 0.0 collective-permute-done.8.got
  44.1 0.2 shard_map.132.r3
  44.3 6.8 %all-to-all-done = f32[128,1,128]{2,1,0:T(1,128)S(1)} async-done(((f32[128,1,128]{2,1,0:T(1,128)}), f32[128,1,128]{2,1,0:T(1,128)S(1)}, u32[]{:S(2)}, u32[]{:S(2)}) %all-to-all-start) | async-done | bytes 65568 | tf_op jit(solution)/shard_map/all_to_all | solution.py:549
  51.1 1.1 %shard_map.133 = (f32[128,512]{1,0:T(8,128)}, f32[128,512]{1,0:T(8,128)}) custom-call(f32[128,128]{1,0:T(8,128)S(1)} %bitcast.8, f32[8,128]{1,0:T(8,128)S(1)} %get-tuple-element.93.refs_1_.gain.refs_0_, f32[128,512]{1,0:T(8,128)S(1)} %get-tuple-element.76.prior, f32[128,512]{1,0:T(8,128)S(1)} %get-tuple-element.129.before.r0, ...), custom_call_target="tpu_custom_call" | custom-call | tf_op jit(solution)/shard_map/pallas_call | solution.py:454
Async XLA Ops:
  0.6 2.6 %copy-start.1 = (f32[96,512]{1,0:T(8,128)S(1)}, f32[96,512]{1,0:T(8,128)}, u32[]{:S(2)}) copy-start(f32[96,512]{1,0:T(8,128)} %demand.1) | copy-start | bytes 589828
  1.8 2.3 %collective-permute-start = (f32[16,512]{1,0:T(8,128)S(1)}, f32[16,512]{1,0:T(8,128)S(1)}, u32[]{:S(2)}, u32[]{:S(2)}) collective-permute-start(f32[16,512]{1,0:T(8,128)S(1)} %get-tuple-element.75.sent), channel_id=1, source_target_pairs={{0,4},{4,0},{8,12},{12,8},{16,20},{20,16},{24,28},{28,24},{32,36},... | collective-permute-start | bytes 98312 | tf_op jit(solution)/shard_map/ppermute | solution.py:499
  3.3 3.0 %copy-start = (f32[128,512]{1,0:T(8,128)S(1)}, f32[128,512]{1,0:T(8,128)}, u32[]{:S(2)}) copy-start(f32[128,512]{1,0:T(8,128)} %measured.1) | copy-start | bytes 786436
  4.2 4.0 %collective-permute-start.1 = (f32[16,640]{1,0:T(8,128)S(1)}, f32[16,640]{1,0:T(8,128)S(1)}, u32[]{:S(2)}, u32[]{:S(2)}) collective-permute-start(f32[16,640]{1,0:T(8,128)S(1)} %get-tuple-element.85.sent), channel_id=1, source_target_pairs={{4,8},{8,4},{12,16},{16,12},{20,24},{24,20},{28,32},{32,28},{36,40... | collective-permute-start | bytes 122888 | tf_op jit(solution)/shard_map/ppermute | solution.py:502
  8.3 1.2 %collective-permute-start.2 = (f32[16,512]{1,0:T(8,128)S(1)}, f32[16,512]{1,0:T(8,128)S(1)}, u32[]{:S(2)}, u32[]{:S(2)}) collective-permute-start(f32[16,512]{1,0:T(8,128)S(1)} %shard_map.117.sent_back.sent), channel_id=1, source_target_pairs={{0,4},{4,0},{8,12},{12,8},{16,20},{20,16},{24,28},{28,24},{32,36},... | collective-permute-start | bytes 98312 | tf_op jit(solution)/shard_map/ppermute | solution.py:499
  9.7 3.7 %collective-permute-start.3 = (f32[16,512]{1,0:T(8,128)S(1)}, f32[16,512]{1,0:T(8,128)S(1)}, u32[]{:S(2)}, u32[]{:S(2)}) collective-permute-start(f32[16,512]{1,0:T(8,128)S(1)} %get-tuple-element.104.refs_2_.sent), channel_id=1, source_target_pairs={{4,8},{8,4},{12,16},{16,12},{20,24},{24,20},{28,32},{32,28},{36,40... | collective-permute-start | bytes 98312 | tf_op jit(solution)/shard_map/ppermute | solution.py:502
  13.5 1.4 %collective-permute-start.4 = (f32[16,512]{1,0:T(8,128)S(1)}, f32[16,512]{1,0:T(8,128)S(1)}, u32[]{:S(2)}, u32[]{:S(2)}) collective-permute-start(f32[16,512]{1,0:T(8,128)S(1)} %shard_map.121.sent_back.sent), channel_id=1, source_target_pairs={{0,4},{4,0},{8,12},{12,8},{16,20},{20,16},{24,28},{28,24},{32,36},... | collective-permute-start | bytes 98312 | tf_op jit(solution)/shard_map/ppermute | solution.py:499
  15.1 3.6 %collective-permute-start.5 = (f32[16,512]{1,0:T(8,128)S(1)}, f32[16,512]{1,0:T(8,128)S(1)}, u32[]{:S(2)}, u32[]{:S(2)}) collective-permute-start(f32[16,512]{1,0:T(8,128)S(1)} %get-tuple-element.128.refs_2_.sent), channel_id=1, source_target_pairs={{4,8},{8,4},{12,16},{16,12},{20,24},{24,20},{28,32},{32,28},{36,40... | collective-permute-start | bytes 98312 | tf_op jit(solution)/shard_map/ppermute | solution.py:502
  18.9 1.5 %collective-permute-start.6 = (f32[16,512]{1,0:T(8,128)S(1)}, f32[16,512]{1,0:T(8,128)S(1)}, u32[]{:S(2)}, u32[]{:S(2)}) collective-permute-start(f32[16,512]{1,0:T(8,128)S(1)} %shard_map.125.sent_back.sent), channel_id=1, source_target_pairs={{0,4},{4,0},{8,12},{12,8},{16,20},{20,16},{24,28},{28,24},{32,36},... | collective-permute-start | bytes 98312 | tf_op jit(solution)/shard_map/ppermute | solution.py:499
  20.5 5.1 %collective-permute-start.7 = (f32[16,512]{1,0:T(8,128)S(1)}, f32[16,512]{1,0:T(8,128)S(1)}, u32[]{:S(2)}, u32[]{:S(2)}) collective-permute-start(f32[16,512]{1,0:T(8,128)S(1)} %get-tuple-element.136.refs_2_.sent), channel_id=1, source_target_pairs={{4,8},{8,4},{12,16},{16,12},{20,24},{24,20},{28,32},{32,28},{36,40... | collective-permute-start | bytes 98312 | tf_op jit(solution)/shard_map/ppermute | solution.py:502
  26.4 24.7 %all-to-all-start = ((f32[128,1,128]{2,1,0:T(1,128)}), f32[128,1,128]{2,1,0:T(1,128)S(1)}, u32[]{:S(2)}, u32[]{:S(2)}) async-start(f32[128,1,128]{2,1,0:T(1,128)} %bitcast.5), calls=%async_computation | async-start | bytes 131072 | tf_op jit(solution)/shard_map/all_to_all | solution.py:549
  41.8 2.3 %collective-permute-start.8 = (f32[16,512]{1,0:T(8,128)S(1)}, f32[16,512]{1,0:T(8,128)S(1)}, u32[]{:S(2)}, u32[]{:S(2)}) collective-permute-start(f32[16,512]{1,0:T(8,128)S(1)} %shard_map.130.sent_back), channel_id=1, source_target_pairs={{0,4},{4,0},{8,12},{12,8},{16,20},{20,16},{24,28},{28,24},{32,36},... | collective-permute-start | bytes 98312 | tf_op jit(solution)/shard_map/ppermute | solution.py:499

commit v9 on v8

--- a/solution.py
+++ b/solution.py
@@ -115,7 +115,7 @@
 def open_kernel(prior_in, *refs):
     count = 8
     ins, prior, copies = (prior_in, *refs[: count - 1]), refs[count - 1], refs[count - 1 : 2 * count - 1]
-    msg, sems, pipe_of, count_of = refs[2 * count - 1 :]
+    msg, flow, sems, pipe_of, count_of = refs[2 * count - 1 :]
     moves = [pltpu.make_async_copy(ins[1], pipe_of, sems.at[count]), pltpu.make_async_copy(ins[2], count_of, sems.at[count + 1])]
     piece = prior.shape[0] // 4
     for k in range(4):
@@ -129,15 +129,18 @@
     cap = pipe_of.shape[2]
     side = jnp.where(is_odd(), 0, 1)
     live = count_of[0, side]
+    live_b = count_of[0, 1 - side]
     for k in range(cap):
         row = prior[pl.ds(pipe_of[0, side, k], 1), :]
         msg[k : k + 1, :] = jnp.where(k < live, -row, 0.0)
+        row = prior[pl.ds(pipe_of[0, 1 - side, k], 1), :]
+        flow[k : k + 1, :] = jnp.where(k < live_b, -row, 0.0)
     msg[cap:, :] = jnp.where(iota((cap, prior.shape[1]), 0) < live, 1.0, 0.0)
     for m in moves[6:]:
         m.wait()
 
 
-def lists_kernel(sent, prior, bp, bc, aj, head, tail, demand, s_a, s_at, inc, l_a, l_b, it_sb, out_b, out_a, mid_b, mid_a, own, gain, part, base):
+def lists_kernel(sent, prior, bp, bc, aj, head, tail, demand, s_ab, s_abt, inc, inc_t, l_a, l_b, out_b, out_a, mid_b, mid_a, own, gain, live_b, part, base):
     cap = bp.shape[2]
     pipes = prior.shape[0]
     juncs = inc.shape[0]
@@ -159,78 +162,109 @@
     both_t = square[:, :juncs]
     pad = jnp.zeros((128 - 2 * cap, 128), F32)
     turned = jnp.transpose(jnp.concatenate([sel_a, sel_b, pad], axis=0))
-    sel_at, sel_bt = turned[:, :cap], turned[:, cap : 2 * cap]
     both16, a16, b16 = both.astype(BF16), land_a.astype(BF16), land_b.astype(BF16)
-    bt16 = land_bt.astype(BF16)
-    s_a[...] = sel_a.astype(BF16)
-    s_at[...] = sel_at.astype(BF16)
+    at16, bt16, inc_t16 = land_at.astype(BF16), land_bt.astype(BF16), both_t.astype(BF16)
+    sel16, selt16 = jnp.concatenate([sel_a, sel_b], axis=0).astype(BF16), turned[:, : 2 * cap].astype(BF16)
+    s_ab[...] = sel16
+    s_abt[...] = selt16
     inc[...] = both16
+    inc_t[...] = inc_t16
     l_a[...] = a16
     l_b[...] = b16
-    it_sb[...] = jnp.concatenate([both_t, sel_bt], axis=1).astype(BF16)
     b_inc = mm(bt16, both16)
-    a_inc = mm(sel_a.astype(BF16), both_t.astype(BF16))
-    out_b[...] = jnp.concatenate([sel_b, b_inc], axis=0).astype(BF16)
-    out_a[...] = jnp.concatenate([land_at, a_inc], axis=0).astype(BF16)
-    mid_b[...] = thrice(jnp.concatenate([mm(b_inc.astype(BF16), sel_at.astype(BF16)), mm(bt16, a16)], axis=1))
-    mid_a[...] = thrice(jnp.concatenate([mm(land_at.astype(BF16), b16), mm(a_inc.astype(BF16), b16)], axis=0))
+    b_inc16 = b_inc.astype(BF16)
+    out_b[...] = b_inc16
+    ends = jnp.concatenate([land_at, mm(sel16, inc_t16)], axis=0)
+    out_a[...] = ends.astype(BF16)
+    to_sel = mm(b_inc16, selt16)
+    mid_b[...] = thrice(jnp.concatenate([to_sel, mm(bt16, a16)], axis=1))
+    mid_a[...] = thrice(mm(ends.astype(BF16), b16))
     own[...] = mm(bt16, b16)
     gain[...] = jnp.full(gain.shape, PENALTY, F32)
-    x = prior[...]
-    p = demand[...] - pick(both16, x)
+    live_b[...] = jnp.broadcast_to(jnp.sum(sel_b, axis=1, keepdims=True), live_b.shape)
+    p = demand[...] - pick(both16, prior[...])
     part[...] = p
-    base[0:cap, :] = -pick(sel_b.astype(BF16), x)
-    base[cap:, :] = pick(bt16, p)
+    base[...] = pick(bt16, p)
 
 
 def across_first(got, base, mid_b, own, msg, arrived, live):
-    cap = own.shape[0]
-    hours = base.shape[1]
+    cap, hours = base.shape
     arr = got[0:cap, :]
     arrived[...] = arr
     live[...] = got[cap:, 0:128]
-    msg[0:cap, 0:hours] = base[0:cap, :]
-    both = jnp.concatenate([jnp.zeros_like(arr), arr], axis=0)
-    msg[cap:, 0:hours] = base[cap:, :] + mm(mid_b[...], stack3(both))
-    msg[:, hours:] = jnp.zeros((2 * cap, msg.shape[1] - hours), F32)
-    msg[0:cap, hours : hours + cap] = own[...]
+    none = jnp.zeros_like(arr)
+    msg[:, 0:hours] = base[...] + mm(mid_b[...], stack3(jnp.concatenate([none, none, arr], axis=0)))
+    msg[:, hours:] = jnp.zeros((cap, msg.shape[1] - hours), F32)
+    msg[:, hours : hours + cap] = own[...]
 
 
 def wide(tile, v):
     return jnp.concatenate([tile] * (v.shape[1] // 128), axis=1)
 
 
-def across_next(gain, sent, got, live, base, mid_b, msg, arrived):
+def across(gain, sent, got, live, base, mid_b, cut_b, adds, arrived):
     cap = live.shape[0]
     g = gain[...]
     added = wide(g, sent) * got[0:cap, :]
     arr = got[cap:, :] + wide(g * live[...], sent) * sent[0:cap, :]
     arrived[...] = arr
-    msg[0:cap, :] = base[0:cap, :]
-    msg[cap:, :] = base[cap:, :] + mm(mid_b[...], stack3(jnp.concatenate([added, arr], axis=0)))
-
-
-def whole_kernel(gain, w, got, s_at, r_out):
-    cap = s_at.shape[1]
-    r_out[...] = w[...] + gain[0:1, 0:1] * pick(s_at[...], got[0:cap, :])
-
-
-def back_kernel(gain, got, base, mid_a, msg):
-    cap, hours = msg.shape[0] // 2, msg.shape[1]
-    x = mm(mid_a[...], stack3(got[0:cap, 0:hours]))
+    adds[0:cap, :] = added
+    adds[cap:, :] = cut_b
+    return base[...] + mm(mid_b[...], stack3(jnp.concatenate([added, cut_b, arr], axis=0)))
+
+
+def across_zero(gain, sent, got, live, base, mid_b, flow, heads, sent_flow, live_b, msg, adds, arrived, far):
+    cap, hours = base.shape
+    match = heads[:, hours : hours + cap]
+    far[...] = match
+    y_far = heads[:, 0:hours] + mm(thrice(match), stack3(sent_flow[...]))
+    cut_b = wide(gain[...] * live_b[...], y_far) * y_far
+    msg[0:cap, :] = flow[...] + cut_b
+    msg[cap:, :] = across(gain, sent, got, live, base, mid_b, cut_b, adds, arrived)
+
+
+def across_both(gain, sent, got, live, base, mid_b, flow, cut_b, msg, adds, arrived):
+    cap = base.shape[0]
+    msg[0:cap, :] = flow[...]
+    msg[cap:, :] = across(gain, sent, got, live, base, mid_b, cut_b[...], adds, arrived)
+
+
+def whole_kernel(gain, w, got, cut_b, s_abt, r_out):
+    cap = cut_b.shape[0]
+    added = jnp.concatenate([gain[0:1, 0:1] * got[0:cap, :], cut_b[...]], axis=0)
+    r_out[...] = w[...] + pick(s_abt[...], added)
+
+
+def back(gain, flows, base, mid_a, msg):
+    cap = flows.shape[0]
+    x = mm(mid_a[...], stack3(flows))
+    g = wide(gain[...], x)
     msg[0:cap, :] = base[0:cap, :] + x[0:cap]
-    msg[cap:, :] = base[cap:, :] + wide(gain[...], msg) * x[cap:]
-
-
-def outward(gain, part, near, s_a, out_a, base):
-    cap = s_a.shape[0]
+    msg[cap:, :] = base[cap : 2 * cap, :] + g * x[cap : 2 * cap]
+    return base[2 * cap :, :] + g * x[2 * cap :]
+
+
+def back_flows(gain, got, base, mid_a, msg, flow):
+    flow[...] = back(gain, got[...], base, mid_a, msg)
+
+
+def back_both(gain, got, base, mid_a, own_heads, live_b, msg, flow, cut_b):
+    cap = own_heads.shape[0]
+    y_far = got[cap:, :] + own_heads[...]
+    c = wide(gain[...] * live_b[...], y_far) * y_far
+    cut_b[...] = c
+    flow[...] = back(gain, got[0:cap, :], base, mid_a, msg) + c
+
+
+def outward(gain, part, near, s_ab, out_a, base):
+    cap = s_ab.shape[0] // 2
     x = pick(out_a[...], part)
     base[0:cap, :] = x[0:cap]
-    base[cap:, :] = gain * x[cap:] + pick(s_a[...], near)
+    base[cap:, :] = gain * x[cap:] + pick(s_ab[...], near)
 
 
 def inside_first(
-    sent, coef, sigma, measured, prior, part_in, arrived, l_a, s_a, out_a, *outs,
+    sent, coef, sigma, measured, prior, part_in, arrived, l_a, s_ab, out_a, *outs,
 ):
     taps, (weight, near, rvar, gain, part, base) = outs[:12], outs[12:]
     length = coef.shape[1]
@@ -256,38 +290,40 @@
     rvar[...] = jnp.broadcast_to(rsig * rsig * scale, rvar.shape)
     p = part_in[...] + pick(l_a[...], arrived[...])
     part[...] = p
-    outward(PENALTY, p, n, s_a, out_a, base)
-
-
-def inside(gain0, gain, sent, w, got, arrived, weight, rvar, s_a, s_at, inc, l_a, out_a, taps, r_out, part, near, base):
-    cap = s_a.shape[0]
-    r = w[...] + gain0[0:1, 0:1] * pick(s_at[...], got[0:cap, :])
+    outward(PENALTY, p, n, s_ab, out_a, base)
+
+
+def inside(refs):
+    gain, sent, w, adds, arrived, far, weight, rvar, s_ab, s_abt, inc, l_a, out_a = refs[:13]
+    taps, (r_out, part, near, base, heads) = refs[13:25], refs[25:]
+    r = w[...] + pick(s_abt[...], adds[...])
     r_out[...] = r
     p = pick(inc[...], r) + pick(l_a[...], arrived[...])
     part[...] = p
     n = backward(weight[...] * forward(r, taps[:6]), taps[6:]) * rvar[:, 0:1]
     near[...] = n
-    outward(gain[0:1, 0:1], p, n, s_a, out_a, base)
+    outward(gain[0:1, 0:1], p, n, s_ab, out_a, base)
+    heads[...] = pick(far[...].astype(BF16), sent[0 : heads.shape[0], :])
     return r, p, n
 
 
 def inside_one(*refs):
     *refs, sums = refs
-    r, _, _ = inside(*refs[:13], refs[13:25], *refs[25:])
+    r, _, _ = inside(refs)
     sums[...] = lanes_sum(r * r)
 
 
 def inside_two(before, *refs):
     *refs, sums = refs
-    r, _, _ = inside(*refs[:13], refs[13:25], *refs[25:])
+    r, _, _ = inside(refs)
     sums[0:8, :] = lanes_sum(before[...] * r)
     sums[8:16, :] = lanes_sum(r * r)
 
 
 def inside_three(before, sum0, sum1, *refs):
     *refs, row = refs
-    gain = refs[1]
-    r, p, n = inside(*refs[:13], refs[13:25], *refs[25:])
+    gain = refs[0]
+    r, p, n = inside(refs)
     tiles = (
         sum0[0:8, :], sum1[0:8, :], sum1[8:16, :], lanes_sum(before[...] * r), lanes_sum(r * r),
         lanes_sum(r * n) + gain[0:1, 0:1] * lanes_sum(p * p),
@@ -310,25 +346,11 @@
     rows[...] = jnp.broadcast_to(out, rows.shape)
 
 
-def join(gain, sent_back, got, sent, far, part, near, l_b, it_sb, w_out):
-    cap, hours = far.shape[0], part.shape[1]
-    y = part[...] + pick(l_b[...], got[0:cap, 0:hours])
-    y_far = got[cap:, 0:hours] + pick(far[...].astype(BF16), sent[0:cap, 0:hours])
-    w = near[...] + gain[0:1, 0:1] * pick(it_sb[...], jnp.concatenate([y, y_far], axis=0))
+def join(gain, sent_back, got, part, near, l_b, inc_t, out_b, w_out, base):
+    cap = l_b.shape[1]
+    y = part[...] + pick(l_b[...], got[0:cap, :])
+    w = near[...] + gain[0:1, 0:1] * pick(inc_t[...], y)
     w_out[...] = w
-    return w
-
-
-def join_first(gain, sent_back, got, sent, part, near, l_b, it_sb, out_b, w_out, base, far):
-    cap = far.shape[0]
-    hours = part.shape[1]
-    far[...] = got[0:cap, hours : hours + cap]
-    w = join(gain, sent_back, got, sent, far, part, near, l_b, it_sb, w_out)
-    base[...] = pick(out_b[...], w)
-
-
-def join_next(gain, sent_back, got, sent, far, part, near, l_b, it_sb, out_b, w_out, base):
-    w = join(gain, sent_back, got, sent, far, part, near, l_b, it_sb, w_out)
     base[...] = pick(out_b[...], w)
 
 
@@ -436,13 +458,13 @@
     )(*(pltpu.with_memory_space_constraint(x, pltpu.VMEM) for x in args))
 
 
-def bring(args, msg):
+def bring(args, *msgs):
     lists = (args[1], args[2])
     return pl.pallas_call(
         open_kernel,
-        out_shape=tuple(pltpu.VMEM(x.shape, x.dtype) for x in args) + (pltpu.VMEM(*msg),),
+        out_shape=tuple(pltpu.VMEM(x.shape, x.dtype) for x in args) + tuple(pltpu.VMEM(*m) for m in msgs),
         in_specs=[pl.BlockSpec(memory_space=pltpu.HBM)] * len(args),
-        out_specs=tuple(pl.BlockSpec(memory_space=pltpu.VMEM) for _ in range(len(args) + 1)),
+        out_specs=tuple(pl.BlockSpec(memory_space=pltpu.VMEM) for _ in range(len(args) + len(msgs))),
         scratch_shapes=[pltpu.SemaphoreType.DMA((len(args) + 6,))] + [pltpu.SMEM(x.shape, x.dtype) for x in lists],
         compiler_params=pltpu.CompilerParams(vmem_limit_bytes=16 * 2**20),
     )(*(pltpu.with_memory_space_constraint(x, pltpu.HBM) for x in args))
@@ -483,77 +505,95 @@
     heads = ((juncs, hours), F32)
     slots = ((cap, hours), F32)
     msg2 = ((2 * cap, hours), F32)
-    wide = ((2 * cap, hours + 128), F32)
+    msg3 = ((3 * cap, hours), F32)
     tile = ((8, 128), F32)
     half = ((hours // 2, hours // 2), BF16)
     on_chip = [(i, i ^ 1) for i in range(nets)]
-    across = []
+    across_pairs = []
     for h in range(hour_blocks):
         for i in range(1, nets - 1, 2):
             a, b = i * hour_blocks + h, (i + 1) * hour_blocks + h
-            across += [(a, b), (b, a)]
+            across_pairs += [(a, b), (b, a)]
         for i in (0, nets - 1):
-            across.append((i * hour_blocks + h, i * hour_blocks + (h ^ 1)))
+            across_pairs.append((i * hour_blocks + h, i * hour_blocks + (h ^ 1)))
 
     def swap(x):
         return lax.ppermute(x, NET, on_chip)
 
     def cross(x):
-        return lax.ppermute(x, (*NET, "hour"), across)
+        return lax.ppermute(x, (*NET, "hour"), across_pairs)
 
     args = (
         prior_flow, boundary_pipe, boundary_count, arrival_junction,
         pipe_head.reshape(1, pipes), pipe_tail.reshape(1, pipes), whiten_coef.reshape(1, hours), pipe_sigma.reshape(1, pipes),
     )
-    prior, bp, bc, aj, head, tail, coef, sigma, back = bring(args, msg2)
-    got = swap(back)
-    s_a, s_at, inc, l_a, l_b, it_sb, out_b, out_a, mid_b, mid_a, own, gain0, part, base = call(
+    prior, bp, bc, aj, head, tail, coef, sigma, msg, flow = bring(args, msg2, slots)
+    got = swap(msg)
+    flow_got = cross(flow)
+    s_ab, s_abt, inc, inc_t, l_a, l_b, out_b, out_a, mid_b, mid_a, own, gain0, live_b, part, base = call(
         lists_kernel,
         [
-            ((cap, pipes), BF16), ((pipes, cap), BF16), ((juncs, pipes), BF16), ((juncs, cap), BF16),
-            ((juncs, cap), BF16), ((pipes, juncs + cap), BF16), ((2 * cap, pipes), BF16), ((2 * cap, juncs), BF16),
-            ((cap, 6 * cap), BF16), ((2 * cap, 3 * cap), BF16), ((cap, cap), F32), tile, heads, msg2,
+            ((2 * cap, pipes), BF16), ((pipes, 2 * cap), BF16), ((juncs, pipes), BF16), ((pipes, juncs), BF16),
+            ((juncs, cap), BF16), ((juncs, cap), BF16), ((cap, pipes), BF16), ((3 * cap, juncs), BF16),
+            ((cap, 9 * cap), BF16), ((3 * cap, 3 * cap), BF16), ((cap, cap), F32), tile, tile, heads, slots,
         ],
-        back, prior, bp, bc, aj, head, tail, demand,
+        msg, prior, bp, bc, aj, head, tail, demand,
     )
-    sent, arrived, live = call(across_first, [wide, slots, tile], got, base, mid_b, own)
-    got = cross(sent)
+    sent, arrived, live = call(across_first, [((cap, hours + 128), F32), slots, tile], got, base, mid_b, own)
+    heads_got = cross(sent)
     out = call(
         inside_first,
-        [half] * 12 + [field, field, ((pipes, 128), F32), tile, heads, msg2],
-        sent, coef, sigma, measured, prior, part, arrived, l_a, s_a, out_a,
+        [half] * 12 + [field, field, ((pipes, 128), F32), tile, heads, msg3],
+        sent, coef, sigma, measured, prior, part, arrived, l_a, s_ab, out_a,
     )
     taps, (weight, near, rvar, gain, part, base) = out[:12], out[12:]
-    (back,) = call(back_kernel, [msg2], gain0, got, base, mid_a)
-    back_got = swap(back)
-    w, base, far = call(
-        join_first, [field, msg2, ((cap, cap), F32)], gain0, back, got, sent, part, near, l_b, it_sb, out_b
+
+    def joined(g, msg, flows):
+        return call(join, [field, slots], g, msg, flows, part, near, l_b, inc_t, out_b)
+
+    def filtered(kernel, acc, first, sent, w, adds, arrived):
+        return call(
+            kernel, [field, heads, field, msg3, slots, acc],
+            *first, gain, sent, w, adds, arrived, far, weight, rvar, s_ab, s_abt, inc, l_a, out_a, *taps,
+        )
+
+    msg, fore = call(back_flows, [msg2, slots], gain0, flow_got, base, mid_a)
+    got = swap(msg)
+    w, base = joined(gain0, msg, flow_got)
+    both, adds, arrived, far = call(
+        across_zero, [msg2, msg2, slots, ((cap, cap), F32)],
+        gain0, msg, got, live, base, mid_b, fore, heads_got, flow, live_b,
     )
-    fields, sums = [], []
-    for step in range(3):
-        g = gain if step else gain0
-        sent, arrived = call(across_next, [msg2, slots], g, back, back_got, live, base, mid_b)
-        got = cross(sent)
-        given = (g, gain, sent, w, back_got, arrived, weight, rvar, s_a, s_at, inc, l_a, out_a, *taps)
-        gives = [field, heads, field, msg2]
-        if step == 0:
-            r, part, near, base, acc = call(inside_one, gives + [tile], *given)
-        elif step == 1:
-            r, part, near, base, acc = call(inside_two, gives + [((16, 128), F32)], fields[-1], *given)
+    both_got = cross(both)
+    r0, part, near, base, own_heads, sum0 = filtered(inside_one, tile, (), both, w, adds, arrived)
+    fields, sums = [r0], [sum0]
+    for k in (1, 2):
+        msg, flow, cut_b = call(back_both, [msg2, slots, slots], gain, both_got, base, mid_a, own_heads, live_b)
+        got = swap(msg)
+        w, base = joined(gain, msg, both_got)
+        both, adds, arrived = call(
+            across_both, [msg2, msg2, slots], gain, msg, got, live, base, mid_b, flow, cut_b
+        )
+        both_got = cross(both)
+        if k == 1:
+            r, part, near, base, own_heads, acc = filtered(
+                inside_two, ((16, 128), F32), (fields[0],), both, w, adds, arrived
+            )
         else:
-            r, part, near, base, acc = call(inside_three, gives + [tile], fields[-1], *sums, *given)
+            r, part, near, base, own_heads, acc = filtered(
+                inside_three, tile, (fields[1], *sums), both, w, adds, arrived
+            )
         fields.append(r)
         sums.append(acc)
-        if step == 2:
-            (rows,) = call(close_kernel, [((devices, 128), F32)], gain, sent, got, own, acc)
-            rows = lax.all_to_all(
-                rows.reshape(devices, 1, 128), ("core", "z", "y", "hour"), 0, 0, tiled=True
-            ).reshape(devices, 128)
-        (back,) = call(back_kernel, [msg2], gain, got, base, mid_a)
-        back_got = swap(back)
-        w, base = call(join_next, [field, msg2], gain, back, got, sent, far, part, near, l_b, it_sb, out_b)
-    (last,) = call(whole_kernel, [field], gain, w, back_got, s_at)
-    return finish(rows, gain, prior, *fields, last)
+    (rows,) = call(close_kernel, [((devices, 128), F32)], gain, both, both_got, own, acc)
+    rows = lax.all_to_all(
+        rows.reshape(devices, 1, 128), ("core", "z", "y", "hour"), 0, 0, tiled=True
+    ).reshape(devices, 128)
+    msg, _, cut_b = call(back_both, [msg2, slots, slots], gain, both_got, base, mid_a, own_heads, live_b)
+    got = swap(msg)
+    w, _ = joined(gain, msg, both_got)
+    (r3,) = call(whole_kernel, [field], gain, w, got, cut_b, s_abt)
+    return finish(rows, gain, prior, *fields, r3)
 
 
 def solution(mesh):
@@ -571,6 +611,7 @@
         P(NET, None),
         P(NET, None, None),
     )
+
     return jax.shard_map(
         shards,
         mesh=fine,

time: 52.4 us -> 55.7 us (1.063)
  starting transfers between devices: 26.8 us -> 28.6 us
  Pallas kernels: 16.7 us -> 17.5 us
  waiting for transfers between devices: 8.03 us -> 8.66 us
    all_to_all x1, starting transfers between devices: 15.2 us -> 17.1 us  [shards(): lax.all_to_all(rows.reshape(devices, 1, 128), ('core', 'z', 'y', 'hour'),...]
    ppermute x4 -> x5, waiting for transfers between devices: 0.44 us -> 2.04 us  [cross(): return lax.ppermute(x, (*NET, 'hour'), across_pairs)]
    pallas_call x19, Pallas kernels: 14.4 us -> 15.2 us  [call(): pl.pallas_call(kernel, out_shape=tuple((pltpu.VMEM(s, d) for s, d in outs...]
    all_to_all x1, waiting for transfers between devices: 6.77 us -> 6.14 us  [shards(): lax.all_to_all(rows.reshape(devices, 1, 128), ('core', 'z', 'y', 'hour'),...]
    ppermute x4 -> x5, starting transfers between devices: 7.48 us -> 7.22 us  [cross(): return lax.ppermute(x, (*NET, 'hour'), across_pairs)]
  transfers between devices with their start and end apart: 10 -> 11, of which waited for: 6 -> 5; matrix products, arithmetic and copies ran while one was open for 0% -> 0% of each run, Pallas kernels for 24% -> 24%
where the time goes in v9:
time: 55.7 us; the launch traced here: 55.5 us
  starting transfers between devices  28.6 us (51%)
  Pallas kernels  17.5 us (31%)
  waiting for transfers between devices  8.66 us (16%)
  between operations  0.7 us (1%)
    all_to_all x1, starting transfers between devices, shards(): lax.all_to_all(rows.reshape(devices, 1, 128), ('core', 'z', 'y', 'hour'),...  17.1 us
    pallas_call x19, Pallas kernels, call(): pl.pallas_call(kernel, out_shape=tuple((pltpu.VMEM(s, d) for s, d in outs...  15.2 us
    ppermute x5, starting transfers between devices, cross(): return lax.ppermute(x, (*NET, 'hour'), across_pairs)  7.22 us
    all_to_all x1, waiting for transfers between devices, shards(): lax.all_to_all(rows.reshape(devices, 1, 128), ('core', 'z', 'y', 'hour'),...  6.14 us
    ppermute x5, starting transfers between devices, swap(): return lax.ppermute(x, NET, on_chip)  4.24 us
    ppermute x5, waiting for transfers between devices, cross(): return lax.ppermute(x, (*NET, 'hour'), across_pairs)  2.04 us
    pallas_call x1, Pallas kernels, bring(): pl.pallas_call(open_kernel, out_shape=tuple((pltpu.VMEM(x.shape, x.dtype)...  1.16 us
    pallas_call x1, Pallas kernels, finish(): pl.pallas_call(finish_kernel, out_shape=(jax.ShapeDtypeStruct(field.shape...  1.14 us
  transfers between devices with their start and end apart: 11, of which 5 were waited for; matrix products, arithmetic and copies ran while one was open for 0% of the time, Pallas kernels for 24%

profile of v9, /device:TPU:1, one launch (start us, length us, event | category | flops | bytes accessed | tf_op | source)
XLA Modules:
  0.0 55.5 jit_solution(3254297165201326807)
XLA Ops:
  0.6 0.0 copy-start.1
  0.6 1.2 %shard_map.113 = (f32[128,512]{1,0:T(8,128)S(1)}, s32[1,2,8]{2,1,0:T(2,128)S(1)}, s32[1,2]{1,0:T(1,128)S(1)}, s32[1,2,8]{2,1,0:T(2,128)S(1)}, s32[1,128]{1,0:T(1...) custom-call(f32[128,512]{1,0:T(8,128)} %prior_in.1, ...), custom_call_target="tpu_custom_call" | custom-call | tf_op jit(solution)/shard_map/pallas_call | solution.py:463
  1.8 1.5 %collective-permute-start = (f32[16,512]{1,0:T(8,128)S(1)}, f32[16,512]{1,0:T(8,128)S(1)}, u32[]{:S(2)}, u32[]{:S(2)}) collective-permute-start(f32[16,512]{1,0:T(8,128)S(1)} %get-tuple-element.93.sent), channel_id=1, source_target_pairs={{0,4},{4,0},{8,12},{12,8},{16,20},{20,16},{24,28},{28,24},{32,36},... | collective-permute-start | bytes 98312 | tf_op jit(solution)/shard_map/ppermute | solution.py:521
  3.3 1.7 %collective-permute-start.1 = (f32[8,512]{1,0:T(8,128)S(1)}, f32[8,512]{1,0:T(8,128)S(1)}, u32[]{:S(2)}, u32[]{:S(2)}) collective-permute-start(f32[8,512]{1,0:T(8,128)S(1)} %get-tuple-element.113.sent_flow), channel_id=1, source_target_pairs={{4,8},{8,4},{12,16},{16,12},{20,24},{24,20},{28,32},{32,28},{36,40... | collective-permute-start | bytes 49160 | tf_op jit(solution)/shard_map/ppermute | solution.py:524
  5.0 0.0 copy-done.1
  5.0 0.0 copy-start
  5.0 0.7 %shard_map.114 = (bf16[16,128]{1,0:T(8,128)(2,1)S(1)}, bf16[128,16]{1,0:T(8,128)(2,1)S(1)}, bf16[96,128]{1,0:T(8,128)(2,1)S(1)}, bf16[128,96]{1,0:T(8,128)(2,1)S...) custom-call(f32[16,512]{1,0:T(8,128)S(1)} %get-tuple-element.93.sent, ...), custom_call_target="tpu_custom_call" | custom-call | tf_op jit(solution)/shard_map/pallas_call | solution.py:452
  5.7 0.0 collective-permute-done.got
  5.7 0.1 shard_map.115
  5.9 0.1 copy-done
  6.0 2.0 %shard_map.116 = (bf16[256,256]{1,0:T(8,128)(2,1)S(1)}, bf16[256,256]{1,0:T(8,128)(2,1)S(1)}, bf16[256,256]{1,0:T(8,128)(2,1)S(1)}, bf16[256,256]{1,0:T(8,128)(2...) custom-call(f32[8,640]{1,0:T(8,128)S(1)} %get-tuple-element.103.sent, ...), custom_call_target="tpu_custom_call" | custom-call | tf_op jit(solution)/shard_map/pallas_call | solution.py:452
  7.9 0.0 collective-permute-done.1.got
  7.9 0.1 shard_map.117
  8.1 0.0 collective-permute-start.2
  8.1 2.0 %collective-permute-start.3 = (f32[8,640]{1,0:T(8,128)S(1)}, f32[8,640]{1,0:T(8,128)S(1)}, u32[]{:S(2)}, u32[]{:S(2)}) collective-permute-start(f32[8,640]{1,0:T(8,128)S(1)} %get-tuple-element.103.sent), channel_id=1, source_target_pairs={{4,8},{8,4},{12,16},{16,12},{20,24},{24,20},{28,32},{32,28},{36,40... | collective-permute-start | bytes 61448 | tf_op jit(solution)/shard_map/ppermute | solution.py:524
  10.1 0.6 %shard_map.118 = (f32[128,512]{1,0:T(8,128)S(1)}, f32[8,512]{1,0:T(8,128)S(1)}) custom-call(f32[8,128]{1,0:T(8,128)S(1)} %get-tuple-element.112.gain, f32[16,512]{1,0:T(8,128)S(1)} %get-tuple-element.116.sent_back.sent, f32[8,512]{1,0:T(8,128)S(1)} %collective-permute-done.1.got, f32[96,512]{1,0:T(8,128)S(1)} %get-tuple-element.118.part, ...), custom_call_target="tpu_custom_call" | custom-call | tf_op jit(solution)/shard_map/pallas_call | solution.py:452
  10.7 1.1 %collective-permute-done.3.heads = f32[8,640]{1,0:T(8,128)S(1)} collective-permute-done((f32[8,640]{1,0:T(8,128)S(1)}, f32[8,640]{1,0:T(8,128)S(1)}, u32[]{:S(2)}, u32[]{:S(2)}) %collective-permute-start.3) | collective-permute-done | bytes 20512 | tf_op jit(solution)/shard_map/ppermute | solution.py:524
  11.9 0.0 collective-permute-done.2.got
  11.9 0.3 shard_map.119
  12.2 1.5 %collective-permute-start.4 = (f32[16,512]{1,0:T(8,128)S(1)}, f32[16,512]{1,0:T(8,128)S(1)}, u32[]{:S(2)}, u32[]{:S(2)}) collective-permute-start(f32[16,512]{1,0:T(8,128)S(1)} %get-tuple-element.126.refs_1_), channel_id=1, source_target_pairs={{4,8},{8,4},{12,16},{16,12},{20,24},{24,20},{28,32},{32,28},{36,40... | collective-permute-start | bytes 98312 | tf_op jit(solution)/shard_map/ppermute | solution.py:524
  13.6 2.0 %shard_map.120 = (f32[128,512]{1,0:T(8,128)S(1)}, f32[96,512]{1,0:T(8,128)S(1)}, f32[128,512]{1,0:T(8,128)S(1)}, f32[24,512]{1,0:T(8,128)S(1)}, f32[8,512]{1,0:T(8,128)S(1)}, /*index=5*/f32[8,128]{1,0:T(8,128)S(1)}) custom-call(f32[8,128]{1,0:T(8,128)S(1)} %get-tuple-element.111.refs_0_.gain, f32[16,512]{1,0:T(8,128)S(1)} %get-tuple-element.126.refs_1_, ...), custom_call_target="tpu_custom_call" | custom-call | tf_op jit(solution)/shard_map/pallas_call | solution.py:452
  15.6 0.0 collective-permute-done.4.got
  15.6 0.1 shard_map.121
  15.8 1.0 %collective-permute-start.5 = (f32[16,512]{1,0:T(8,128)S(1)}, f32[16,512]{1,0:T(8,128)S(1)}, u32[]{:S(2)}, u32[]{:S(2)}) collective-permute-start(f32[16,512]{1,0:T(8,128)S(1)} %get-tuple-element.149.sent_back.sent), channel_id=1, source_target_pairs={{0,4},{4,0},{8,12},{12,8},{16,20},{20,16},{24,28},{28,24},{32,36},... | collective-permute-start | bytes 98312 | tf_op jit(solution)/shard_map/ppermute | solution.py:521
  16.8 0.6 %shard_map.122 = (f32[128,512]{1,0:T(8,128)S(1)}, f32[8,512]{1,0:T(8,128)S(1)}) custom-call(f32[8,128]{1,0:T(8,128)S(1)} %get-tuple-element.111.refs_0_.gain, f32[16,512]{1,0:T(8,128)S(1)} %get-tuple-element.149.sent_back.sent, f32[16,512]{1,0:T(8,128)S(1)} %collective-permute-done.4.got, f32[96,512]{1,0:T(8,128)S(1)} %get-tuple-element.150.part, ...), custom_call_target="tpu_custom_call" | custom-call | tf_op jit(solution)/shard_map/pallas_call | solution.py:452
  17.4 0.2 collective-permute-done.5.got
  17.7 0.1 shard_map.123
  17.8 0.8 %collective-permute-start.6 = (f32[16,512]{1,0:T(8,128)S(1)}, f32[16,512]{1,0:T(8,128)S(1)}, u32[]{:S(2)}, u32[]{:S(2)}) collective-permute-start(f32[16,512]{1,0:T(8,128)S(1)} %get-tuple-element.155.refs_1_), channel_id=1, source_target_pairs={{4,8},{8,4},{12,16},{16,12},{20,24},{24,20},{28,32},{32,28},{36,40... | collective-permute-start | bytes 98312 | tf_op jit(solution)/shard_map/ppermute | solution.py:524
  18.6 2.0 %shard_map.124 = (f32[128,512]{1,0:T(8,128)S(1)}, f32[96,512]{1,0:T(8,128)S(1)}, f32[128,512]{1,0:T(8,128)S(1)}, f32[24,512]{1,0:T(8,128)S(1)}, f32[8,512]{1,0:T(8,128)S(1)}, /*index=5*/f32[16,128]{1,0:T(8,128)S(1)}) custom-call(f32[128,512]{1,0:T(8,128)S(1)} %get-tuple-element.156.before.r0, f32[8,128]{1,0:T(8,128)S(1)} %get-tuple-element.111.refs_0_.gain, ...), custom_call_target="tpu_custom_call" | custom-call | tf_op jit(solution)/shard_map/pallas_call | solution.py:452
  20.5 0.9 %collective-permute-done.6.got = f32[16,512]{1,0:T(8,128)S(1)} collective-permute-done((f32[16,512]{1,0:T(8,128)S(1)}, f32[16,512]{1,0:T(8,128)S(1)}, u32[]{:S(2)}, u32[]{:S(2)}) %collective-permute-start.6) | collective-permute-done | bytes 32800 | tf_op jit(solution)/shard_map/ppermute | solution.py:524
  21.4 0.1 shard_map.125
  21.6 0.7 %collective-permute-start.7 = (f32[16,512]{1,0:T(8,128)S(1)}, f32[16,512]{1,0:T(8,128)S(1)}, u32[]{:S(2)}, u32[]{:S(2)}) collective-permute-start(f32[16,512]{1,0:T(8,128)S(1)} %get-tuple-element.162.sent_back.sent), channel_id=1, source_target_pairs={{0,4},{4,0},{8,12},{12,8},{16,20},{20,16},{24,28},{28,24},{32,36},... | collective-permute-start | bytes 98312 | tf_op jit(solution)/shard_map/ppermute | solution.py:521
  22.2 0.6 %shard_map.126 = (f32[128,512]{1,0:T(8,128)S(1)}, f32[8,512]{1,0:T(8,128)S(1)}) custom-call(f32[8,128]{1,0:T(8,128)S(1)} %get-tuple-element.111.refs_0_.gain, f32[16,512]{1,0:T(8,128)S(1)} %get-tuple-element.162.sent_back.sent, f32[16,512]{1,0:T(8,128)S(1)} %collective-permute-done.6.got, f32[96,512]{1,0:T(8,128)S(1)} %get-tuple-element.163.part, ...), custom_call_target="tpu_custom_call" | custom-call | tf_op jit(solution)/shard_map/pallas_call | solution.py:452
  22.9 0.2 collective-permute-done.7.got
  23.1 0.1 shard_map.127
  23.3 1.2 %collective-permute-start.8 = (f32[16,512]{1,0:T(8,128)S(1)}, f32[16,512]{1,0:T(8,128)S(1)}, u32[]{:S(2)}, u32[]{:S(2)}) collective-permute-start(f32[16,512]{1,0:T(8,128)S(1)} %get-tuple-element.168.refs_1_.sent), channel_id=1, source_target_pairs={{4,8},{8,4},{12,16},{16,12},{20,24},{24,20},{28,32},{32,28},{36,40... | collective-permute-start | bytes 98312 | tf_op jit(solution)/shard_map/ppermute | solution.py:524
  24.5 2.4 %shard_map.128 = (f32[128,512]{1,0:T(8,128)S(1)}, f32[96,512]{1,0:T(8,128)S(1)}, f32[128,512]{1,0:T(8,128)S(1)}, f32[24,512]{1,0:T(8,128)S(1)}, f32[8,512]{1,0:T(8,128)S(1)}, /*index=5*/f32[8,128]{1,0:T(8,128)S(1)}) custom-call(f32[128,512]{1,0:T(8,128)S(1)} %get-tuple-element.169.before.r1, f32[8,128]{1,0:T(8,128)S(1)} %get-tuple-element.170.sum0, ...), custom_call_target="tpu_custom_call" | custom-call | tf_op jit(solution)/shard_map/pallas_call | solution.py:452
  26.9 0.0 collective-permute-done.8.got
  26.9 0.8 %shard_map.129 = f32[128,128]{1,0:T(8,128)} custom-call(f32[8,128]{1,0:T(8,128)S(1)} %get-tuple-element.111.refs_0_.gain, f32[16,512]{1,0:T(8,128)S(1)} %get-tuple-element.168.refs_1_.sent, f32[16,512]{1,0:T(8,128)S(1)} %collective-permute-done.8.got, f32[8,8]{1,0:T(8,128)S(1)} %get-tuple-element.102.own, f32[8,128]{1,0:T(8,128)S(1)} %get-tuple-element.175.row), custom_call_target="tpu_custom_call" | custom-call | tf_op jit(solution)/shard_map/pallas_call | solution.py:452
  27.8 17.1 %all-to-all-start = ((f32[128,1,128]{2,1,0:T(1,128)}), f32[128,1,128]{2,1,0:T(1,128)S(1)}, u32[]{:S(2)}, u32[]{:S(2)}) async-start(f32[128,1,128]{2,1,0:T(1,128)} %bitcast.5), calls=%async_computation | async-start | bytes 131072 | tf_op jit(solution)/shard_map/all_to_all | solution.py:589
  44.9 0.7 %shard_map.130 = (f32[16,512]{1,0:T(8,128)S(1)}, f32[8,512]{1,0:T(8,128)}, f32[8,512]{1,0:T(8,128)S(1)}) custom-call(f32[8,128]{1,0:T(8,128)S(1)} %get-tuple-element.111.refs_0_.gain, f32[16,512]{1,0:T(8,128)S(1)} %collective-permute-done.8.got, f32[24,512]{1,0:T(8,128)S(1)} %get-tuple-element.177.base, bf16[24,24]{1,0:T(8,128)(2,1)S(1)} %get-tuple-element.115.mid_a, ...), custom_call_target="tpu_custom_call" | custom-call | tf_op jit(solution)/shard_map/pallas_call | solution.py:452
  45.6 1.1 %collective-permute-start.9 = (f32[16,512]{1,0:T(8,128)S(1)}, f32[16,512]{1,0:T(8,128)S(1)}, u32[]{:S(2)}, u32[]{:S(2)}) collective-permute-start(f32[16,512]{1,0:T(8,128)S(1)} %get-tuple-element.179.sent_back), channel_id=1, source_target_pairs={{0,4},{4,0},{8,12},{12,8},{16,20},{20,16},{24,28},{28,24},{32,36},... | collective-permute-start | bytes 98312 | tf_op jit(solution)/shard_map/ppermute | solution.py:521
  46.7 1.2 %shard_map.131 = (f32[128,512]{1,0:T(8,128)S(1)}, f32[8,512]{1,0:T(8,128)}) custom-call(f32[8,128]{1,0:T(8,128)S(1)} %get-tuple-element.111.refs_0_.gain, f32[16,512]{1,0:T(8,128)S(1)} %get-tuple-element.179.sent_back, f32[16,512]{1,0:T(8,128)S(1)} %collective-permute-done.8.got, f32[96,512]{1,0:T(8,128)S(1)} %get-tuple-element.180.part, ...), custom_call_target="tpu_custom_call" | custom-call | tf_op jit(solution)/shard_map/pallas_call | solution.py:452
  47.9 0.0 collective-permute-done.9.got
  48.0 0.3 shard_map.132.r3
  48.2 6.1 %all-to-all-done = f32[128,1,128]{2,1,0:T(1,128)S(1)} async-done(((f32[128,1,128]{2,1,0:T(1,128)}), f32[128,1,128]{2,1,0:T(1,128)S(1)}, u32[]{:S(2)}, u32[]{:S(2)}) %all-to-all-start) | async-done | bytes 65568 | tf_op jit(solution)/shard_map/all_to_all | solution.py:589
  54.4 1.1 %shard_map.133 = (f32[128,512]{1,0:T(8,128)}, f32[128,512]{1,0:T(8,128)}) custom-call(f32[128,128]{1,0:T(8,128)S(1)} %bitcast.8, f32[8,128]{1,0:T(8,128)S(1)} %get-tuple-element.111.refs_0_.gain, f32[128,512]{1,0:T(8,128)S(1)} %get-tuple-element.94.prior, f32[128,512]{1,0:T(8,128)S(1)} %get-tuple-element.156.before.r0, ...), custom_call_target="tpu_custom_call" | custom-call | tf_op jit(solution)/shard_map/pallas_call | solution.py:476
Async XLA Ops:
  0.6 4.4 %copy-start.1 = (f32[96,512]{1,0:T(8,128)S(1)}, f32[96,512]{1,0:T(8,128)}, u32[]{:S(2)}) copy-start(f32[96,512]{1,0:T(8,128)} %demand.1) | copy-start | bytes 589828
  1.8 3.9 %collective-permute-start = (f32[16,512]{1,0:T(8,128)S(1)}, f32[16,512]{1,0:T(8,128)S(1)}, u32[]{:S(2)}, u32[]{:S(2)}) collective-permute-start(f32[16,512]{1,0:T(8,128)S(1)} %get-tuple-element.93.sent), channel_id=1, source_target_pairs={{0,4},{4,0},{8,12},{12,8},{16,20},{20,16},{24,28},{28,24},{32,36},... | collective-permute-start | bytes 98312 | tf_op jit(solution)/shard_map/ppermute | solution.py:521
  3.3 4.7 %collective-permute-start.1 = (f32[8,512]{1,0:T(8,128)S(1)}, f32[8,512]{1,0:T(8,128)S(1)}, u32[]{:S(2)}, u32[]{:S(2)}) collective-permute-start(f32[8,512]{1,0:T(8,128)S(1)} %get-tuple-element.113.sent_flow), channel_id=1, source_target_pairs={{4,8},{8,4},{12,16},{16,12},{20,24},{24,20},{28,32},{32,28},{36,40... | collective-permute-start | bytes 49160 | tf_op jit(solution)/shard_map/ppermute | solution.py:524
  5.0 1.0 %copy-start = (f32[128,512]{1,0:T(8,128)S(1)}, f32[128,512]{1,0:T(8,128)}, u32[]{:S(2)}) copy-start(f32[128,512]{1,0:T(8,128)} %measured.1) | copy-start | bytes 786436
  8.1 3.8 %collective-permute-start.2 = (f32[16,512]{1,0:T(8,128)S(1)}, f32[16,512]{1,0:T(8,128)S(1)}, u32[]{:S(2)}, u32[]{:S(2)}) collective-permute-start(f32[16,512]{1,0:T(8,128)S(1)} %get-tuple-element.116.sent_back.sent), channel_id=1, source_target_pairs={{0,4},{4,0},{8,12},{12,8},{16,20},{20,16},{24,28},{28,24},{32,36},... | collective-permute-start | bytes 98312 | tf_op jit(solution)/shard_map/ppermute | solution.py:521
  8.1 3.8 %collective-permute-start.3 = (f32[8,640]{1,0:T(8,128)S(1)}, f32[8,640]{1,0:T(8,128)S(1)}, u32[]{:S(2)}, u32[]{:S(2)}) collective-permute-start(f32[8,640]{1,0:T(8,128)S(1)} %get-tuple-element.103.sent), channel_id=1, source_target_pairs={{4,8},{8,4},{12,16},{16,12},{20,24},{24,20},{28,32},{32,28},{36,40... | collective-permute-start | bytes 61448 | tf_op jit(solution)/shard_map/ppermute | solution.py:524
  12.2 3.4 %collective-permute-start.4 = (f32[16,512]{1,0:T(8,128)S(1)}, f32[16,512]{1,0:T(8,128)S(1)}, u32[]{:S(2)}, u32[]{:S(2)}) collective-permute-start(f32[16,512]{1,0:T(8,128)S(1)} %get-tuple-element.126.refs_1_), channel_id=1, source_target_pairs={{4,8},{8,4},{12,16},{16,12},{20,24},{24,20},{28,32},{32,28},{36,40... | collective-permute-start | bytes 98312 | tf_op jit(solution)/shard_map/ppermute | solution.py:524
  15.8 1.9 %collective-permute-start.5 = (f32[16,512]{1,0:T(8,128)S(1)}, f32[16,512]{1,0:T(8,128)S(1)}, u32[]{:S(2)}, u32[]{:S(2)}) collective-permute-start(f32[16,512]{1,0:T(8,128)S(1)} %get-tuple-element.149.sent_back.sent), channel_id=1, source_target_pairs={{0,4},{4,0},{8,12},{12,8},{16,20},{20,16},{24,28},{28,24},{32,36},... | collective-permute-start | bytes 98312 | tf_op jit(solution)/shard_map/ppermute | solution.py:521
  17.8 3.6 %collective-permute-start.6 = (f32[16,512]{1,0:T(8,128)S(1)}, f32[16,512]{1,0:T(8,128)S(1)}, u32[]{:S(2)}, u32[]{:S(2)}) collective-permute-start(f32[16,512]{1,0:T(8,128)S(1)} %get-tuple-element.155.refs_1_), channel_id=1, source_target_pairs={{4,8},{8,4},{12,16},{16,12},{20,24},{24,20},{28,32},{32,28},{36,40... | collective-permute-start | bytes 98312 | tf_op jit(solution)/shard_map/ppermute | solution.py:524
  21.6 1.5 %collective-permute-start.7 = (f32[16,512]{1,0:T(8,128)S(1)}, f32[16,512]{1,0:T(8,128)S(1)}, u32[]{:S(2)}, u32[]{:S(2)}) collective-permute-start(f32[16,512]{1,0:T(8,128)S(1)} %get-tuple-element.162.sent_back.sent), channel_id=1, source_target_pairs={{0,4},{4,0},{8,12},{12,8},{16,20},{20,16},{24,28},{28,24},{32,36},... | collective-permute-start | bytes 98312 | tf_op jit(solution)/shard_map/ppermute | solution.py:521
  23.3 3.6 %collective-permute-start.8 = (f32[16,512]{1,0:T(8,128)S(1)}, f32[16,512]{1,0:T(8,128)S(1)}, u32[]{:S(2)}, u32[]{:S(2)}) collective-permute-start(f32[16,512]{1,0:T(8,128)S(1)} %get-tuple-element.168.refs_1_.sent), channel_id=1, source_target_pairs={{4,8},{8,4},{12,16},{16,12},{20,24},{24,20},{28,32},{32,28},{36,40... | collective-permute-start | bytes 98312 | tf_op jit(solution)/shard_map/ppermute | solution.py:524
  27.8 26.6 %all-to-all-start = ((f32[128,1,128]{2,1,0:T(1,128)}), f32[128,1,128]{2,1,0:T(1,128)S(1)}, u32[]{:S(2)}, u32[]{:S(2)}) async-start(f32[128,1,128]{2,1,0:T(1,128)} %bitcast.5), calls=%async_computation | async-start | bytes 131072 | tf_op jit(solution)/shard_map/all_to_all | solution.py:589
  45.6 2.3 %collective-permute-start.9 = (f32[16,512]{1,0:T(8,128)S(1)}, f32[16,512]{1,0:T(8,128)S(1)}, u32[]{:S(2)}, u32[]{:S(2)}) collective-permute-start(f32[16,512]{1,0:T(8,128)S(1)} %get-tuple-element.179.sent_back), channel_id=1, source_target_pairs={{0,4},{4,0},{8,12},{12,8},{16,20},{20,16},{24,28},{28,24},{32,36},... | collective-permute-start | bytes 98312 | tf_op jit(solution)/shard_map/ppermute | solution.py:521
